TPU v7x, 32 devices: a whole 2x2x4 slice. The times are simulated.
32 devices in a mesh: animal: 8 (over z, y), snp: 4 (over x, core).
Axes of the slice: x: 2, y: 2, z: 4, core: 2. Of those that a mesh axis runs over, the one named last changes fastest.
Arguments:
- genotype: bfloat16 [8192, 32768], P('animal', 'snp')
- allele_freq: float32 [32768], P('snp')
- right_side: float32 [8192, 128], P('animal'), may hold values from -6 to 6
- diagonal: float32 [8192, 128], P('animal'), may hold values from 0.5 to 2
- mendelian: float32 [8192], P('animal'), may hold values from 2 to 4
- genomic_weight: float32 [128], replicated, may hold values from 1 to 8
- send_rows: int32 [8, 8, 64], P('animal'), may hold values from 0 to 1023, as said below
- sire_slot: int32 [8192], P('animal'), may hold values from 0 to 463, as said below
- dam_slot: int32 [8192], P('animal'), may hold values from 16 to 511, as said below
Outputs:
- solution: float32 [8192, 128], P('animal')
- residual: float32 [8192, 128], P('animal')
Inputs may be any that keep to these rules, and one draw needn't show every extreme that they name: send_rows[o, d, :] lists 64 distinct local rows of owner o's 1024 animals, those sent to device d. sire_slot[i] = o * 64 + k with k < 16. dam_slot[i] = o * 64 + k with k >= 16.
All inputs are finite; a program needn't handle non-finite values.
Results may differ from a plain program's by a relative error of at most 0.0067.
Values may be sent and summed in bfloat16 or wider, within the bound.
No kernel may reach another device: no remote copies, remote signals or barrier semaphores. Data moves between devices by JAX's collectives and lax.ppermute only.
A program may use at most 64 MiB of HBM per device.

v0:
```python
import jax
import jax.numpy as jnp
from jax import lax
from jax.experimental import pallas as pl
from jax.experimental.pallas import tpu as pltpu
from jax.sharding import PartitionSpec as P


BF16, F32, I32 = jnp.bfloat16, jnp.float32, jnp.int32
LANES = 128
VMEM = pl.BlockSpec(memory_space=pltpu.VMEM)
SMEM = pl.BlockSpec(memory_space=pltpu.SMEM)
HBM = pl.BlockSpec(memory_space=pltpu.HBM)


def call(body, ins, outs, specs=None, limit=24, scratch=(), flops=0,
         placed=True):
    specs = specs or [VMEM] * (len(ins) - 1)
    outs = tuple(o if hasattr(o, "memory_space") else jax.ShapeDtypeStruct(*o) for o in outs)
    moved = sum(a.size * a.dtype.itemsize for a in ins)
    return pl.pallas_call(
        body,
        in_specs=[SMEM, *specs] if placed else [VMEM] * len(ins),
        out_specs=tuple(VMEM for _ in outs),
        out_shape=outs,
        scratch_shapes=scratch,
        cost_estimate=pl.CostEstimate(flops=flops, bytes_accessed=moved, transcendentals=0),
        compiler_params=pltpu.CompilerParams(vmem_limit_bytes=limit << 20),
    )(*ins)


def positions(order):
    if not order:
        return [0]
    rest = positions(order[1:])
    return rest + [j | order[0] for j in rest]


def swap(x, axis, bit):
    size = lax.axis_size(axis)
    return lax.ppermute(x, axis, [(i, i ^ bit) for i in range(size)])


def bits_of(size):
    return [1 << b for b in range(size.bit_length() - 1)]


def part_count(owned):
    return max(1, min(4, owned // LANES))


def colsum(x):
    return jnp.sum(x, axis=0, keepdims=True)


def stack_rows(rows):
    wide = rows[0].shape[1]
    return jnp.concatenate([*rows, jnp.zeros((8 - len(rows), wide), F32)], axis=0)


def split(x):
    high = x.astype(BF16)
    return high, (x - high.astype(F32)).astype(BF16)


def hot_dot(hot, x, dims):
    high, low = split(x)
    dims = (dims, ((), ()))
    out = lax.dot_general(hot, high, dims, preferred_element_type=F32)
    return out + lax.dot_general(hot, low, dims, preferred_element_type=F32)


class Plan:
    def __init__(self, genotype, right_side, send_rows, carry):
        self.owners = lax.axis_size("animal")
        self.rows, self.snps = genotype.shape
        self.cols = right_side.shape[1]
        self.slots = send_rows.shape[2]
        self.half = self.owners // 2
        self.owned = self.snps // self.owners
        self.parts = part_count(self.owned)
        self.width = self.owned // self.parts
        self.nb = self.width // LANES
        bits = bits_of(self.owners)
        flip = [bits[1], bits[0], *bits[2:]]
        self.orders = [bits if part % 2 == 0 else flip for part in range(self.parts)]
        self.bits = bits
        self.sets = [[0, 1], [2, 3]] if self.parts == 4 else [list(range(self.parts))]

        self.groups = lax.axis_size("snp")
        self.kinds = max(1, self.groups // 2)
        self.lane_shift = (self.cols // self.groups).bit_length() - 1
        self.packed = self.slots // self.kinds
        self.pedigree = self.owners * self.packed
        self.carry = carry
        self.line = self.packed + carry

    def tile(self, blocks, slots=0):
        return ((blocks * LANES + slots * self.line, self.cols), BF16)

    def message_shapes(self, group):
        half, nb = self.half, self.nb
        shapes = []
        for part in group:
            if part:
                shapes += [self.tile(half * nb), self.tile(half * nb)]
            else:
                shapes += [self.tile(half * nb, half), self.tile(half * nb), self.tile(0, half)]
        return shapes

    def share(self, group):
        return self.width * len(group)

    def kept_shapes(self, group):
        wide = self.owners * self.share(group)
        return [pltpu.VMEM((self.rows, wide), BF16), ((1, wide), F32)]

    def lane_group(self, shape):
        return lax.broadcasted_iota(I32, shape, 1) >> self.lane_shift

    def fold(self, x):
        shift = self.cols // 2
        while shift >> self.lane_shift:
            x = x + pltpu.roll(x, shift, 1)
            shift //= 2
        return x

    def mine(self, place, x):
        return jnp.where(self.lane_group(x.shape) == place[1], x, 0.0)

    def mix(self, x):
        high = x.astype(BF16).astype(F32)
        return jnp.where(self.lane_group(x.shape) < self.kinds, high, x - high)

    def select(self, pieces):
        kind = self.lane_group(pieces[0].shape) & (self.kinds - 1)
        out = pieces[0]
        for k in range(1, self.kinds):
            out = jnp.where(kind == k, pieces[k], out)
        return out

    def pack(self, x):
        size = self.pedigree
        pieces = [x[k * size : (k + 1) * size] for k in range(self.kinds)]
        return self.select(pieces).astype(BF16)


def encode(plan, rows):
    lines = []
    for row in rows:
        high = row.astype(BF16).astype(F32)
        mid = (row - high).astype(BF16).astype(F32)
        lines += [high, mid, row - high - mid]
    lines.append(jnp.zeros((plan.carry - len(lines), plan.cols), F32))
    return jnp.concatenate(lines, axis=0).astype(BF16)


def decode(total, count):
    return [colsum(total[3 * i : 3 * i + 3]) for i in range(count)]


def put_rows(plan, order, packed, send, offset, keep, sums=None):
    size = plan.packed
    for at, r in enumerate(positions(order)):
        block = packed[r * size : (r + 1) * size]
        out, first = keep, at * plan.line
        if at >= plan.half:
            out, first = send, offset + (at - plan.half) * plan.line
        out[first : first + size] = block
        if sums is not None:
            out[first + size : first + plan.line] = sums


def take_rows(plan, keep_p, got, edge):
    blocks, sums = [], None
    for at in range(plan.owners):
        from_, first = keep_p, at * plan.line
        if at >= plan.half:
            from_, first = got, edge + (at - plan.half) * plan.line
        blocks.append(from_[first : first + plan.packed])
        if plan.carry:
            under = from_[first + plan.packed : first + plan.line].astype(F32)
            sums = under if sums is None else sums + under
    return blocks, sums


def copy_in(plan, group, place, geno, freq, kept, kept_freq, sem, freq_sem):
    wide = plan.share(group)
    copies = []
    for r in range(plan.owners):
        first = (place[0] ^ r) * plan.owned + group[0] * plan.width
        there = pl.ds(pl.multiple_of(first, LANES), wide)
        here = pl.ds(r * wide, wide)
        copies.append((
            pltpu.make_async_copy(freq.at[:, there], kept_freq.at[:, here], freq_sem.at[r]),
            pltpu.make_async_copy(geno.at[:, there], kept.at[:, here], sem.at[r]),
        ))
        for copy in copies[-1]:
            copy.start()
    return copies


def put_effects(plan, group, r, geno, freq, turned, sums, messages):
    wide = plan.share(group)
    here = slice(r * wide, (r + 1) * wide)
    acc = jnp.dot(turned, geno[:, here], preferred_element_type=F32)
    acc = (acc - sums * (2.0 * freq[:, here])).astype(BF16)
    half, nb = plan.half, plan.nb
    messages = list(messages)
    for index, part in enumerate(group):
        send, keep = messages[:2]
        messages = messages[2 if part else 3 :]
        at = positions(plan.orders[part]).index(r)
        out, at = (keep, at) if at < half else (send, at - half)
        for b in range(nb):
            first = index * plan.width + b * LANES
            row = (at * nb + b) * LANES
            out[row : row + LANES] = acc[:, first : first + LANES]


def emit_rows(plan, place, field, gather_hot, messages, sums=None):
    mixed = plan.mix(plan.fold(plan.mine(place, field))).astype(BF16)
    rows = lax.dot_general(
        gather_hot[...], mixed, (((0,), (0,)), ((), ())), preferred_element_type=F32
    )
    offset = plan.half * plan.nb * LANES
    put_rows(plan, plan.bits, plan.pack(rows), messages[0], offset, messages[2], sums)


def turn(field):
    turned = field.T.astype(BF16)
    return turned, jnp.sum(turned.astype(F32), axis=1, keepdims=True)


def turn_out(field, flipped, sums):
    turned, side = turn(field)
    flipped[...] = turned
    sums[...] = jnp.broadcast_to(side, sums.shape)
    return turned, side


def begin_body(plan, place, geno, freq, right_in, send_in, sire_in, dam_in,
               kept, kept_freq, gather_hot, parent_hot, flipped, sums, *rest):
    messages, scratch = rest[:-8], rest[-8:]
    right, send_rows, sire, dam, index, sem, freq_sem, small_sem = scratch
    pairs = ((send_in, send_rows), (sire_in, sire), (dam_in, dam), (right_in, right))
    small = [pltpu.make_async_copy(*pair, small_sem.at[i]) for i, pair in enumerate(pairs)]
    for copy in small:
        copy.start()
    group = plan.sets[0]
    copies = copy_in(plan, group, place, geno, freq, kept, kept_freq, sem, freq_sem)
    me, slots, packed = place[0], plan.slots, plan.packed
    shift, short = slots.bit_length() - 1, packed.bit_length() - 1
    for copy in small[:3]:
        copy.wait()
    for r in range(plan.owners):
        line = send_rows[pl.ds(me ^ r, 1), :]
        for k in range(plan.kinds):
            first = k * plan.pedigree + r * packed
            index[:, first : first + packed] = line[:, k * packed : (k + 1) * packed]

    def spot(slot):
        owner, row = (slot >> shift) ^ me, slot & (slots - 1)
        return (row >> short) * plan.pedigree + (owner << short) + (row & (packed - 1))

    sires, dams = spot(sire[...]), spot(dam[...])
    animal = lax.broadcasted_iota(I32, (plan.rows, LANES), 0)
    row = lax.broadcasted_iota(I32, (LANES, plan.rows), 0)
    for first in range(0, plan.owners * slots, LANES):
        here = slice(first, first + LANES)
        gather_hot[:, here] = jnp.where(animal == index[:, here], 1.0, 0.0).astype(BF16)
        hot = jnp.where(row == sires - first, 1.0, 0.0) + jnp.where(row == dams - first, 1.0, 0.0)
        parent_hot[here, :] = hot.astype(BF16)
    for copy in small[3:]:
        copy.wait()
    emit_rows(plan, place, right[...], gather_hot, messages)
    turned, side = turn_out(right[...], flipped, sums)
    for r in range(plan.owners):
        for copy in copies[r]:
            copy.wait()
        put_effects(plan, group, r, kept, kept_freq, turned, side, messages)


def begin_more_body(plan, group, place, geno, freq, flipped, sums, kept, kept_freq, *rest):
    messages, (sem, freq_sem) = rest[:-2], rest[-2:]
    copies = copy_in(plan, group, place, geno, freq, kept, kept_freq, sem, freq_sem)
    for r in range(plan.owners):
        for copy in copies[r]:
            copy.wait()
        put_effects(plan, group, r, kept, kept_freq, flipped[...], sums[:, :1], messages)


def more_body(plan, group, geno, freq, flipped, sums, *messages):
    for r in range(plan.owners):
        put_effects(plan, group, r, geno, freq, flipped[...], sums[:, :1], messages)


def merge_body(plan, slots_left, sources, got, keep_e, keep_p, send, next_e, next_p):
    half = slots_left // 2
    count = slots_left * plan.nb * LANES
    summed = (keep_e[...].astype(F32) + got[0:count].astype(F32)).astype(BF16)
    next_e[...] = summed[: count // 2]
    send[0 : count // 2] = summed[count // 2 :]
    size, step = half * plan.line, slots_left * plan.line
    for s in range(2 * sources):
        from_, at = (keep_p, s * step) if s < sources else (got, count + (s - sources) * step)
        next_p[s * size : (s + 1) * size] = from_[at : at + size]
        first = count // 2 + s * size
        send[first : first + size] = from_[at + size : at + step]


def add_body(got, keep, *out):
    summed = (keep[...].astype(F32) + got[...].astype(F32)).astype(BF16)
    size = summed.shape[0] // len(out)
    for i, ref in enumerate(out):
        ref[...] = summed[i * size : (i + 1) * size]


def join_body(sent, got, out):
    size = sent.shape[0]
    out[0:size] = sent[...]
    out[size:] = got[...]


def offspring_body(plan, second, place, got, keep_e, keep_p, field, parent_hot, mendelian, *rest):
    if second:
        plain_before, diagonal, right, *rest = rest
    send, keep_back, term, extra = rest
    edge, size = plan.nb * LANES, plan.pedigree
    send[0:edge] = (keep_e[...].astype(F32) + got[0:edge].astype(F32)).astype(BF16)
    blocks, under = take_rows(plan, keep_p, got, edge)
    received = jnp.concatenate(blocks, axis=0)
    pieces = [
        lax.dot_general(
            parent_hot[k * size : (k + 1) * size],
            received,
            (((0,), (0,)), ((), ())),
            preferred_element_type=F32,
        )
        for k in range(plan.kinds)
    ]
    parents = plan.fold(plan.select(pieces))
    weight = jnp.broadcast_to(mendelian[...], (plan.cols, plan.rows)).T
    plain = plan.fold(plan.mine(place, field[...])) - 0.5 * parents
    mendel = weight * plain
    term[...] = mendel
    back = -0.5 * hot_dot(parent_hot[...], mendel, ((1,), (0,)))
    sums = None
    if second:
        gamma, delta = decode(under, 2)
        extra[...] = stack_rows([gamma, delta])
        alpha = gamma / delta
        residual = right[...] - alpha * field[...]
        moved = plain_before[...] - alpha * plain
        sums = encode(plan, [
            colsum(residual * residual),
            colsum(field[...] * residual),
            colsum(diagonal[...] * field[...] * residual),
            plan.mine(place, colsum(mendel * moved)),
        ])
    else:
        extra[...] = plain
    put_rows(plan, plan.bits[::-1], plan.pack(plan.mix(back)), send, edge, keep_back, sums)


def spread_body(plan, slots_held, sources, sent, got, keep_p, send, next_p):
    count = slots_held * plan.nb * LANES
    send[0:count] = sent[0:count]
    send[count : 2 * count] = got[0:count]
    step = plan.half // sources * plan.line
    size = step // 2
    for s in range(2 * sources):
        from_, at = (keep_p, s * step) if s < sources else (got, count + (s - sources) * step)
        next_p[s * size : (s + 1) * size] = from_[at : at + size]
        first = 2 * count + s * size
        send[first : first + size] = from_[at + size : at + step]


def home_rows(plan, place, term, keep_p, got, gather_hot):
    blocks, under = take_rows(plan, keep_p, got, plan.half * plan.nb * LANES)
    order = positions(plan.bits)
    returned = jnp.concatenate([blocks[order.index(r)] for r in range(plan.owners)], axis=0)
    size = plan.pedigree
    pieces = [
        jnp.dot(gather_hot[:, k * size : (k + 1) * size], returned, preferred_element_type=F32)
        for k in range(plan.kinds)
    ]
    return plan.mine(place, term[...] + plan.fold(plan.select(pieces))), under


def lane_total(plan, x):
    side = jnp.sum(x, axis=1, keepdims=True)
    return jnp.broadcast_to(side, (plan.cols, LANES)).T[0:1, :]


def values_body(plan, group, first, last, place, geno, freq, scale, *refs):
    second = plan.carry > 0
    pairs, refs = refs[: 2 * len(group)], refs[2 * len(group) :]
    if second:
        earlier, dots, refs = refs[: 2 * len(group)], refs[2 * len(group)], refs[2 * len(group) + 1 :]
        alpha = dots[0:1, :] / dots[1:2, :]
        alpha = jnp.broadcast_to(alpha, (LANES, plan.cols)).T[:, :1]
    if first:
        term, keep_p, gather_hot, *refs = refs
    elif second:
        before, more_before, *refs = refs
    else:
        before, *refs = refs
    *outs, acc = refs
    turned = (((1,), (1,)), ((), ()))
    nb, half = plan.nb, plan.half

    def block_of(near, far, at):
        held, at = (near, at) if at < half else (far, at - half)
        tiles = [held[(at * nb + b) * LANES : (at * nb + b + 1) * LANES] for b in range(nb)]
        return jnp.concatenate(tiles, axis=1)

    spread, inner = None, None
    for index, part in enumerate(group):
        near, far = pairs[2 * index : 2 * index + 2]
        for at, r in enumerate(positions(plan.orders[part])):
            first_column = r * plan.share(group) + index * plan.width
            here = slice(first_column, first_column + plan.width)
            block = block_of(near, far, at)
            wide = block.astype(F32)
            off = wide * (2.0 * freq[:, here])
            if second:
                old = block_of(*earlier[2 * index : 2 * index + 2], at).astype(F32)
                product = wide * (old - alpha * wide)
                inner = product if inner is None else inner + product
            value = lax.dot_general(geno[:, here], block, turned, preferred_element_type=F32)
            if spread is None:
                spread, acc[...] = off, value
            else:
                spread = spread + off
                acc[...] += value
    shift = lane_total(plan, spread)
    if first:
        base, under = home_rows(plan, place, term, keep_p, pairs[1], gather_hot)
    else:
        base = before[...]
    if second:
        inner = scale[...] * lane_total(plan, inner)
        if first:
            gamma, cross, own_part, pedigree = decode(under, 4)
            inner = inner + pedigree
            outs[-1][...] = stack_rows([gamma, cross, own_part, inner])
        else:
            inner = inner + more_before[3:4, :]
    if last:
        acc[...] = base + scale[...] * (acc[...] - shift)
        own, other = outs[:2]
        rows = plan.rows // 2
        at = (place[1] & 1) * rows
        own[0:rows] = acc[pl.ds(pl.multiple_of(at, rows), rows), :]
        other[0:rows] = acc[pl.ds(pl.multiple_of(rows - at, rows), rows), :]
        if second:
            own[rows:] = stack_rows([inner])
            other[rows:] = stack_rows([inner])
    else:
        outs[0][...] = base + scale[...] * (acc[...] - shift)


def apply_operator(place, field, diagonal, own, other, full):
    rows = field.shape[0] // 2
    at = (place[1] & 1) * rows
    full[pl.ds(pl.multiple_of(at, rows), rows), :] = own[0:rows]
    full[pl.ds(pl.multiple_of(rows - at, rows), rows), :] = other[0:rows]
    return diagonal[...] * field[...] + full[...]


def middle_body(plan, place, field, diagonal, own, other, geno, freq, gather_hot,
                image, flipped, sums, *rest):
    messages, full = rest[:-1], rest[-1]
    out = apply_operator(place, field, diagonal, own, other, full)
    image[...] = out
    dots = encode(plan, [colsum(field[...] * field[...]), colsum(out * field[...])])
    emit_rows(plan, place, image[...], gather_hot, messages, dots)
    turned, side = turn_out(image[...], flipped, sums)
    for r in range(plan.owners):
        put_effects(plan, plan.sets[0], r, geno, freq, turned, side, messages)


def final_body(place, field, diagonal, own, other, right, dots, more,
               solution, residual, full):
    q = apply_operator(place, field, diagonal, own, other, full)
    alpha0 = dots[0:1, :] / dots[1:2, :]
    gamma = more[0:1, :]
    rows = field.shape[0] // 2
    delta = more[1:2, :] - alpha0 * (more[2:3, :] + own[rows : rows + 1, :])
    beta = gamma / dots[0:1, :]
    alpha = gamma / (delta - beta * gamma / alpha0)
    left = right[...] - alpha0 * field[...]
    w = field[...] - alpha0 * q
    s = w + beta * field[...]
    p = left + beta * right[...]
    solution[...] = alpha0 * right[...] + alpha * p
    residual[...] = left - alpha * s


def local(genotype, allele_freq, right_side, diagonal, mendelian, genomic_weight, send_rows,
          sire_slot, dam_slot):
    blocks = lax.axis_size("snp")
    plan = Plan(genotype, right_side, send_rows, 0)
    summing = Plan(genotype, right_side, send_rows, 16)
    rows, cols, half, nb, parts = plan.rows, plan.cols, plan.half, plan.nb, plan.parts
    place = jnp.stack([lax.axis_index("animal"), lax.axis_index("snp")]).astype(I32)
    freq = allele_freq.reshape(1, plan.snps)
    scale = (genomic_weight / (plan.snps * blocks)).reshape(1, cols)
    weight = mendelian.reshape(1, rows)
    square = ((rows, cols), F32)
    lines = ((8, cols), F32)
    wide = plan.owners * plan.slots
    work = 2 * rows * cols * plan.snps
    groups = plan.sets
    turned = (((cols, rows), BF16), ((cols, LANES), F32))
    full = [pltpu.VMEM((rows, cols), F32)]

    whole, frequency = (
        pltpu.with_memory_space_constraint(x, pltpu.HBM) for x in (genotype, freq)
    )
    copies = [pltpu.SemaphoreType.DMA((plan.owners,))] * 2
    geno, freq, gather_hot, parent_hot, flipped, sums, *messages = call(
        lambda *r: begin_body(plan, *r),
        (place, whole, frequency, *[
            pltpu.with_memory_space_constraint(x, pltpu.HBM)
            for x in (right_side, send_rows[0], sire_slot.reshape(1, rows),
                      dam_slot.reshape(1, rows))
        ]),
        (*plan.kept_shapes(groups[0]), ((rows, wide), BF16), ((wide, rows), BF16), *turned,
         *plan.message_shapes(groups[0])),
        specs=[HBM] * 6,
        scratch=[
            pltpu.VMEM((rows, cols), F32),
            pltpu.VMEM(send_rows.shape[1:], I32),
            pltpu.VMEM((1, rows), I32),
            pltpu.VMEM((1, rows), I32),
            pltpu.VMEM((1, wide), I32),
            *copies,
            pltpu.SemaphoreType.DMA((4,)),
        ],
        flops=work,
    )
    kept = [(geno, freq)]
    for group in groups[1:]:
        *pair, = call(
            lambda *r, group=group: begin_more_body(plan, group, *r),
            (place, whole, frequency, flipped, sums),
            (*plan.kept_shapes(group), *plan.message_shapes(group)),
            specs=[HBM] * 2 + [VMEM] * 2,
            scratch=copies,
            flops=work,
        )
        kept.append(tuple(pair[:2]))
        messages += pair[2:]

    def round_trip(op, plan, field, messages, extra, earlier):
        order = plan.bits
        send, keep_e, keep_p = messages[:3]
        left, sources = half, 1
        got = swap(send, "animal", order[0])
        for bit in order[1:]:
            send, keep_e, keep_p = call(
                lambda *r, left=left, sources=sources: merge_body(plan, left, sources, *r),
                (got, keep_e, keep_p),
                (plan.tile(left // 2 * nb, half), plan.tile(left // 2 * nb), plan.tile(0, half)),
                placed=False,
            )
            left, sources = left // 2, sources * 2
            got = swap(send, "animal", bit)
        others = []
        for part in range(1, parts):
            other, keep = messages[2 * part + 1 : 2 * part + 3]
            for i, bit in enumerate(plan.orders[part]):
                got_e = swap(other, "animal", bit)
                size = half >> i
                outs = (plan.tile(size // 2 * nb),) * 2 if size > 1 else (plan.tile(nb),)
                keep, *other = call(add_body, (got_e, keep), outs, placed=False)
                other = other[0] if other else None
            others.append(keep)
        sent, keep_p, term, more = call(
            lambda *r: offspring_body(plan, bool(extra), *r),
            (place, got, keep_e, keep_p, field, parent_hot, weight, *extra),
            (plan.tile(nb, half), plan.tile(0, half), square, lines if extra else square),
        )
        got = swap(sent, "animal", order[-1])
        held, sources = 1, 1
        for bit in order[-2::-1]:
            sent, keep_p = call(
                lambda *r, held=held, sources=sources: spread_body(plan, held, sources, *r),
                (sent, got, keep_p),
                (plan.tile(2 * held * nb, half), plan.tile(0, half)),
                placed=False,
            )
            held, sources = held * 2, sources * 2
            got = swap(sent, "animal", bit)
        pairs = [(sent, got)]
        for part in range(1, parts):
            x = others[part - 1]
            for step, bit in enumerate(plan.orders[part][::-1]):
                got_e = swap(x, "animal", bit)
                if bit == plan.orders[part][0]:
                    pairs.append((x, got_e))
                else:
                    outs = (plan.tile(2 * nb << step),)
                    (x,) = call(join_body, (x, got_e), outs, placed=False)
        acc = (term, keep_p, gather_hot)
        tail = ((rows // 2 + (8 if op else 0), cols), F32)
        for index, group in enumerate(groups):
            first, last = index == 0, index == len(groups) - 1
            mine = [x for part in group for x in pairs[part]]
            if op:
                mine += [*(x for part in group for x in earlier[part]), more]
            outs = [tail, tail] if last else [square]
            if op and first:
                outs.append(lines)
            acc = call(
                lambda *r, group=group, first=first, last=last: values_body(
                    plan, group, first, last, *r
                ),
                (place, *kept[index], scale, *mine, *acc),
                outs,
                scratch=full,
                flops=work * len(group) // parts,
            )
            if op and first:
                sums = acc[-1]
                acc = acc if not last else acc[:-1]
        own, other = acc
        value = own + swap(other, "snp", 1)
        for bit in bits_of(blocks)[1:]:
            value = value + swap(value, "snp", bit)
        after = (more, sums) if op else (more, pairs)
        return value, swap(value, "snp", 1), *after

    own, other, plain, earlier = round_trip(0, plan, right_side, messages, (), None)
    image, flipped, sums, *messages = call(
        lambda *r: middle_body(summing, *r),
        (place, right_side, diagonal, own, other, *kept[0], gather_hot),
        (square, *turned, *summing.message_shapes(groups[0])),
        scratch=full,
        flops=work,
    )
    for index, group in enumerate(groups[1:]):
        messages += call(
            lambda *r, group=group: more_body(plan, group, *r),
            (*kept[index + 1], flipped, sums),
            plan.message_shapes(group),
            flops=work,
            placed=False,
        )
    own, other, dots, more = round_trip(
        1, summing, image, messages, (plain, diagonal, right_side), earlier
    )
    return call(
        final_body,
        (place, image, diagonal, own, other, right_side, dots, more),
        (square, square),
        scratch=full,
    )


def solution(mesh):
    placed = (
        P("animal", "snp"),
        P("snp"),
        P("animal", None),
        P("animal", None),
        P("animal"),
        P(),
        P("animal", None, None),
        P("animal"),
        P("animal"),
    )

    return jax.shard_map(
        local,
        mesh=mesh,
        in_specs=placed,
        out_specs=(P("animal", None), P("animal", None)),
        check_vma=False,
    )
```

profile of v0, /device:TPU:0, one launch (start us, length us, event | category | flops | bytes accessed | tf_op | source)
XLA Modules:
  0.0 181.0 jit_solution(14189893094399429621)
XLA Ops:
  0.7 8.8 %shard_map.104 = (bf16[1024,4096]{1,0:T(8,128)(2,1)S(1)}, f32[1,4096]{1,0:T(1,128)S(1)}, bf16[1024,512]{1,0:T(8,128)(2,1)S(1)}, bf16[512,1024]{1,0:T(8,128)(2,1)...) custom-call(s32[2]{0:T(128)S(1)} %pad_add_fusion.r_0_.place, ...), custom_call_target="tpu_custom_call" | custom-call | flops 2147483648 | bytes 17344520 | tf_op jit(solution)/shard_map/pallas_call | solution.py:21
  9.6 3.1 %collective-permute-start.12 = (bf16[1152,128]{1,0:T(8,128)(2,1)S(1)}, bf16[1152,128]{1,0:T(8,128)(2,1)S(1)}, u32[]{:S(2)}, u32[]{:S(2)}) collective-permute-start(bf16[1152,128]{1,0:T(8,128)(2,1)S(1)} %get-tuple-element.107), channel_id=1, source_target_pairs={{0,4},{4,0},{8,12},{12,8},{16,20},{20,16},{24,28},{28,24},{1,5},{5... | collective-permute-start | bytes 884744 | tf_op jit(solution)/shard_map/ppermute | solution.py:41
  14.1 4.6 %shard_map.105 = (bf16[1024,4096]{1,0:T(8,128)(2,1)S(1)}, f32[1,4096]{1,0:T(1,128)S(1)}, bf16[1024,128]{1,0:T(8,128)(2,1)S(1)}, bf16[1024,128]{1,0:T(8,128)(2,1)...) custom-call(s32[2]{0:T(128)S(1)} %pad_add_fusion.r_0_.place, bf16[1024,8192]{1,0:T(8,128)(2,1)} %r_1_.4, ...), custom_call_target="tpu_custom_call" | custom-call | flops 2147483648 | bytes 17137672 | tf_op jit(solution)/shard_map/pallas_call | solution.py:21
  19.7 1.9 %collective-permute-start.13 = (bf16[640,128]{1,0:T(8,128)(2,1)S(1)}, bf16[640,128]{1,0:T(8,128)(2,1)S(1)}, u32[]{:S(2)}, u32[]{:S(2)}) collective-permute-start(bf16[640,128]{1,0:T(8,128)(2,1)S(1)} %get-tuple-element.110), channel_id=1, source_target_pairs={{0,8},{4,12},{8,0},{12,4},{16,24},{20,28},{24,16},{28,20},{1,9},{5... | collective-permute-start | bytes 491528 | tf_op jit(solution)/shard_map/ppermute | solution.py:41
  21.7 2.5 %collective-permute-start.19 = (bf16[512,128]{1,0:T(8,128)(2,1)S(1)}, bf16[512,128]{1,0:T(8,128)(2,1)S(1)}, u32[]{:S(2)}, u32[]{:S(2)}) collective-permute-start(bf16[512,128]{1,0:T(8,128)(2,1)S(1)} %get-tuple-element.124), channel_id=1, source_target_pairs={{0,4},{4,0},{8,12},{12,8},{16,20},{20,16},{24,28},{28,24},{1,5},{5... | collective-permute-start | bytes 393224 | tf_op jit(solution)/shard_map/ppermute | solution.py:41
  24.2 5.8 %collective-permute-done.13.r_0_ = bf16[640,128]{1,0:T(8,128)(2,1)S(1)} collective-permute-done((bf16[640,128]{1,0:T(8,128)(2,1)S(1)}, bf16[640,128]{1,0:T(8,128)(2,1)S(1)}, u32[]{:S(2)}, u32[]{:S(2)}) %collective-permute-start.13) | collective-permute-done | bytes 163872 | tf_op jit(solution)/shard_map/ppermute | solution.py:41
  30.0 2.8 %collective-permute-start.14 = (bf16[384,128]{1,0:T(8,128)(2,1)S(1)}, bf16[384,128]{1,0:T(8,128)(2,1)S(1)}, u32[]{:S(2)}, u32[]{:S(2)}) collective-permute-start(bf16[384,128]{1,0:T(8,128)(2,1)S(1)} %get-tuple-element.113), channel_id=1, source_target_pairs={{0,16},{4,20},{8,24},{12,28},{16,0},{20,4},{24,8},{28,12},{1,17},{... | collective-permute-start | bytes 294920 | tf_op jit(solution)/shard_map/ppermute | solution.py:41
  35.1 1.6 collective-permute-done.14.r_1_
  36.8 2.5 %shard_map.118 = (bf16[384,128]{1,0:T(8,128)(2,1)S(1)}, bf16[128,128]{1,0:T(8,128)(2,1)S(1)}, f32[1024,128]{1,0:T(8,128)S(1)}, f32[1024,128]{1,0:T(8,128)S(1)}) custom-call(s32[2]{0:T(128)S(1)} %pad_add_fusion.r_0_.place, bf16[384,128]{1,0:T(8,128)(2,1)S(1)} %collective-permute-done.14.r_1_, bf16[256,128]{1,0:T(8,128)(2,1)S(1)} %get-tuple-element.114.r_2_, ...), custom_call_target="tpu_custom_call" | custom-call | bytes 1773576 | tf_op jit(solution)/shard_map/pallas_call | solution.py:21
  39.3 1.8 %collective-permute-start.15 = (bf16[384,128]{1,0:T(8,128)(2,1)S(1)}, bf16[384,128]{1,0:T(8,128)(2,1)S(1)}, u32[]{:S(2)}, u32[]{:S(2)}) collective-permute-start(bf16[384,128]{1,0:T(8,128)(2,1)S(1)} %get-tuple-element.117.r_0_), channel_id=1, source_target_pairs={{0,16},{4,20},{8,24},{12,28},{16,0},{20,4},{24,8},{28,12},{1,17},{... | collective-permute-start | bytes 294920 | tf_op jit(solution)/shard_map/ppermute | solution.py:41
  42.4 1.8 %collective-permute-start.2 = (bf16[256,128]{1,0:T(8,128)(2,1)S(1)}, bf16[256,128]{1,0:T(8,128)(2,1)S(1)}, u32[]{:S(2)}, u32[]{:S(2)}) collective-permute-start(bf16[256,128]{1,0:T(8,128)(2,1)S(1)} %get-tuple-element.97), channel_id=1, source_target_pairs={{0,16},{4,20},{8,24},{12,28},{16,0},{20,4},{24,8},{28,12},{1,17},{... | collective-permute-start | bytes 196616 | tf_op jit(solution)/shard_map/ppermute | solution.py:41
  45.5 6.1 %collective-permute-done.20.got = bf16[256,128]{1,0:T(8,128)(2,1)S(1)} collective-permute-done((bf16[256,128]{1,0:T(8,128)(2,1)S(1)}, bf16[256,128]{1,0:T(8,128)(2,1)S(1)}, u32[]{:S(2)}, u32[]{:S(2)}) %collective-permute-start.20) | collective-permute-done | bytes 65568 | tf_op jit(solution)/shard_map/ppermute | solution.py:41
  51.8 2.8 %collective-permute-start.16 = (bf16[640,128]{1,0:T(8,128)(2,1)S(1)}, bf16[640,128]{1,0:T(8,128)(2,1)S(1)}, u32[]{:S(2)}, u32[]{:S(2)}) collective-permute-start(bf16[640,128]{1,0:T(8,128)(2,1)S(1)} %get-tuple-element.119.r_0_), channel_id=1, source_target_pairs={{0,8},{4,12},{8,0},{12,4},{16,24},{20,28},{24,16},{28,20},{1,9},{5... | collective-permute-start | bytes 491528 | tf_op jit(solution)/shard_map/ppermute | solution.py:41
  54.9 2.8 %collective-permute-start.9 = (bf16[256,128]{1,0:T(8,128)(2,1)S(1)}, bf16[256,128]{1,0:T(8,128)(2,1)S(1)}, u32[]{:S(2)}, u32[]{:S(2)}) collective-permute-start(bf16[256,128]{1,0:T(8,128)(2,1)S(1)} %shard_map.113.sent), channel_id=1, source_target_pairs={{0,16},{4,20},{8,24},{12,28},{16,0},{20,4},{24,8},{28,12},{1,17},{... | collective-permute-start | bytes 196616 | tf_op jit(solution)/shard_map/ppermute | solution.py:41
  57.7 1.5 collective-permute-done.21.got
  59.8 2.0 %collective-permute-done.3.got = bf16[256,128]{1,0:T(8,128)(2,1)S(1)} collective-permute-done((bf16[256,128]{1,0:T(8,128)(2,1)S(1)}, bf16[256,128]{1,0:T(8,128)(2,1)S(1)}, u32[]{:S(2)}, u32[]{:S(2)}) %collective-permute-start.3) | collective-permute-done | bytes 65568 | tf_op jit(solution)/shard_map/ppermute | solution.py:41
  63.2 1.6 collective-permute-start.17
  70.5 3.6 %collective-permute-done.23.r_7_.r_11_ = bf16[1024,128]{1,0:T(8,128)(2,1)S(1)} collective-permute-done((bf16[1024,128]{1,0:T(8,128)(2,1)S(1)}, bf16[1024,128]{1,0:T(8,128)(2,1)S(1)}, u32[]{:S(2)}, u32[]{:S(2)}) %collective-permute-start.23) | collective-permute-done | bytes 262176 | tf_op jit(solution)/shard_map/ppermute | solution.py:41
  75.4 3.3 %shard_map.126.r_8_ = f32[1024,128]{1,0:T(8,128)S(1)} custom-call(s32[2]{0:T(128)S(1)} %pad_add_fusion.r_0_.place, bf16[1024,4096]{1,0:T(8,128)(2,1)S(1)} %get-tuple-element.105.r_1_.r_5_, f32[1,4096]{1,0:T(1,128)S(1)} %get-tuple-element.106.r_2_.r_6_, f32[1,128]{1,0:T(1,128)S(1)} %multiply_bitcast_fusion.r_3_, ...), custom_call_target="tpu_custom_call" | custom-call | flops 1073741824 | bytes 11125256 | tf_op jit(solution)/shard_map/pallas_call | solution.py:21
  79.3 3.0 %shard_map.127 = (f32[512,128]{1,0:T(8,128)S(1)}, f32[512,128]{1,0:T(8,128)S(1)}) custom-call(s32[2]{0:T(128)S(1)} %pad_add_fusion.r_0_.place, bf16[1024,4096]{1,0:T(8,128)(2,1)S(1)} %get-tuple-element.91.r_1_.r_0_, f32[1,4096]{1,0:T(1,128)S(1)} %get-tuple-element.92.r_2_.r_1_, f32[1,128]{1,0:T(1,128)S(1)} %multiply_bitcast_fusion.r_3_, ...), custom_call_target="tpu_custom_call" | custom-call | flops 1073741824 | bytes 9978376 | tf_op jit(solution)/shard_map/pallas_call | solution.py:21
  82.4 1.5 collective-permute-done.24
  84.0 1.6 collective-permute-start.25
  85.6 6.8 %collective-permute-done.25 = f32[512,128]{1,0:T(8,128)S(1)} collective-permute-done((f32[512,128]{1,0:T(8,128)S(1)}, f32[512,128]{1,0:T(8,128)S(1)}, u32[]{:S(2)}, u32[]{:S(2)}) %collective-permute-start.25) | collective-permute-done | bytes 262176 | tf_op jit(solution)/shard_map/ppermute | solution.py:41
  92.5 1.5 collective-permute-done.26.r_4_
  94.0 2.8 %shard_map.128 = (f32[1024,128]{1,0:T(8,128)S(1)}, bf16[128,1024]{1,0:T(8,128)(2,1)S(1)}, f32[128,128]{1,0:T(8,128)S(1)}, bf16[1216,128]{1,0:T(8,128)(2,1)S(1)},...) custom-call(s32[2]{0:T(128)S(1)} %pad_add_fusion.r_0_.place, ...), custom_call_target="tpu_custom_call" | custom-call | flops 2147483648 | bytes 11026440 | tf_op jit(solution)/shard_map/pallas_call | solution.py:21
  97.4 8.9 %collective-permute-done.39.r_0_ = bf16[1216,128]{1,0:T(8,128)(2,1)S(1)} collective-permute-done((bf16[1216,128]{1,0:T(8,128)(2,1)S(1)}, bf16[1216,128]{1,0:T(8,128)(2,1)S(1)}, u32[]{:S(2)}, u32[]{:S(2)}) %collective-permute-start.39) | collective-permute-done | bytes 311328 | tf_op jit(solution)/shard_map/ppermute | solution.py:41
  108.4 2.0 %collective-permute-start.33 = (bf16[1024,128]{1,0:T(8,128)(2,1)S(1)}, bf16[1024,128]{1,0:T(8,128)(2,1)S(1)}, u32[]{:S(2)}, u32[]{:S(2)}) collective-permute-start(bf16[1024,128]{1,0:T(8,128)(2,1)S(1)} %get-tuple-element.142), channel_id=1, source_target_pairs={{0,8},{4,12},{8,0},{12,4},{16,24},{20,28},{24,16},{28,20},{1,9},{5... | collective-permute-start | bytes 786440 | tf_op jit(solution)/shard_map/ppermute | solution.py:41
  110.3 3.5 %collective-permute-done.40.r_0_ = bf16[704,128]{1,0:T(8,128)(2,1)S(1)} collective-permute-done((bf16[704,128]{1,0:T(8,128)(2,1)S(1)}, bf16[704,128]{1,0:T(8,128)(2,1)S(1)}, u32[]{:S(2)}, u32[]{:S(2)}) %collective-permute-start.40) | collective-permute-done | bytes 180256 | tf_op jit(solution)/shard_map/ppermute | solution.py:41
  114.2 6.6 %collective-permute-done.41.r_1_ = bf16[448,128]{1,0:T(8,128)(2,1)S(1)} collective-permute-done((bf16[448,128]{1,0:T(8,128)(2,1)S(1)}, bf16[448,128]{1,0:T(8,128)(2,1)S(1)}, u32[]{:S(2)}, u32[]{:S(2)}) %collective-permute-start.41) | collective-permute-done | bytes 114720 | tf_op jit(solution)/shard_map/ppermute | solution.py:41
  120.8 2.6 %shard_map.142 = (bf16[448,128]{1,0:T(8,128)(2,1)S(1)}, bf16[192,128]{1,0:T(8,128)(2,1)S(1)}, f32[1024,128]{1,0:T(8,128)S(1)}, f32[8,128]{1,0:T(8,128)S(1)}) custom-call(s32[2]{0:T(128)S(1)} %pad_add_fusion.r_0_.place, bf16[448,128]{1,0:T(8,128)(2,1)S(1)} %collective-permute-done.41.r_1_, bf16[256,128]{1,0:T(8,128)(2,1)S(1)} %get-tuple-element.155.r_2_, ...), custom_call_target="tpu_custom_call" | custom-call | bytes 3379208 | tf_op jit(solution)/shard_map/pallas_call | solution.py:21
  124.3 1.7 collective-permute-start.28
  127.0 3.2 %collective-permute-done.42.r_1_ = bf16[448,128]{1,0:T(8,128)(2,1)S(1)} collective-permute-done((bf16[448,128]{1,0:T(8,128)(2,1)S(1)}, bf16[448,128]{1,0:T(8,128)(2,1)S(1)}, u32[]{:S(2)}, u32[]{:S(2)}) %collective-permute-start.42) | collective-permute-done | bytes 114720 | tf_op jit(solution)/shard_map/ppermute | solution.py:41
  130.2 1.7 collective-permute-done.47.got
  132.0 3.5 %collective-permute-start.48 = (bf16[256,128]{1,0:T(8,128)(2,1)S(1)}, bf16[256,128]{1,0:T(8,128)(2,1)S(1)}, u32[]{:S(2)}, u32[]{:S(2)}) collective-permute-start(bf16[256,128]{1,0:T(8,128)(2,1)S(1)} %shard_map.147.sent), channel_id=1, source_target_pairs={{0,16},{4,20},{8,24},{12,28},{16,0},{20,4},{24,8},{28,12},{1,17},{... | collective-permute-start | bytes 196616 | tf_op jit(solution)/shard_map/ppermute | solution.py:41
  135.7 3.0 %collective-permute-start.35 = (bf16[256,128]{1,0:T(8,128)(2,1)S(1)}, bf16[256,128]{1,0:T(8,128)(2,1)S(1)}, u32[]{:S(2)}, u32[]{:S(2)}) collective-permute-start(bf16[256,128]{1,0:T(8,128)(2,1)S(1)} %get-tuple-element.146), channel_id=1, source_target_pairs={{0,16},{4,20},{8,24},{12,28},{16,0},{20,4},{24,8},{28,12},{1,17},{... | collective-permute-start | bytes 196616 | tf_op jit(solution)/shard_map/ppermute | solution.py:41
  138.7 1.7 collective-permute-start.49
  140.4 2.9 %collective-permute-done.29.got = bf16[256,128]{1,0:T(8,128)(2,1)S(1)} collective-permute-done((bf16[256,128]{1,0:T(8,128)(2,1)S(1)}, bf16[256,128]{1,0:T(8,128)(2,1)S(1)}, u32[]{:S(2)}, u32[]{:S(2)}) %collective-permute-start.29) | collective-permute-done | bytes 65568 | tf_op jit(solution)/shard_map/ppermute | solution.py:41
  144.7 1.8 collective-permute-start.36
  147.7 1.5 collective-permute-done.30.got
  151.1 2.6 %collective-permute-start.50 = (bf16[1024,128]{1,0:T(8,128)(2,1)S(1)}, bf16[1024,128]{1,0:T(8,128)(2,1)S(1)}, u32[]{:S(2)}, u32[]{:S(2)}) collective-permute-start(bf16[1024,128]{1,0:T(8,128)(2,1)S(1)} %shard_map.149.r_6_), channel_id=1, source_target_pairs={{0,8},{4,12},{8,0},{12,4},{16,24},{20,28},{24,16},{28,20},{1,9},{5... | collective-permute-start | bytes 786440 | tf_op jit(solution)/shard_map/ppermute | solution.py:41
  153.8 1.8 %collective-permute-done.31.got = bf16[512,128]{1,0:T(8,128)(2,1)S(1)} collective-permute-done((bf16[512,128]{1,0:T(8,128)(2,1)S(1)}, bf16[512,128]{1,0:T(8,128)(2,1)S(1)}, u32[]{:S(2)}, u32[]{:S(2)}) %collective-permute-start.31) | collective-permute-done | bytes 131104 | tf_op jit(solution)/shard_map/ppermute | solution.py:41
  159.3 3.9 %shard_map.150 = (f32[1024,128]{1,0:T(8,128)S(1)}, f32[8,128]{1,0:T(8,128)S(1)}) custom-call(s32[2]{0:T(128)S(1)} %pad_add_fusion.r_0_.place, bf16[1024,4096]{1,0:T(8,128)(2,1)S(1)} %get-tuple-element.105.r_1_.r_5_, f32[1,4096]{1,0:T(1,128)S(1)} %get-tuple-element.106.r_2_.r_6_, f32[1,128]{1,0:T(1,128)S(1)} %multiply_bitcast_fusion.r_3_, ...), custom_call_target="tpu_custom_call" | custom-call | flops 1073741824 | bytes 12292616 | tf_op jit(solution)/shard_map/pallas_call | solution.py:21
  163.8 3.3 %shard_map.151 = (f32[520,128]{1,0:T(8,128)S(1)}, f32[520,128]{1,0:T(8,128)S(1)}) custom-call(s32[2]{0:T(128)S(1)} %pad_add_fusion.r_0_.place, bf16[1024,4096]{1,0:T(8,128)(2,1)S(1)} %get-tuple-element.91.r_1_.r_0_, f32[1,4096]{1,0:T(1,128)S(1)} %get-tuple-element.92.r_2_.r_1_, f32[1,128]{1,0:T(1,128)S(1)} %multiply_bitcast_fusion.r_3_, ...), custom_call_target="tpu_custom_call" | custom-call | flops 1073741824 | bytes 11035144 | tf_op jit(solution)/shard_map/pallas_call | solution.py:21
  167.2 1.5 collective-permute-done.51
  168.7 1.6 collective-permute-start.52
  170.3 6.9 %collective-permute-done.52 = f32[520,128]{1,0:T(8,128)S(1)} collective-permute-done((f32[520,128]{1,0:T(8,128)S(1)}, f32[520,128]{1,0:T(8,128)S(1)}, u32[]{:S(2)}, u32[]{:S(2)}) %collective-permute-start.52) | collective-permute-done | bytes 266272 | tf_op jit(solution)/shard_map/ppermute | solution.py:41
  177.4 1.5 collective-permute-done.53.other
  178.9 2.1 %shard_map.152 = (f32[1024,128]{1,0:T(8,128)}, f32[1024,128]{1,0:T(8,128)}) custom-call(s32[2]{0:T(128)S(1)} %pad_add_fusion.r_0_.place, f32[1024,128]{1,0:T(8,128)S(1)} %get-tuple-element.133.r_4_.field, f32[1024,128]{1,0:T(8,128)S(1)} %copy-done.1, f32[520,128]{1,0:T(8,128)S(1)} %add.15.own, f32[520,128]{1,0:T(8,128)S(1)} %collective-permute-done.53.other, ...), custom_call_target="tpu_custom_call" | custom-call | bytes 2113544 | tf_op jit(solution)/shard_map/pallas_call | solution.py:21
  (123 shorter events, 31.8 us)
Async XLA Ops:
  9.6 10.1 %collective-permute-start.12 = (bf16[1152,128]{1,0:T(8,128)(2,1)S(1)}, bf16[1152,128]{1,0:T(8,128)(2,1)S(1)}, u32[]{:S(2)}, u32[]{:S(2)}) collective-permute-start(bf16[1152,128]{1,0:T(8,128)(2,1)S(1)} %get-tuple-element.107), channel_id=1, source_target_pairs={{0,4},{4,0},{8,12},{12,8},{16,20},{20,16},{24,28},{28,24},{1,5},{5... | collective-permute-start | bytes 884744 | tf_op jit(solution)/shard_map/ppermute | solution.py:41
  12.6 9.0 %collective-permute-start.18 = (bf16[1024,128]{1,0:T(8,128)(2,1)S(1)}, bf16[1024,128]{1,0:T(8,128)(2,1)S(1)}, u32[]{:S(2)}, u32[]{:S(2)}) collective-permute-start(bf16[1024,128]{1,0:T(8,128)(2,1)S(1)} %get-tuple-element.122), channel_id=1, source_target_pairs={{0,8},{4,12},{8,0},{12,4},{16,24},{20,28},{24,16},{28,20},{1,9},{5... | collective-permute-start | bytes 786440 | tf_op jit(solution)/shard_map/ppermute | solution.py:41
  18.7 14.1 %collective-permute-start = (bf16[1024,128]{1,0:T(8,128)(2,1)S(1)}, bf16[1024,128]{1,0:T(8,128)(2,1)S(1)}, u32[]{:S(2)}, u32[]{:S(2)}) collective-permute-start(bf16[1024,128]{1,0:T(8,128)(2,1)S(1)} %get-tuple-element.93), channel_id=1, source_target_pairs={{0,4},{4,0},{8,12},{12,8},{16,20},{20,16},{24,28},{28,24},{1,5},{5... | collective-permute-start | bytes 786440 | tf_op jit(solution)/shard_map/ppermute | solution.py:41
  19.3 14.7 %collective-permute-start.6 = (bf16[1024,128]{1,0:T(8,128)(2,1)S(1)}, bf16[1024,128]{1,0:T(8,128)(2,1)S(1)}, u32[]{:S(2)}, u32[]{:S(2)}) collective-permute-start(bf16[1024,128]{1,0:T(8,128)(2,1)S(1)} %get-tuple-element.99), channel_id=1, source_target_pairs={{0,8},{4,12},{8,0},{12,4},{16,24},{20,28},{24,16},{28,20},{1,9},{5... | collective-permute-start | bytes 786440 | tf_op jit(solution)/shard_map/ppermute | solution.py:41
  19.7 10.3 %collective-permute-start.13 = (bf16[640,128]{1,0:T(8,128)(2,1)S(1)}, bf16[640,128]{1,0:T(8,128)(2,1)S(1)}, u32[]{:S(2)}, u32[]{:S(2)}) collective-permute-start(bf16[640,128]{1,0:T(8,128)(2,1)S(1)} %get-tuple-element.110), channel_id=1, source_target_pairs={{0,8},{4,12},{8,0},{12,4},{16,24},{20,28},{24,16},{28,20},{1,9},{5... | collective-permute-start | bytes 491528 | tf_op jit(solution)/shard_map/ppermute | solution.py:41
  21.7 19.4 %collective-permute-start.19 = (bf16[512,128]{1,0:T(8,128)(2,1)S(1)}, bf16[512,128]{1,0:T(8,128)(2,1)S(1)}, u32[]{:S(2)}, u32[]{:S(2)}) collective-permute-start(bf16[512,128]{1,0:T(8,128)(2,1)S(1)} %get-tuple-element.124), channel_id=1, source_target_pairs={{0,4},{4,0},{8,12},{12,8},{16,20},{20,16},{24,28},{28,24},{1,5},{5... | collective-permute-start | bytes 393224 | tf_op jit(solution)/shard_map/ppermute | solution.py:41
  30.0 6.7 %collective-permute-start.14 = (bf16[384,128]{1,0:T(8,128)(2,1)S(1)}, bf16[384,128]{1,0:T(8,128)(2,1)S(1)}, u32[]{:S(2)}, u32[]{:S(2)}) collective-permute-start(bf16[384,128]{1,0:T(8,128)(2,1)S(1)} %get-tuple-element.113), channel_id=1, source_target_pairs={{0,16},{4,20},{8,24},{12,28},{16,0},{20,4},{24,8},{28,12},{1,17},{... | collective-permute-start | bytes 294920 | tf_op jit(solution)/shard_map/ppermute | solution.py:41
  32.9 9.5 %collective-permute-start.1 = (bf16[512,128]{1,0:T(8,128)(2,1)S(1)}, bf16[512,128]{1,0:T(8,128)(2,1)S(1)}, u32[]{:S(2)}, u32[]{:S(2)}) collective-permute-start(bf16[512,128]{1,0:T(8,128)(2,1)S(1)} %get-tuple-element.95), channel_id=1, source_target_pairs={{0,8},{4,12},{8,0},{12,4},{16,24},{20,28},{24,16},{28,20},{1,9},{5... | collective-permute-start | bytes 393224 | tf_op jit(solution)/shard_map/ppermute | solution.py:41
  34.1 10.2 %collective-permute-start.7 = (bf16[512,128]{1,0:T(8,128)(2,1)S(1)}, bf16[512,128]{1,0:T(8,128)(2,1)S(1)}, u32[]{:S(2)}, u32[]{:S(2)}) collective-permute-start(bf16[512,128]{1,0:T(8,128)(2,1)S(1)} %get-tuple-element.101), channel_id=1, source_target_pairs={{0,4},{4,0},{8,12},{12,8},{16,20},{20,16},{24,28},{28,24},{1,5},{5... | collective-permute-start | bytes 393224 | tf_op jit(solution)/shard_map/ppermute | solution.py:41
  39.3 12.5 %collective-permute-start.15 = (bf16[384,128]{1,0:T(8,128)(2,1)S(1)}, bf16[384,128]{1,0:T(8,128)(2,1)S(1)}, u32[]{:S(2)}, u32[]{:S(2)}) collective-permute-start(bf16[384,128]{1,0:T(8,128)(2,1)S(1)} %get-tuple-element.117.r_0_), channel_id=1, source_target_pairs={{0,16},{4,20},{8,24},{12,28},{16,0},{20,4},{24,8},{28,12},{1,17},{... | collective-permute-start | bytes 294920 | tf_op jit(solution)/shard_map/ppermute | solution.py:41
  41.1 10.5 %collective-permute-start.20 = (bf16[256,128]{1,0:T(8,128)(2,1)S(1)}, bf16[256,128]{1,0:T(8,128)(2,1)S(1)}, u32[]{:S(2)}, u32[]{:S(2)}) collective-permute-start(bf16[256,128]{1,0:T(8,128)(2,1)S(1)} %get-tuple-element.126), channel_id=1, source_target_pairs={{0,16},{4,20},{8,24},{12,28},{16,0},{20,4},{24,8},{28,12},{1,17},{... | collective-permute-start | bytes 196616 | tf_op jit(solution)/shard_map/ppermute | solution.py:41
  42.4 12.2 %collective-permute-start.2 = (bf16[256,128]{1,0:T(8,128)(2,1)S(1)}, bf16[256,128]{1,0:T(8,128)(2,1)S(1)}, u32[]{:S(2)}, u32[]{:S(2)}) collective-permute-start(bf16[256,128]{1,0:T(8,128)(2,1)S(1)} %get-tuple-element.97), channel_id=1, source_target_pairs={{0,16},{4,20},{8,24},{12,28},{16,0},{20,4},{24,8},{28,12},{1,17},{... | collective-permute-start | bytes 196616 | tf_op jit(solution)/shard_map/ppermute | solution.py:41
  44.3 10.6 %collective-permute-start.8 = (bf16[256,128]{1,0:T(8,128)(2,1)S(1)}, bf16[256,128]{1,0:T(8,128)(2,1)S(1)}, u32[]{:S(2)}, u32[]{:S(2)}) collective-permute-start(bf16[256,128]{1,0:T(8,128)(2,1)S(1)} %get-tuple-element.103), channel_id=1, source_target_pairs={{0,16},{4,20},{8,24},{12,28},{16,0},{20,4},{24,8},{28,12},{1,17},{... | collective-permute-start | bytes 196616 | tf_op jit(solution)/shard_map/ppermute | solution.py:41
  51.6 7.5 %collective-permute-start.21 = (bf16[256,128]{1,0:T(8,128)(2,1)S(1)}, bf16[256,128]{1,0:T(8,128)(2,1)S(1)}, u32[]{:S(2)}, u32[]{:S(2)}) collective-permute-start(bf16[256,128]{1,0:T(8,128)(2,1)S(1)} %shard_map.123.sent), channel_id=1, source_target_pairs={{0,16},{4,20},{8,24},{12,28},{16,0},{20,4},{24,8},{28,12},{1,17},{... | collective-permute-start | bytes 196616 | tf_op jit(solution)/shard_map/ppermute | solution.py:41
  51.8 11.5 %collective-permute-start.16 = (bf16[640,128]{1,0:T(8,128)(2,1)S(1)}, bf16[640,128]{1,0:T(8,128)(2,1)S(1)}, u32[]{:S(2)}, u32[]{:S(2)}) collective-permute-start(bf16[640,128]{1,0:T(8,128)(2,1)S(1)} %get-tuple-element.119.r_0_), channel_id=1, source_target_pairs={{0,8},{4,12},{8,0},{12,4},{16,24},{20,28},{24,16},{28,20},{1,9},{5... | collective-permute-start | bytes 491528 | tf_op jit(solution)/shard_map/ppermute | solution.py:41
  54.6 7.3 %collective-permute-start.3 = (bf16[256,128]{1,0:T(8,128)(2,1)S(1)}, bf16[256,128]{1,0:T(8,128)(2,1)S(1)}, u32[]{:S(2)}, u32[]{:S(2)}) collective-permute-start(bf16[256,128]{1,0:T(8,128)(2,1)S(1)} %shard_map.108.sent), channel_id=1, source_target_pairs={{0,16},{4,20},{8,24},{12,28},{16,0},{20,4},{24,8},{28,12},{1,17},{... | collective-permute-start | bytes 196616 | tf_op jit(solution)/shard_map/ppermute | solution.py:41
  54.9 7.8 %collective-permute-start.9 = (bf16[256,128]{1,0:T(8,128)(2,1)S(1)}, bf16[256,128]{1,0:T(8,128)(2,1)S(1)}, u32[]{:S(2)}, u32[]{:S(2)}) collective-permute-start(bf16[256,128]{1,0:T(8,128)(2,1)S(1)} %shard_map.113.sent), channel_id=1, source_target_pairs={{0,16},{4,20},{8,24},{12,28},{16,0},{20,4},{24,8},{28,12},{1,17},{... | collective-permute-start | bytes 196616 | tf_op jit(solution)/shard_map/ppermute | solution.py:41
  59.1 5.7 %collective-permute-start.22 = (bf16[512,128]{1,0:T(8,128)(2,1)S(1)}, bf16[512,128]{1,0:T(8,128)(2,1)S(1)}, u32[]{:S(2)}, u32[]{:S(2)}) collective-permute-start(bf16[512,128]{1,0:T(8,128)(2,1)S(1)} %shard_map.124.sent), channel_id=1, source_target_pairs={{0,4},{4,0},{8,12},{12,8},{16,20},{20,16},{24,28},{28,24},{1,5},{5... | collective-permute-start | bytes 393224 | tf_op jit(solution)/shard_map/ppermute | solution.py:41
  62.7 6.4 %collective-permute-start.10 = (bf16[512,128]{1,0:T(8,128)(2,1)S(1)}, bf16[512,128]{1,0:T(8,128)(2,1)S(1)}, u32[]{:S(2)}, u32[]{:S(2)}) collective-permute-start(bf16[512,128]{1,0:T(8,128)(2,1)S(1)} %shard_map.114.sent), channel_id=1, source_target_pairs={{0,4},{4,0},{8,12},{12,8},{16,20},{20,16},{24,28},{28,24},{1,5},{5... | collective-permute-start | bytes 393224 | tf_op jit(solution)/shard_map/ppermute | solution.py:41
  63.2 12.2 %collective-permute-start.17 = (bf16[1152,128]{1,0:T(8,128)(2,1)S(1)}, bf16[1152,128]{1,0:T(8,128)(2,1)S(1)}, u32[]{:S(2)}, u32[]{:S(2)}) collective-permute-start(bf16[1152,128]{1,0:T(8,128)(2,1)S(1)} %get-tuple-element.121.r_4_.r_8_), channel_id=1, source_target_pairs={{0,4},{4,0},{8,12},{12,8},{16,20},{20,16},{24,28},{28,24},{1,5},{5... | collective-permute-start | bytes 884744 | tf_op jit(solution)/shard_map/ppermute | solution.py:41
  64.9 9.2 %collective-permute-start.23 = (bf16[1024,128]{1,0:T(8,128)(2,1)S(1)}, bf16[1024,128]{1,0:T(8,128)(2,1)S(1)}, u32[]{:S(2)}, u32[]{:S(2)}) collective-permute-start(bf16[1024,128]{1,0:T(8,128)(2,1)S(1)} %shard_map.125.r_6_.r_10_), channel_id=1, source_target_pairs={{0,8},{4,12},{8,0},{12,4},{16,24},{20,28},{24,16},{28,20},{1,9},{5... | collective-permute-start | bytes 786440 | tf_op jit(solution)/shard_map/ppermute | solution.py:41
  67.6 11.7 %collective-permute-start.5 = (bf16[1024,128]{1,0:T(8,128)(2,1)S(1)}, bf16[1024,128]{1,0:T(8,128)(2,1)S(1)}, u32[]{:S(2)}, u32[]{:S(2)}) collective-permute-start(bf16[1024,128]{1,0:T(8,128)(2,1)S(1)} %shard_map.110.r_4_.r_8_), channel_id=1, source_target_pairs={{0,4},{4,0},{8,12},{12,8},{16,20},{20,16},{24,28},{28,24},{1,5},{5... | collective-permute-start | bytes 786440 | tf_op jit(solution)/shard_map/ppermute | solution.py:41
  69.1 10.2 %collective-permute-start.11 = (bf16[1024,128]{1,0:T(8,128)(2,1)S(1)}, bf16[1024,128]{1,0:T(8,128)(2,1)S(1)}, u32[]{:S(2)}, u32[]{:S(2)}) collective-permute-start(bf16[1024,128]{1,0:T(8,128)(2,1)S(1)} %shard_map.115.r_6_.r_10_), channel_id=1, source_target_pairs={{0,8},{4,12},{8,0},{12,4},{16,24},{20,28},{24,16},{28,20},{1,9},{5... | collective-permute-start | bytes 786440 | tf_op jit(solution)/shard_map/ppermute | solution.py:41
  84.0 8.4 %collective-permute-start.25 = (f32[512,128]{1,0:T(8,128)S(1)}, f32[512,128]{1,0:T(8,128)S(1)}, u32[]{:S(2)}, u32[]{:S(2)}) collective-permute-start(f32[512,128]{1,0:T(8,128)S(1)} %add.12), channel_id=1, source_target_pairs={{0,2},{1,3},{2,0},{3,1},{4,6},{5,7},{6,4},{7,5},{8,10},{9,11},{10,... | collective-permute-start | bytes 786440 | tf_op jit(solution)/shard_map/ppermute | solution.py:41
  96.9 9.5 %collective-permute-start.39 = (bf16[1216,128]{1,0:T(8,128)(2,1)S(1)}, bf16[1216,128]{1,0:T(8,128)(2,1)S(1)}, u32[]{:S(2)}, u32[]{:S(2)}) collective-permute-start(bf16[1216,128]{1,0:T(8,128)(2,1)S(1)} %get-tuple-element.148), channel_id=1, source_target_pairs={{0,4},{4,0},{8,12},{12,8},{16,20},{20,16},{24,28},{28,24},{1,5},{5... | collective-permute-start | bytes 933896 | tf_op jit(solution)/shard_map/ppermute | solution.py:41
  97.4 16.6 %collective-permute-start.45 = (bf16[1024,128]{1,0:T(8,128)(2,1)S(1)}, bf16[1024,128]{1,0:T(8,128)(2,1)S(1)}, u32[]{:S(2)}, u32[]{:S(2)}) collective-permute-start(bf16[1024,128]{1,0:T(8,128)(2,1)S(1)} %get-tuple-element.164), channel_id=1, source_target_pairs={{0,8},{4,12},{8,0},{12,4},{16,24},{20,28},{24,16},{28,20},{1,9},{5... | collective-permute-start | bytes 786440 | tf_op jit(solution)/shard_map/ppermute | solution.py:41
  106.4 7.5 %collective-permute-start.40 = (bf16[704,128]{1,0:T(8,128)(2,1)S(1)}, bf16[704,128]{1,0:T(8,128)(2,1)S(1)}, u32[]{:S(2)}, u32[]{:S(2)}) collective-permute-start(bf16[704,128]{1,0:T(8,128)(2,1)S(1)} %get-tuple-element.151), channel_id=1, source_target_pairs={{0,8},{4,12},{8,0},{12,4},{16,24},{20,28},{24,16},{28,20},{1,9},{5... | collective-permute-start | bytes 540680 | tf_op jit(solution)/shard_map/ppermute | solution.py:41
  107.8 16.4 %collective-permute-start.27 = (bf16[1024,128]{1,0:T(8,128)(2,1)S(1)}, bf16[1024,128]{1,0:T(8,128)(2,1)S(1)}, u32[]{:S(2)}, u32[]{:S(2)}) collective-permute-start(bf16[1024,128]{1,0:T(8,128)(2,1)S(1)} %get-tuple-element.136), channel_id=1, source_target_pairs={{0,4},{4,0},{8,12},{12,8},{16,20},{20,16},{24,28},{28,24},{1,5},{5... | collective-permute-start | bytes 786440 | tf_op jit(solution)/shard_map/ppermute | solution.py:41
  108.4 17.7 %collective-permute-start.33 = (bf16[1024,128]{1,0:T(8,128)(2,1)S(1)}, bf16[1024,128]{1,0:T(8,128)(2,1)S(1)}, u32[]{:S(2)}, u32[]{:S(2)}) collective-permute-start(bf16[1024,128]{1,0:T(8,128)(2,1)S(1)} %get-tuple-element.142), channel_id=1, source_target_pairs={{0,8},{4,12},{8,0},{12,4},{16,24},{20,28},{24,16},{28,20},{1,9},{5... | collective-permute-start | bytes 786440 | tf_op jit(solution)/shard_map/ppermute | solution.py:41
  113.9 6.9 %collective-permute-start.41 = (bf16[448,128]{1,0:T(8,128)(2,1)S(1)}, bf16[448,128]{1,0:T(8,128)(2,1)S(1)}, u32[]{:S(2)}, u32[]{:S(2)}) collective-permute-start(bf16[448,128]{1,0:T(8,128)(2,1)S(1)} %get-tuple-element.154), channel_id=1, source_target_pairs={{0,16},{4,20},{8,24},{12,28},{16,0},{20,4},{24,8},{28,12},{1,17},{... | collective-permute-start | bytes 344072 | tf_op jit(solution)/shard_map/ppermute | solution.py:41
  114.1 12.1 %collective-permute-start.46 = (bf16[512,128]{1,0:T(8,128)(2,1)S(1)}, bf16[512,128]{1,0:T(8,128)(2,1)S(1)}, u32[]{:S(2)}, u32[]{:S(2)}) collective-permute-start(bf16[512,128]{1,0:T(8,128)(2,1)S(1)} %get-tuple-element.166), channel_id=1, source_target_pairs={{0,4},{4,0},{8,12},{12,8},{16,20},{20,16},{24,28},{28,24},{1,5},{5... | collective-permute-start | bytes 393224 | tf_op jit(solution)/shard_map/ppermute | solution.py:41
  123.4 6.7 %collective-permute-start.42 = (bf16[448,128]{1,0:T(8,128)(2,1)S(1)}, bf16[448,128]{1,0:T(8,128)(2,1)S(1)}, u32[]{:S(2)}, u32[]{:S(2)}) collective-permute-start(bf16[448,128]{1,0:T(8,128)(2,1)S(1)} %get-tuple-element.159.r_0_), channel_id=1, source_target_pairs={{0,16},{4,20},{8,24},{12,28},{16,0},{20,4},{24,8},{28,12},{1,17},{... | collective-permute-start | bytes 344072 | tf_op jit(solution)/shard_map/ppermute | solution.py:41
  124.3 11.3 %collective-permute-start.28 = (bf16[512,128]{1,0:T(8,128)(2,1)S(1)}, bf16[512,128]{1,0:T(8,128)(2,1)S(1)}, u32[]{:S(2)}, u32[]{:S(2)}) collective-permute-start(bf16[512,128]{1,0:T(8,128)(2,1)S(1)} %get-tuple-element.138), channel_id=1, source_target_pairs={{0,8},{4,12},{8,0},{12,4},{16,24},{20,28},{24,16},{28,20},{1,9},{5... | collective-permute-start | bytes 393224 | tf_op jit(solution)/shard_map/ppermute | solution.py:41
  126.1 9.6 %collective-permute-start.34 = (bf16[512,128]{1,0:T(8,128)(2,1)S(1)}, bf16[512,128]{1,0:T(8,128)(2,1)S(1)}, u32[]{:S(2)}, u32[]{:S(2)}) collective-permute-start(bf16[512,128]{1,0:T(8,128)(2,1)S(1)} %get-tuple-element.144), channel_id=1, source_target_pairs={{0,4},{4,0},{8,12},{12,8},{16,20},{20,16},{24,28},{28,24},{1,5},{5... | collective-permute-start | bytes 393224 | tf_op jit(solution)/shard_map/ppermute | solution.py:41
  126.2 5.7 %collective-permute-start.47 = (bf16[256,128]{1,0:T(8,128)(2,1)S(1)}, bf16[256,128]{1,0:T(8,128)(2,1)S(1)}, u32[]{:S(2)}, u32[]{:S(2)}) collective-permute-start(bf16[256,128]{1,0:T(8,128)(2,1)S(1)} %get-tuple-element.168), channel_id=1, source_target_pairs={{0,16},{4,20},{8,24},{12,28},{16,0},{20,4},{24,8},{28,12},{1,17},{... | collective-permute-start | bytes 196616 | tf_op jit(solution)/shard_map/ppermute | solution.py:41
  130.2 16.3 %collective-permute-start.43 = (bf16[704,128]{1,0:T(8,128)(2,1)S(1)}, bf16[704,128]{1,0:T(8,128)(2,1)S(1)}, u32[]{:S(2)}, u32[]{:S(2)}) collective-permute-start(bf16[704,128]{1,0:T(8,128)(2,1)S(1)} %get-tuple-element.161.r_0_), channel_id=1, source_target_pairs={{0,8},{4,12},{8,0},{12,4},{16,24},{20,28},{24,16},{28,20},{1,9},{5... | collective-permute-start | bytes 540680 | tf_op jit(solution)/shard_map/ppermute | solution.py:41
  132.0 6.7 %collective-permute-start.48 = (bf16[256,128]{1,0:T(8,128)(2,1)S(1)}, bf16[256,128]{1,0:T(8,128)(2,1)S(1)}, u32[]{:S(2)}, u32[]{:S(2)}) collective-permute-start(bf16[256,128]{1,0:T(8,128)(2,1)S(1)} %shard_map.147.sent), channel_id=1, source_target_pairs={{0,16},{4,20},{8,24},{12,28},{16,0},{20,4},{24,8},{28,12},{1,17},{... | collective-permute-start | bytes 196616 | tf_op jit(solution)/shard_map/ppermute | solution.py:41
  135.6 7.7 %collective-permute-start.29 = (bf16[256,128]{1,0:T(8,128)(2,1)S(1)}, bf16[256,128]{1,0:T(8,128)(2,1)S(1)}, u32[]{:S(2)}, u32[]{:S(2)}) collective-permute-start(bf16[256,128]{1,0:T(8,128)(2,1)S(1)} %get-tuple-element.140), channel_id=1, source_target_pairs={{0,16},{4,20},{8,24},{12,28},{16,0},{20,4},{24,8},{28,12},{1,17},{... | collective-permute-start | bytes 196616 | tf_op jit(solution)/shard_map/ppermute | solution.py:41
  135.7 8.9 %collective-permute-start.35 = (bf16[256,128]{1,0:T(8,128)(2,1)S(1)}, bf16[256,128]{1,0:T(8,128)(2,1)S(1)}, u32[]{:S(2)}, u32[]{:S(2)}) collective-permute-start(bf16[256,128]{1,0:T(8,128)(2,1)S(1)} %get-tuple-element.146), channel_id=1, source_target_pairs={{0,16},{4,20},{8,24},{12,28},{16,0},{20,4},{24,8},{28,12},{1,17},{... | collective-permute-start | bytes 196616 | tf_op jit(solution)/shard_map/ppermute | solution.py:41
  138.7 12.4 %collective-permute-start.49 = (bf16[512,128]{1,0:T(8,128)(2,1)S(1)}, bf16[512,128]{1,0:T(8,128)(2,1)S(1)}, u32[]{:S(2)}, u32[]{:S(2)}) collective-permute-start(bf16[512,128]{1,0:T(8,128)(2,1)S(1)} %shard_map.148.sent), channel_id=1, source_target_pairs={{0,4},{4,0},{8,12},{12,8},{16,20},{20,16},{24,28},{28,24},{1,5},{5... | collective-permute-start | bytes 393224 | tf_op jit(solution)/shard_map/ppermute | solution.py:41
  143.3 5.8 %collective-permute-start.30 = (bf16[256,128]{1,0:T(8,128)(2,1)S(1)}, bf16[256,128]{1,0:T(8,128)(2,1)S(1)}, u32[]{:S(2)}, u32[]{:S(2)}) collective-permute-start(bf16[256,128]{1,0:T(8,128)(2,1)S(1)} %shard_map.132.sent), channel_id=1, source_target_pairs={{0,16},{4,20},{8,24},{12,28},{16,0},{20,4},{24,8},{28,12},{1,17},{... | collective-permute-start | bytes 196616 | tf_op jit(solution)/shard_map/ppermute | solution.py:41
  146.4 12.8 %collective-permute-start.44 = (bf16[1216,128]{1,0:T(8,128)(2,1)S(1)}, bf16[1216,128]{1,0:T(8,128)(2,1)S(1)}, u32[]{:S(2)}, u32[]{:S(2)}) collective-permute-start(bf16[1216,128]{1,0:T(8,128)(2,1)S(1)} %get-tuple-element.163.r_4_), channel_id=1, source_target_pairs={{0,4},{4,0},{8,12},{12,8},{16,20},{20,16},{24,28},{28,24},{1,5},{5... | collective-permute-start | bytes 933896 | tf_op jit(solution)/shard_map/ppermute | solution.py:41
  149.2 6.4 %collective-permute-start.31 = (bf16[512,128]{1,0:T(8,128)(2,1)S(1)}, bf16[512,128]{1,0:T(8,128)(2,1)S(1)}, u32[]{:S(2)}, u32[]{:S(2)}) collective-permute-start(bf16[512,128]{1,0:T(8,128)(2,1)S(1)} %shard_map.133.sent), channel_id=1, source_target_pairs={{0,8},{4,12},{8,0},{12,4},{16,24},{20,28},{24,16},{28,20},{1,9},{5... | collective-permute-start | bytes 393224 | tf_op jit(solution)/shard_map/ppermute | solution.py:41
  149.9 7.5 %collective-permute-start.37 = (bf16[512,128]{1,0:T(8,128)(2,1)S(1)}, bf16[512,128]{1,0:T(8,128)(2,1)S(1)}, u32[]{:S(2)}, u32[]{:S(2)}) collective-permute-start(bf16[512,128]{1,0:T(8,128)(2,1)S(1)} %shard_map.138.sent), channel_id=1, source_target_pairs={{0,4},{4,0},{8,12},{12,8},{16,20},{20,16},{24,28},{28,24},{1,5},{5... | collective-permute-start | bytes 393224 | tf_op jit(solution)/shard_map/ppermute | solution.py:41
  151.1 8.2 %collective-permute-start.50 = (bf16[1024,128]{1,0:T(8,128)(2,1)S(1)}, bf16[1024,128]{1,0:T(8,128)(2,1)S(1)}, u32[]{:S(2)}, u32[]{:S(2)}) collective-permute-start(bf16[1024,128]{1,0:T(8,128)(2,1)S(1)} %shard_map.149.r_6_), channel_id=1, source_target_pairs={{0,8},{4,12},{8,0},{12,4},{16,24},{20,28},{24,16},{28,20},{1,9},{5... | collective-permute-start | bytes 786440 | tf_op jit(solution)/shard_map/ppermute | solution.py:41
  155.6 7.5 %collective-permute-start.32 = (bf16[1024,128]{1,0:T(8,128)(2,1)S(1)}, bf16[1024,128]{1,0:T(8,128)(2,1)S(1)}, u32[]{:S(2)}, u32[]{:S(2)}) collective-permute-start(bf16[1024,128]{1,0:T(8,128)(2,1)S(1)} %shard_map.134.r_4_), channel_id=1, source_target_pairs={{0,4},{4,0},{8,12},{12,8},{16,20},{20,16},{24,28},{28,24},{1,5},{5... | collective-permute-start | bytes 786440 | tf_op jit(solution)/shard_map/ppermute | solution.py:41
  157.4 6.4 %collective-permute-start.38 = (bf16[1024,128]{1,0:T(8,128)(2,1)S(1)}, bf16[1024,128]{1,0:T(8,128)(2,1)S(1)}, u32[]{:S(2)}, u32[]{:S(2)}) collective-permute-start(bf16[1024,128]{1,0:T(8,128)(2,1)S(1)} %shard_map.139.r_6_), channel_id=1, source_target_pairs={{0,8},{4,12},{8,0},{12,4},{16,24},{20,28},{24,16},{28,20},{1,9},{5... | collective-permute-start | bytes 786440 | tf_op jit(solution)/shard_map/ppermute | solution.py:41
  168.7 8.5 %collective-permute-start.52 = (f32[520,128]{1,0:T(8,128)S(1)}, f32[520,128]{1,0:T(8,128)S(1)}, u32[]{:S(2)}, u32[]{:S(2)}) collective-permute-start(f32[520,128]{1,0:T(8,128)S(1)} %add.14), channel_id=1, source_target_pairs={{0,2},{1,3},{2,0},{3,1},{4,6},{5,7},{6,4},{7,5},{8,10},{9,11},{10,... | collective-permute-start | bytes 798728 | tf_op jit(solution)/shard_map/ppermute | solution.py:41
  (10 other events, 129.8 us)
where the time goes:
time: 181 us
  waiting for transfers between devices  79.8 us (44%)
  starting transfers between devices  60.5 us (33%)
  Pallas kernels  39.4 us (22%)
    ppermute x54, waiting for transfers between devices, swap(): return lax.ppermute(x, axis, [(i, i ^ bit) for i in range(size)])  79.8 us
    ppermute x54, starting transfers between devices, swap(): return lax.ppermute(x, axis, [(i, i ^ bit) for i in range(size)])  60.5 us
    pallas_call x49, Pallas kernels, call(): pl.pallas_call(body, in_specs=[SMEM, *specs] if placed else [VMEM] * len(...  39.4 us
  transfers between devices with their start and end apart: 54, of which 31 were waited for; matrix products, arithmetic and copies ran while one was open for 0% of the time, Pallas kernels for 11%

commit v1 on v0

--- a/solution.py
+++ b/solution.py
@@ -83,7 +83,8 @@
         self.nb = self.width // LANES
         bits = bits_of(self.owners)
         flip = [bits[1], bits[0], *bits[2:]]
-        self.orders = [bits if part % 2 == 0 else flip for part in range(self.parts)]
+        early = [bits[0], *bits[2:], bits[1]]
+        self.orders = [bits, flip, early, flip][: self.parts]
         self.bits = bits
         self.sets = [[0, 1], [2, 3]] if self.parts == 4 else [list(range(self.parts))]
 
@@ -218,11 +219,9 @@
             out[row : row + LANES] = acc[:, first : first + LANES]
 
 
-def emit_rows(plan, place, field, gather_hot, messages, sums=None):
+def emit_rows(plan, place, field, gather_turned, messages, sums=None):
     mixed = plan.mix(plan.fold(plan.mine(place, field))).astype(BF16)
-    rows = lax.dot_general(
-        gather_hot[...], mixed, (((0,), (0,)), ((), ())), preferred_element_type=F32
-    )
+    rows = jnp.dot(gather_turned[...], mixed, preferred_element_type=F32)
     offset = plan.half * plan.nb * LANES
     put_rows(plan, plan.bits, plan.pack(rows), messages[0], offset, messages[2], sums)
 
@@ -230,6 +229,15 @@
 def turn(field):
     turned = field.T.astype(BF16)
     return turned, jnp.sum(turned.astype(F32), axis=1, keepdims=True)
+
+
+def fill_index(plan, place, send_rows, index):
+    packed = plan.packed
+    for r in range(plan.owners):
+        line = send_rows[pl.ds(place[0] ^ r, 1), :]
+        for k in range(plan.kinds):
+            first = k * plan.pedigree + r * packed
+            index[:, first : first + packed] = line[:, k * packed : (k + 1) * packed]
 
 
 def turn_out(field, flipped, sums):
@@ -239,46 +247,59 @@
     return turned, side
 
 
-def begin_body(plan, place, geno, freq, right_in, send_in, sire_in, dam_in,
-               kept, kept_freq, gather_hot, parent_hot, flipped, sums, *rest):
-    messages, scratch = rest[:-8], rest[-8:]
-    right, send_rows, sire, dam, index, sem, freq_sem, small_sem = scratch
-    pairs = ((send_in, send_rows), (sire_in, sire), (dam_in, dam), (right_in, right))
+def begin_body(plan, place, geno, freq, right_in, send_in,
+               kept, kept_freq, gather_turned, flipped, sums, *rest):
+    messages, scratch = rest[:-6], rest[-6:]
+    right, send_rows, index, sem, freq_sem, small_sem = scratch
+    pairs = ((send_in, send_rows), (right_in, right))
     small = [pltpu.make_async_copy(*pair, small_sem.at[i]) for i, pair in enumerate(pairs)]
     for copy in small:
         copy.start()
     group = plan.sets[0]
     copies = copy_in(plan, group, place, geno, freq, kept, kept_freq, sem, freq_sem)
-    me, slots, packed = place[0], plan.slots, plan.packed
-    shift, short = slots.bit_length() - 1, packed.bit_length() - 1
-    for copy in small[:3]:
-        copy.wait()
-    for r in range(plan.owners):
-        line = send_rows[pl.ds(me ^ r, 1), :]
-        for k in range(plan.kinds):
-            first = k * plan.pedigree + r * packed
-            index[:, first : first + packed] = line[:, k * packed : (k + 1) * packed]
-
-    def spot(slot):
-        owner, row = (slot >> shift) ^ me, slot & (slots - 1)
-        return (row >> short) * plan.pedigree + (owner << short) + (row & (packed - 1))
-
-    sires, dams = spot(sire[...]), spot(dam[...])
-    animal = lax.broadcasted_iota(I32, (plan.rows, LANES), 0)
-    row = lax.broadcasted_iota(I32, (LANES, plan.rows), 0)
-    for first in range(0, plan.owners * slots, LANES):
-        here = slice(first, first + LANES)
-        gather_hot[:, here] = jnp.where(animal == index[:, here], 1.0, 0.0).astype(BF16)
-        hot = jnp.where(row == sires - first, 1.0, 0.0) + jnp.where(row == dams - first, 1.0, 0.0)
-        parent_hot[here, :] = hot.astype(BF16)
-    for copy in small[3:]:
-        copy.wait()
-    emit_rows(plan, place, right[...], gather_hot, messages)
+    small[0].wait()
+    fill_index(plan, place, send_rows, index)
+    tall = jnp.broadcast_to(index[...].astype(F32), (LANES, index.shape[1])).T
+    lane = lax.broadcasted_iota(I32, tall.shape, 1).astype(F32)
+    for first in range(0, plan.rows, LANES):
+        hot = jnp.where(lane + first == tall, 1.0, 0.0)
+        gather_turned[:, first : first + LANES] = hot.astype(BF16)
+    small[1].wait()
+    emit_rows(plan, place, right[...], gather_turned, messages)
     turned, side = turn_out(right[...], flipped, sums)
     for r in range(plan.owners):
         for copy in copies[r]:
             copy.wait()
         put_effects(plan, group, r, kept, kept_freq, turned, side, messages)
+
+
+def tables_body(plan, place, sire, dam, mendelian, send_rows, parent_hot, parent_turned, weight,
+                gather_hot, index):
+    me, slots, packed = place[0], plan.slots, plan.packed
+    shift, short = slots.bit_length() - 1, packed.bit_length() - 1
+
+    def spot(slot):
+        owner, row = (slot >> shift) ^ me, slot & (slots - 1)
+        return (row >> short) * plan.pedigree + (owner << short) + (row & (packed - 1))
+
+    def column(line):
+        return jnp.broadcast_to(line, (LANES, plan.rows)).T
+
+    sires, dams = spot(sire[...]), spot(dam[...])
+    tall = [column(x.astype(F32)) for x in (sires, dams)]
+    weight[...] = column(mendelian[...])
+    fill_index(plan, place, send_rows, index)
+    animal = lax.broadcasted_iota(I32, (plan.rows, LANES), 0)
+    row = lax.broadcasted_iota(I32, (LANES, plan.rows), 0)
+    lane = lax.broadcasted_iota(I32, (plan.rows, LANES), 1).astype(F32)
+    for first in range(0, plan.owners * slots, LANES):
+        here = slice(first, first + LANES)
+        hot = jnp.where(row == sires - first, 1.0, 0.0) + jnp.where(row == dams - first, 1.0, 0.0)
+        parent_hot[here, :] = hot.astype(BF16)
+        hot = jnp.where(lane + first == tall[0], 1.0, 0.0)
+        hot = hot + jnp.where(lane + first == tall[1], 1.0, 0.0)
+        parent_turned[:, here] = hot.astype(BF16)
+        gather_hot[:, here] = jnp.where(animal == index[:, here], 1.0, 0.0).astype(BF16)
 
 
 def begin_more_body(plan, group, place, geno, freq, flipped, sums, kept, kept_freq, *rest):
@@ -322,7 +343,8 @@
     out[size:] = got[...]
 
 
-def offspring_body(plan, second, place, got, keep_e, keep_p, field, parent_hot, mendelian, *rest):
+def offspring_body(plan, second, place, got, keep_e, keep_p, field, parent_hot, parent_turned,
+                   weight, *rest):
     if second:
         plain_before, diagonal, right, *rest = rest
     send, keep_back, term, extra = rest
@@ -331,18 +353,12 @@
     blocks, under = take_rows(plan, keep_p, got, edge)
     received = jnp.concatenate(blocks, axis=0)
     pieces = [
-        lax.dot_general(
-            parent_hot[k * size : (k + 1) * size],
-            received,
-            (((0,), (0,)), ((), ())),
-            preferred_element_type=F32,
-        )
+        jnp.dot(parent_turned[:, k * size : (k + 1) * size], received, preferred_element_type=F32)
         for k in range(plan.kinds)
     ]
     parents = plan.fold(plan.select(pieces))
-    weight = jnp.broadcast_to(mendelian[...], (plan.cols, plan.rows)).T
     plain = plan.fold(plan.mine(place, field[...])) - 0.5 * parents
-    mendel = weight * plain
+    mendel = weight[...] * plain
     term[...] = mendel
     back = -0.5 * hot_dot(parent_hot[...], mendel, ((1,), (0,)))
     sums = None
@@ -393,72 +409,71 @@
     return jnp.broadcast_to(side, (plan.cols, LANES)).T[0:1, :]
 
 
-def values_body(plan, group, first, last, place, geno, freq, scale, *refs):
+def values_body(plan, far, place, *refs):
     second = plan.carry > 0
-    pairs, refs = refs[: 2 * len(group)], refs[2 * len(group) :]
+    kept, refs = refs[: 2 * len(plan.sets)], refs[2 * len(plan.sets) :]
+    scale, refs = refs[0], refs[1:]
+    held, refs = refs[: plan.parts], refs[plan.parts :]
     if second:
-        earlier, dots, refs = refs[: 2 * len(group)], refs[2 * len(group)], refs[2 * len(group) + 1 :]
+        earlier, dots, refs = refs[: plan.parts], refs[plan.parts], refs[plan.parts + 1 :]
         alpha = dots[0:1, :] / dots[1:2, :]
         alpha = jnp.broadcast_to(alpha, (LANES, plan.cols)).T[:, :1]
-    if first:
+    if far:
+        before, refs = refs[0], refs[1:]
+        if second:
+            inner_before, refs = refs[0], refs[1:]
         term, keep_p, gather_hot, *refs = refs
-    elif second:
-        before, more_before, *refs = refs
-    else:
-        before, *refs = refs
     *outs, acc = refs
     turned = (((1,), (1,)), ((), ()))
     nb, half = plan.nb, plan.half
 
-    def block_of(near, far, at):
-        held, at = (near, at) if at < half else (far, at - half)
-        tiles = [held[(at * nb + b) * LANES : (at * nb + b + 1) * LANES] for b in range(nb)]
+    def block_of(ref, at):
+        tiles = [ref[(at * nb + b) * LANES : (at * nb + b + 1) * LANES] for b in range(nb)]
         return jnp.concatenate(tiles, axis=1)
 
     spread, inner = None, None
-    for index, part in enumerate(group):
-        near, far = pairs[2 * index : 2 * index + 2]
-        for at, r in enumerate(positions(plan.orders[part])):
-            first_column = r * plan.share(group) + index * plan.width
-            here = slice(first_column, first_column + plan.width)
-            block = block_of(near, far, at)
-            wide = block.astype(F32)
-            off = wide * (2.0 * freq[:, here])
-            if second:
-                old = block_of(*earlier[2 * index : 2 * index + 2], at).astype(F32)
-                product = wide * (old - alpha * wide)
-                inner = product if inner is None else inner + product
-            value = lax.dot_general(geno[:, here], block, turned, preferred_element_type=F32)
-            if spread is None:
-                spread, acc[...] = off, value
-            else:
-                spread = spread + off
-                acc[...] += value
-    shift = lane_total(plan, spread)
-    if first:
-        base, under = home_rows(plan, place, term, keep_p, pairs[1], gather_hot)
-    else:
-        base = before[...]
+    for number, group in enumerate(plan.sets):
+        geno, freq = kept[2 * number : 2 * number + 2]
+        for index, part in enumerate(group):
+            order = positions(plan.orders[part])
+            for at, r in enumerate(order[half:] if far else order[:half]):
+                first_column = r * plan.share(group) + index * plan.width
+                here = slice(first_column, first_column + plan.width)
+                block = block_of(held[part], at)
+                wide = block.astype(F32)
+                off = wide * (2.0 * freq[:, here])
+                if second:
+                    product = wide * (block_of(earlier[part], at).astype(F32) - alpha * wide)
+                    inner = product if inner is None else inner + product
+                value = lax.dot_general(
+                    geno[:, here], block, turned, preferred_element_type=F32
+                )
+                if spread is None:
+                    spread, acc[...] = off, value
+                else:
+                    spread = spread + off
+                    acc[...] += value
+    values = scale[...] * (acc[...] - lane_total(plan, spread))
     if second:
         inner = scale[...] * lane_total(plan, inner)
-        if first:
-            gamma, cross, own_part, pedigree = decode(under, 4)
-            inner = inner + pedigree
-            outs[-1][...] = stack_rows([gamma, cross, own_part, inner])
-        else:
-            inner = inner + more_before[3:4, :]
-    if last:
-        acc[...] = base + scale[...] * (acc[...] - shift)
-        own, other = outs[:2]
-        rows = plan.rows // 2
-        at = (place[1] & 1) * rows
-        own[0:rows] = acc[pl.ds(pl.multiple_of(at, rows), rows), :]
-        other[0:rows] = acc[pl.ds(pl.multiple_of(rows - at, rows), rows), :]
+    if not far:
+        outs[0][...] = values
         if second:
-            own[rows:] = stack_rows([inner])
-            other[rows:] = stack_rows([inner])
-    else:
-        outs[0][...] = base + scale[...] * (acc[...] - shift)
+            outs[1][...] = stack_rows([inner])
+        return
+    home, under = home_rows(plan, place, term, keep_p, held[0], gather_hot)
+    acc[...] = before[...] + values + home
+    own, other = outs[:2]
+    rows = plan.rows // 2
+    at = (place[1] & 1) * rows
+    own[0:rows] = acc[pl.ds(pl.multiple_of(at, rows), rows), :]
+    other[0:rows] = acc[pl.ds(pl.multiple_of(rows - at, rows), rows), :]
+    if second:
+        gamma, cross, own_part, pedigree = decode(under, 4)
+        outs[2][...] = stack_rows([gamma, cross, own_part])
+        inner = inner + inner_before[0:1, :] + pedigree
+        own[rows:] = stack_rows([inner])
+        other[rows:] = stack_rows([inner])
 
 
 def apply_operator(place, field, diagonal, own, other, full):
@@ -469,13 +484,13 @@
     return diagonal[...] * field[...] + full[...]
 
 
-def middle_body(plan, place, field, diagonal, own, other, geno, freq, gather_hot,
+def middle_body(plan, place, field, diagonal, own, other, geno, freq, gather_turned,
                 image, flipped, sums, *rest):
     messages, full = rest[:-1], rest[-1]
     out = apply_operator(place, field, diagonal, own, other, full)
     image[...] = out
     dots = encode(plan, [colsum(field[...] * field[...]), colsum(out * field[...])])
-    emit_rows(plan, place, image[...], gather_hot, messages, dots)
+    emit_rows(plan, place, image[...], gather_turned, messages, dots)
     turned, side = turn_out(image[...], flipped, sums)
     for r in range(plan.owners):
         put_effects(plan, plan.sets[0], r, geno, freq, turned, side, messages)
@@ -507,7 +522,6 @@
     place = jnp.stack([lax.axis_index("animal"), lax.axis_index("snp")]).astype(I32)
     freq = allele_freq.reshape(1, plan.snps)
     scale = (genomic_weight / (plan.snps * blocks)).reshape(1, cols)
-    weight = mendelian.reshape(1, rows)
     square = ((rows, cols), F32)
     lines = ((8, cols), F32)
     wide = plan.owners * plan.slots
@@ -520,26 +534,30 @@
         pltpu.with_memory_space_constraint(x, pltpu.HBM) for x in (genotype, freq)
     )
     copies = [pltpu.SemaphoreType.DMA((plan.owners,))] * 2
-    geno, freq, gather_hot, parent_hot, flipped, sums, *messages = call(
+    geno, freq, gather_turned, flipped, sums, *messages = call(
         lambda *r: begin_body(plan, *r),
         (place, whole, frequency, *[
             pltpu.with_memory_space_constraint(x, pltpu.HBM)
-            for x in (right_side, send_rows[0], sire_slot.reshape(1, rows),
-                      dam_slot.reshape(1, rows))
+            for x in (right_side, send_rows[0])
         ]),
-        (*plan.kept_shapes(groups[0]), ((rows, wide), BF16), ((wide, rows), BF16), *turned,
+        (*plan.kept_shapes(groups[0]), ((wide, rows), BF16), *turned,
          *plan.message_shapes(groups[0])),
-        specs=[HBM] * 6,
+        specs=[HBM] * 4,
         scratch=[
             pltpu.VMEM((rows, cols), F32),
             pltpu.VMEM(send_rows.shape[1:], I32),
-            pltpu.VMEM((1, rows), I32),
-            pltpu.VMEM((1, rows), I32),
             pltpu.VMEM((1, wide), I32),
             *copies,
-            pltpu.SemaphoreType.DMA((4,)),
+            pltpu.SemaphoreType.DMA((2,)),
         ],
         flops=work,
+    )
+    *tables, gather_hot = call(
+        lambda *r: tables_body(plan, *r),
+        (place, sire_slot.reshape(1, rows), dam_slot.reshape(1, rows), mendelian.reshape(1, rows),
+         send_rows[0]),
+        (((wide, rows), BF16), ((rows, wide), BF16), square, ((rows, wide), BF16)),
+        scratch=[pltpu.VMEM((1, wide), I32)],
     )
     kept = [(geno, freq)]
     for group in groups[1:]:
@@ -580,7 +598,7 @@
             others.append(keep)
         sent, keep_p, term, more = call(
             lambda *r: offspring_body(plan, bool(extra), *r),
-            (place, got, keep_e, keep_p, field, parent_hot, weight, *extra),
+            (place, got, keep_e, keep_p, field, *tables, *extra),
             (plan.tile(nb, half), plan.tile(0, half), square, lines if extra else square),
         )
         got = swap(sent, "animal", order[-1])
@@ -604,39 +622,34 @@
                 else:
                     outs = (plan.tile(2 * nb << step),)
                     (x,) = call(join_body, (x, got_e), outs, placed=False)
-        acc = (term, keep_p, gather_hot)
         tail = ((rows // 2 + (8 if op else 0), cols), F32)
-        for index, group in enumerate(groups):
-            first, last = index == 0, index == len(groups) - 1
-            mine = [x for part in group for x in pairs[part]]
+        acc = ()
+        for far in (0, 1):
+            ins = [x for pair in kept for x in pair] + [scale] + [pair[far] for pair in pairs]
+            outs = [tail, tail] if far else [square]
             if op:
-                mine += [*(x for part in group for x in earlier[part]), more]
-            outs = [tail, tail] if last else [square]
-            if op and first:
+                ins += [pair[far] for pair in earlier] + [more]
                 outs.append(lines)
+            if far:
+                ins += [*acc, term, keep_p, gather_hot]
             acc = call(
-                lambda *r, group=group, first=first, last=last: values_body(
-                    plan, group, first, last, *r
-                ),
-                (place, *kept[index], scale, *mine, *acc),
+                lambda *r, far=far: values_body(plan, far, *r),
+                (place, *ins),
                 outs,
                 scratch=full,
-                flops=work * len(group) // parts,
+                flops=work // 2,
             )
-            if op and first:
-                sums = acc[-1]
-                acc = acc if not last else acc[:-1]
-        own, other = acc
+        own, other, *sums = acc
         value = own + swap(other, "snp", 1)
         for bit in bits_of(blocks)[1:]:
             value = value + swap(value, "snp", bit)
-        after = (more, sums) if op else (more, pairs)
+        after = (more, sums[0]) if op else (more, pairs)
         return value, swap(value, "snp", 1), *after
 
     own, other, plain, earlier = round_trip(0, plan, right_side, messages, (), None)
     image, flipped, sums, *messages = call(
         lambda *r: middle_body(summing, *r),
-        (place, right_side, diagonal, own, other, *kept[0], gather_hot),
+        (place, right_side, diagonal, own, other, *kept[0], gather_turned),
         (square, *turned, *summing.message_shapes(groups[0])),
         scratch=full,
         flops=work,

time: 181 us -> 179 us (0.989)
  waiting for transfers between devices: 79.8 us -> 77.7 us
    ppermute x54, waiting for transfers between devices: 79.8 us -> 77.7 us  [swap(): return lax.ppermute(x, axis, [(i, i ^ bit) for i in range(size)])]
    pallas_call x49 -> x50, Pallas kernels: 39.4 us -> 40.5 us  [call(): pl.pallas_call(body, in_specs=[SMEM, *specs] if placed else [VMEM] * len(...]
  transfers between devices with their start and end apart: 54 -> 54, of which waited for: 31 -> 28; matrix products, arithmetic and copies ran while one was open for 0% -> 0% of each run, Pallas kernels for 11% -> 12%
where the time goes in v1:
time: 179 us; the launch traced here: 178 us
  waiting for transfers between devices  77.7 us (43%)
  starting transfers between devices  58.9 us (33%)
  Pallas kernels  40.5 us (23%)
    ppermute x54, waiting for transfers between devices, swap(): return lax.ppermute(x, axis, [(i, i ^ bit) for i in range(size)])  77.7 us
    ppermute x54, starting transfers between devices, swap(): return lax.ppermute(x, axis, [(i, i ^ bit) for i in range(size)])  58.9 us
    pallas_call x50, Pallas kernels, call(): pl.pallas_call(body, in_specs=[SMEM, *specs] if placed else [VMEM] * len(...  40.5 us
  transfers between devices with their start and end apart: 54, of which 28 were waited for; matrix products, arithmetic and copies ran while one was open for 0% of the time, Pallas kernels for 12%

profile of v1, /device:TPU:0, one launch (start us, length us, event | category | flops | bytes accessed | tf_op | source)
XLA Modules:
  0.0 178.4 jit_solution(2015973395403997515)
XLA Ops:
  0.7 7.7 %shard_map.104 = (bf16[1024,4096]{1,0:T(8,128)(2,1)S(1)}, f32[1,4096]{1,0:T(1,128)S(1)}, bf16[512,1024]{1,0:T(8,128)(2,1)S(1)}, bf16[128,1024]{1,0:T(8,128)(2,1)...) custom-call(s32[2]{0:T(128)S(1)} %pad_add_fusion.r_0_.place, ...), custom_call_target="tpu_custom_call" | custom-call | flops 2147483648 | bytes 17336328 | tf_op jit(solution)/shard_map/pallas_call | solution.py:21
  8.4 3.1 %collective-permute-start.6 = (bf16[1024,128]{1,0:T(8,128)(2,1)S(1)}, bf16[1024,128]{1,0:T(8,128)(2,1)S(1)}, u32[]{:S(2)}, u32[]{:S(2)}) collective-permute-start(bf16[1024,128]{1,0:T(8,128)(2,1)S(1)} %get-tuple-element.116), channel_id=1, source_target_pairs={{0,8},{4,12},{8,0},{12,4},{16,24},{20,28},{24,16},{28,20},{1,9},{5... | collective-permute-start | bytes 786440 | tf_op jit(solution)/shard_map/ppermute | solution.py:41
  13.1 4.6 %shard_map.105 = (bf16[1024,4096]{1,0:T(8,128)(2,1)S(1)}, f32[1,4096]{1,0:T(1,128)S(1)}, bf16[1024,128]{1,0:T(8,128)(2,1)S(1)}, bf16[1024,128]{1,0:T(8,128)(2,1)...) custom-call(s32[2]{0:T(128)S(1)} %pad_add_fusion.r_0_.place, bf16[1024,8192]{1,0:T(8,128)(2,1)} %r_1_.4, ...), custom_call_target="tpu_custom_call" | custom-call | flops 2147483648 | bytes 17137672 | tf_op jit(solution)/shard_map/pallas_call | solution.py:21
  18.4 2.0 %collective-permute-done.r_0_ = bf16[1152,128]{1,0:T(8,128)(2,1)S(1)} collective-permute-done((bf16[1152,128]{1,0:T(8,128)(2,1)S(1)}, bf16[1152,128]{1,0:T(8,128)(2,1)S(1)}, u32[]{:S(2)}, u32[]{:S(2)}) %collective-permute-start) | collective-permute-done | bytes 294944 | tf_op jit(solution)/shard_map/ppermute | solution.py:41
  21.1 2.5 %collective-permute-start.7 = (bf16[512,128]{1,0:T(8,128)(2,1)S(1)}, bf16[512,128]{1,0:T(8,128)(2,1)S(1)}, u32[]{:S(2)}, u32[]{:S(2)}) collective-permute-start(bf16[512,128]{1,0:T(8,128)(2,1)S(1)} %get-tuple-element.118), channel_id=1, source_target_pairs={{0,4},{4,0},{8,12},{12,8},{16,20},{20,16},{24,28},{28,24},{1,5},{5... | collective-permute-start | bytes 393224 | tf_op jit(solution)/shard_map/ppermute | solution.py:41
  23.7 3.3 %collective-permute-done.12.got = bf16[1024,128]{1,0:T(8,128)(2,1)S(1)} collective-permute-done((bf16[1024,128]{1,0:T(8,128)(2,1)S(1)}, bf16[1024,128]{1,0:T(8,128)(2,1)S(1)}, u32[]{:S(2)}, u32[]{:S(2)}) %collective-permute-start.12) | collective-permute-done | bytes 262176 | tf_op jit(solution)/shard_map/ppermute | solution.py:41
  27.0 2.6 %collective-permute-start.13 = (bf16[512,128]{1,0:T(8,128)(2,1)S(1)}, bf16[512,128]{1,0:T(8,128)(2,1)S(1)}, u32[]{:S(2)}, u32[]{:S(2)}) collective-permute-start(bf16[512,128]{1,0:T(8,128)(2,1)S(1)} %get-tuple-element.124), channel_id=1, source_target_pairs={{0,16},{4,20},{8,24},{12,28},{16,0},{20,4},{24,8},{28,12},{1,17},{... | collective-permute-start | bytes 393224 | tf_op jit(solution)/shard_map/ppermute | solution.py:41
  29.8 1.6 collective-permute-start.19
  31.4 2.2 %collective-permute-start.2 = (bf16[384,128]{1,0:T(8,128)(2,1)S(1)}, bf16[384,128]{1,0:T(8,128)(2,1)S(1)}, u32[]{:S(2)}, u32[]{:S(2)}) collective-permute-start(bf16[384,128]{1,0:T(8,128)(2,1)S(1)} %get-tuple-element.105), channel_id=1, source_target_pairs={{0,16},{4,20},{8,24},{12,28},{16,0},{20,4},{24,8},{28,12},{1,17},{... | collective-permute-start | bytes 294920 | tf_op jit(solution)/shard_map/ppermute | solution.py:41
  33.7 2.6 %shard_map.108 = (bf16[512,1024]{1,0:T(8,128)(2,1)S(1)}, bf16[1024,512]{1,0:T(8,128)(2,1)S(1)}, f32[1024,128]{1,0:T(8,128)S(1)}, bf16[1024,512]{1,0:T(8,128)(2,1)S(1)}) custom-call(s32[2]{0:T(128)S(1)} %pad_add_fusion.r_0_.place, s32[1,1024]{1,0:T(1,128)S(1)} %bitcast.11, s32[1,1024]{1,0:T(1,128)S(1)} %bitcast.12, f32[1,1024]{1,0:T(1,128)S(1)} %bitcast.13, ...), custom_call_target="tpu_custom_call" | custom-call | bytes 14344 | tf_op jit(solution)/shard_map/pallas_call | solution.py:21
  37.1 2.2 %collective-permute-done.13.got = bf16[512,128]{1,0:T(8,128)(2,1)S(1)} collective-permute-done((bf16[512,128]{1,0:T(8,128)(2,1)S(1)}, bf16[512,128]{1,0:T(8,128)(2,1)S(1)}, u32[]{:S(2)}, u32[]{:S(2)}) %collective-permute-start.13) | collective-permute-done | bytes 131104 | tf_op jit(solution)/shard_map/ppermute | solution.py:41
  39.5 3.0 %collective-permute-start.20 = (bf16[256,128]{1,0:T(8,128)(2,1)S(1)}, bf16[256,128]{1,0:T(8,128)(2,1)S(1)}, u32[]{:S(2)}, u32[]{:S(2)}) collective-permute-start(bf16[256,128]{1,0:T(8,128)(2,1)S(1)} %get-tuple-element.132), channel_id=1, source_target_pairs={{0,16},{4,20},{8,24},{12,28},{16,0},{20,4},{24,8},{28,12},{1,17},{... | collective-permute-start | bytes 196616 | tf_op jit(solution)/shard_map/ppermute | solution.py:41
  43.6 2.3 %shard_map.109 = (bf16[384,128]{1,0:T(8,128)(2,1)S(1)}, bf16[128,128]{1,0:T(8,128)(2,1)S(1)}, f32[1024,128]{1,0:T(8,128)S(1)}, f32[1024,128]{1,0:T(8,128)S(1)}) custom-call(s32[2]{0:T(128)S(1)} %pad_add_fusion.r_0_.place, bf16[384,128]{1,0:T(8,128)(2,1)S(1)} %collective-permute-done.2.r_1_, bf16[256,128]{1,0:T(8,128)(2,1)S(1)} %get-tuple-element.106.r_2_, ...), custom_call_target="tpu_custom_call" | custom-call | bytes 3342344 | tf_op jit(solution)/shard_map/pallas_call | solution.py:21
  46.0 3.0 %collective-permute-start.9 = (bf16[256,128]{1,0:T(8,128)(2,1)S(1)}, bf16[256,128]{1,0:T(8,128)(2,1)S(1)}, u32[]{:S(2)}, u32[]{:S(2)}) collective-permute-start(bf16[256,128]{1,0:T(8,128)(2,1)S(1)} %shard_map.114.sent), channel_id=1, source_target_pairs={{0,16},{4,20},{8,24},{12,28},{16,0},{20,4},{24,8},{28,12},{1,17},{... | collective-permute-start | bytes 196616 | tf_op jit(solution)/shard_map/ppermute | solution.py:41
  49.1 1.5 collective-permute-start.21
  51.9 2.7 %collective-permute-done.9.got = bf16[256,128]{1,0:T(8,128)(2,1)S(1)} collective-permute-done((bf16[256,128]{1,0:T(8,128)(2,1)S(1)}, bf16[256,128]{1,0:T(8,128)(2,1)S(1)}, u32[]{:S(2)}, u32[]{:S(2)}) %collective-permute-start.9) | collective-permute-done | bytes 65568 | tf_op jit(solution)/shard_map/ppermute | solution.py:41
  54.6 2.6 %collective-permute-start.10 = (bf16[512,128]{1,0:T(8,128)(2,1)S(1)}, bf16[512,128]{1,0:T(8,128)(2,1)S(1)}, u32[]{:S(2)}, u32[]{:S(2)}) collective-permute-start(bf16[512,128]{1,0:T(8,128)(2,1)S(1)} %shard_map.115.sent), channel_id=1, source_target_pairs={{0,4},{4,0},{8,12},{12,8},{16,20},{20,16},{24,28},{28,24},{1,5},{5... | collective-permute-start | bytes 393224 | tf_op jit(solution)/shard_map/ppermute | solution.py:41
  58.6 1.9 %collective-permute-done.10.got = bf16[512,128]{1,0:T(8,128)(2,1)S(1)} collective-permute-done((bf16[512,128]{1,0:T(8,128)(2,1)S(1)}, bf16[512,128]{1,0:T(8,128)(2,1)S(1)}, u32[]{:S(2)}, u32[]{:S(2)}) %collective-permute-start.10) | collective-permute-done | bytes 131104 | tf_op jit(solution)/shard_map/ppermute | solution.py:41
  60.7 3.0 %collective-permute-done.16.got = bf16[512,128]{1,0:T(8,128)(2,1)S(1)} collective-permute-done((bf16[512,128]{1,0:T(8,128)(2,1)S(1)}, bf16[512,128]{1,0:T(8,128)(2,1)S(1)}, u32[]{:S(2)}, u32[]{:S(2)}) %collective-permute-start.16) | collective-permute-done | bytes 131104 | tf_op jit(solution)/shard_map/ppermute | solution.py:41
  66.1 3.1 %shard_map.127.r_10_ = f32[1024,128]{1,0:T(8,128)S(1)} custom-call(s32[2]{0:T(128)S(1)} %pad_add_fusion.r_0_.place, bf16[1024,4096]{1,0:T(8,128)(2,1)S(1)} %get-tuple-element.93.r_1_.r_5_, f32[1,4096]{1,0:T(1,128)S(1)} %get-tuple-element.94.r_2_.r_6_, bf16[1024,4096]{1,0:T(8,128)(2,1)S(1)} %get-tuple-element.97.r_3_.r_0_, ...), custom_call_target="tpu_custom_call" | custom-call | flops 1073741824 | bytes 17891848 | tf_op jit(solution)/shard_map/pallas_call | solution.py:21
  71.0 2.5 %collective-permute-done.5.r_6_.r_10_ = bf16[1152,128]{1,0:T(8,128)(2,1)S(1)} collective-permute-done((bf16[1152,128]{1,0:T(8,128)(2,1)S(1)}, bf16[1152,128]{1,0:T(8,128)(2,1)S(1)}, u32[]{:S(2)}, u32[]{:S(2)}) %collective-permute-start.5) | collective-permute-done | bytes 294944 | tf_op jit(solution)/shard_map/ppermute | solution.py:41
  73.5 3.4 %shard_map.128 = (f32[512,128]{1,0:T(8,128)S(1)}, f32[512,128]{1,0:T(8,128)S(1)}) custom-call(s32[2]{0:T(128)S(1)} %pad_add_fusion.r_0_.place, bf16[1024,4096]{1,0:T(8,128)(2,1)S(1)} %get-tuple-element.93.r_1_.r_5_, f32[1,4096]{1,0:T(1,128)S(1)} %get-tuple-element.94.r_2_.r_6_, bf16[1024,4096]{1,0:T(8,128)(2,1)S(1)} %get-tuple-element.97.r_3_.r_0_, ...), custom_call_target="tpu_custom_call" | custom-call | flops 1073741824 | bytes 20021768 | tf_op jit(solution)/shard_map/pallas_call | solution.py:21
  78.5 1.6 collective-permute-start.25
  80.1 6.9 %collective-permute-done.25 = f32[512,128]{1,0:T(8,128)S(1)} collective-permute-done((f32[512,128]{1,0:T(8,128)S(1)}, f32[512,128]{1,0:T(8,128)S(1)}, u32[]{:S(2)}, u32[]{:S(2)}) %collective-permute-start.25) | collective-permute-done | bytes 262176 | tf_op jit(solution)/shard_map/ppermute | solution.py:41
  88.6 2.5 %shard_map.129 = (f32[1024,128]{1,0:T(8,128)S(1)}, bf16[128,1024]{1,0:T(8,128)(2,1)S(1)}, f32[128,128]{1,0:T(8,128)S(1)}, bf16[1216,128]{1,0:T(8,128)(2,1)S(1)},...) custom-call(s32[2]{0:T(128)S(1)} %pad_add_fusion.r_0_.place, ...), custom_call_target="tpu_custom_call" | custom-call | flops 2147483648 | bytes 11026440 | tf_op jit(solution)/shard_map/pallas_call | solution.py:21
  91.1 2.1 %collective-permute-start.27 = (bf16[1216,128]{1,0:T(8,128)(2,1)S(1)}, bf16[1216,128]{1,0:T(8,128)(2,1)S(1)}, u32[]{:S(2)}, u32[]{:S(2)}) collective-permute-start(bf16[1216,128]{1,0:T(8,128)(2,1)S(1)} %get-tuple-element.141), channel_id=1, source_target_pairs={{0,4},{4,0},{8,12},{12,8},{16,20},{20,16},{24,28},{28,24},{1,5},{5... | collective-permute-start | bytes 933896 | tf_op jit(solution)/shard_map/ppermute | solution.py:41
  94.7 2.0 %collective-permute-start.45 = (bf16[1024,128]{1,0:T(8,128)(2,1)S(1)}, bf16[1024,128]{1,0:T(8,128)(2,1)S(1)}, u32[]{:S(2)}, u32[]{:S(2)}) collective-permute-start(bf16[1024,128]{1,0:T(8,128)(2,1)S(1)} %get-tuple-element.170), channel_id=1, source_target_pairs={{0,8},{4,12},{8,0},{12,4},{16,24},{20,28},{24,16},{28,20},{1,9},{5... | collective-permute-start | bytes 786440 | tf_op jit(solution)/shard_map/ppermute | solution.py:41
  96.7 4.7 %collective-permute-done.27.r_0_ = bf16[1216,128]{1,0:T(8,128)(2,1)S(1)} collective-permute-done((bf16[1216,128]{1,0:T(8,128)(2,1)S(1)}, bf16[1216,128]{1,0:T(8,128)(2,1)S(1)}, u32[]{:S(2)}, u32[]{:S(2)}) %collective-permute-start.27) | collective-permute-done | bytes 311328 | tf_op jit(solution)/shard_map/ppermute | solution.py:41
  101.6 9.2 %collective-permute-done.28.r_0_ = bf16[704,128]{1,0:T(8,128)(2,1)S(1)} collective-permute-done((bf16[704,128]{1,0:T(8,128)(2,1)S(1)}, bf16[704,128]{1,0:T(8,128)(2,1)S(1)}, u32[]{:S(2)}, u32[]{:S(2)}) %collective-permute-start.28) | collective-permute-done | bytes 180256 | tf_op jit(solution)/shard_map/ppermute | solution.py:41
  111.4 3.0 %collective-permute-start.40 = (bf16[512,128]{1,0:T(8,128)(2,1)S(1)}, bf16[512,128]{1,0:T(8,128)(2,1)S(1)}, u32[]{:S(2)}, u32[]{:S(2)}) collective-permute-start(bf16[512,128]{1,0:T(8,128)(2,1)S(1)} %get-tuple-element.166), channel_id=1, source_target_pairs={{0,16},{4,20},{8,24},{12,28},{16,0},{20,4},{24,8},{28,12},{1,17},{... | collective-permute-start | bytes 393224 | tf_op jit(solution)/shard_map/ppermute | solution.py:41
  114.5 1.7 collective-permute-start.46
  116.2 4.9 %collective-permute-done.29.r_1_ = bf16[448,128]{1,0:T(8,128)(2,1)S(1)} collective-permute-done((bf16[448,128]{1,0:T(8,128)(2,1)S(1)}, bf16[448,128]{1,0:T(8,128)(2,1)S(1)}, u32[]{:S(2)}, u32[]{:S(2)}) %collective-permute-start.29) | collective-permute-done | bytes 114720 | tf_op jit(solution)/shard_map/ppermute | solution.py:41
  121.2 2.4 %shard_map.132 = (bf16[448,128]{1,0:T(8,128)(2,1)S(1)}, bf16[192,128]{1,0:T(8,128)(2,1)S(1)}, f32[1024,128]{1,0:T(8,128)S(1)}, f32[8,128]{1,0:T(8,128)S(1)}) custom-call(s32[2]{0:T(128)S(1)} %pad_add_fusion.r_0_.place, bf16[448,128]{1,0:T(8,128)(2,1)S(1)} %collective-permute-done.29.r_1_, bf16[256,128]{1,0:T(8,128)(2,1)S(1)} %get-tuple-element.148.r_2_, ...), custom_call_target="tpu_custom_call" | custom-call | bytes 4947976 | tf_op jit(solution)/shard_map/pallas_call | solution.py:21
  123.7 3.0 %collective-permute-start.35 = (bf16[256,128]{1,0:T(8,128)(2,1)S(1)}, bf16[256,128]{1,0:T(8,128)(2,1)S(1)}, u32[]{:S(2)}, u32[]{:S(2)}) collective-permute-start(bf16[256,128]{1,0:T(8,128)(2,1)S(1)} %get-tuple-element.160), channel_id=1, source_target_pairs={{0,16},{4,20},{8,24},{12,28},{16,0},{20,4},{24,8},{28,12},{1,17},{... | collective-permute-start | bytes 196616 | tf_op jit(solution)/shard_map/ppermute | solution.py:41
  126.9 1.9 %collective-permute-start.47 = (bf16[256,128]{1,0:T(8,128)(2,1)S(1)}, bf16[256,128]{1,0:T(8,128)(2,1)S(1)}, u32[]{:S(2)}, u32[]{:S(2)}) collective-permute-start(bf16[256,128]{1,0:T(8,128)(2,1)S(1)} %get-tuple-element.174), channel_id=1, source_target_pairs={{0,16},{4,20},{8,24},{12,28},{16,0},{20,4},{24,8},{28,12},{1,17},{... | collective-permute-start | bytes 196616 | tf_op jit(solution)/shard_map/ppermute | solution.py:41
  128.7 3.2 %collective-permute-done.30.r_1_ = bf16[448,128]{1,0:T(8,128)(2,1)S(1)} collective-permute-done((bf16[448,128]{1,0:T(8,128)(2,1)S(1)}, bf16[448,128]{1,0:T(8,128)(2,1)S(1)}, u32[]{:S(2)}, u32[]{:S(2)}) %collective-permute-start.30) | collective-permute-done | bytes 114720 | tf_op jit(solution)/shard_map/ppermute | solution.py:41
  134.0 2.3 %collective-permute-start.36 = (bf16[256,128]{1,0:T(8,128)(2,1)S(1)}, bf16[256,128]{1,0:T(8,128)(2,1)S(1)}, u32[]{:S(2)}, u32[]{:S(2)}) collective-permute-start(bf16[256,128]{1,0:T(8,128)(2,1)S(1)} %shard_map.137.sent), channel_id=1, source_target_pairs={{0,16},{4,20},{8,24},{12,28},{16,0},{20,4},{24,8},{28,12},{1,17},{... | collective-permute-start | bytes 196616 | tf_op jit(solution)/shard_map/ppermute | solution.py:41
  137.6 2.9 %collective-permute-done.36.got = bf16[256,128]{1,0:T(8,128)(2,1)S(1)} collective-permute-done((bf16[256,128]{1,0:T(8,128)(2,1)S(1)}, bf16[256,128]{1,0:T(8,128)(2,1)S(1)}, u32[]{:S(2)}, u32[]{:S(2)}) %collective-permute-start.36) | collective-permute-done | bytes 65568 | tf_op jit(solution)/shard_map/ppermute | solution.py:41
  144.0 1.6 collective-permute-start.32
  149.4 2.1 %collective-permute-start.44 = (bf16[1024,128]{1,0:T(8,128)(2,1)S(1)}, bf16[1024,128]{1,0:T(8,128)(2,1)S(1)}, u32[]{:S(2)}, u32[]{:S(2)}) collective-permute-start(bf16[1024,128]{1,0:T(8,128)(2,1)S(1)} %shard_map.145.r_8_), channel_id=1, source_target_pairs={{0,4},{4,0},{8,12},{12,8},{16,20},{20,16},{24,28},{28,24},{1,5},{5... | collective-permute-start | bytes 786440 | tf_op jit(solution)/shard_map/ppermute | solution.py:41
  151.6 3.2 %shard_map.151 = (f32[1024,128]{1,0:T(8,128)S(1)}, f32[8,128]{1,0:T(8,128)S(1)}) custom-call(s32[2]{0:T(128)S(1)} %pad_add_fusion.r_0_.place, bf16[1024,4096]{1,0:T(8,128)(2,1)S(1)} %get-tuple-element.93.r_1_.r_5_, f32[1,4096]{1,0:T(1,128)S(1)} %get-tuple-element.94.r_2_.r_6_, bf16[1024,4096]{1,0:T(8,128)(2,1)S(1)} %get-tuple-element.97.r_3_.r_0_, ...), custom_call_target="tpu_custom_call" | custom-call | flops 1073741824 | bytes 18993672 | tf_op jit(solution)/shard_map/pallas_call | solution.py:21
  154.9 5.7 %collective-permute-done.44.r_8_ = bf16[1024,128]{1,0:T(8,128)(2,1)S(1)} collective-permute-done((bf16[1024,128]{1,0:T(8,128)(2,1)S(1)}, bf16[1024,128]{1,0:T(8,128)(2,1)S(1)}, u32[]{:S(2)}, u32[]{:S(2)}) %collective-permute-start.44) | collective-permute-done | bytes 262176 | tf_op jit(solution)/shard_map/ppermute | solution.py:41
  160.6 3.9 %shard_map.152 = (f32[520,128]{1,0:T(8,128)S(1)}, f32[520,128]{1,0:T(8,128)S(1)}, f32[8,128]{1,0:T(8,128)S(1)}) custom-call(s32[2]{0:T(128)S(1)} %pad_add_fusion.r_0_.place, bf16[1024,4096]{1,0:T(8,128)(2,1)S(1)} %get-tuple-element.93.r_1_.r_5_, f32[1,4096]{1,0:T(1,128)S(1)} %get-tuple-element.94.r_2_.r_6_, ...), custom_call_target="tpu_custom_call" | custom-call | flops 1073741824 | bytes 21144072 | tf_op jit(solution)/shard_map/pallas_call | solution.py:21
  164.6 1.5 collective-permute-done.51
  166.2 1.6 collective-permute-start.52
  167.8 6.9 %collective-permute-done.52 = f32[520,128]{1,0:T(8,128)S(1)} collective-permute-done((f32[520,128]{1,0:T(8,128)S(1)}, f32[520,128]{1,0:T(8,128)S(1)}, u32[]{:S(2)}, u32[]{:S(2)}) %collective-permute-start.52) | collective-permute-done | bytes 266272 | tf_op jit(solution)/shard_map/ppermute | solution.py:41
  174.8 1.5 collective-permute-done.53.other
  176.3 2.1 %shard_map.153 = (f32[1024,128]{1,0:T(8,128)}, f32[1024,128]{1,0:T(8,128)}) custom-call(s32[2]{0:T(128)S(1)} %pad_add_fusion.r_0_.place, f32[1024,128]{1,0:T(8,128)S(1)} %get-tuple-element.140.r_4_.field, f32[1024,128]{1,0:T(8,128)S(1)} %copy-done.1, f32[520,128]{1,0:T(8,128)S(1)} %add.15.own, f32[520,128]{1,0:T(8,128)S(1)} %collective-permute-done.53.other, ...), custom_call_target="tpu_custom_call" | custom-call | bytes 2113544 | tf_op jit(solution)/shard_map/pallas_call | solution.py:21
  (130 shorter events, 29.1 us)
Async XLA Ops:
  8.4 12.6 %collective-permute-start.6 = (bf16[1024,128]{1,0:T(8,128)(2,1)S(1)}, bf16[1024,128]{1,0:T(8,128)(2,1)S(1)}, u32[]{:S(2)}, u32[]{:S(2)}) collective-permute-start(bf16[1024,128]{1,0:T(8,128)(2,1)S(1)} %get-tuple-element.116), channel_id=1, source_target_pairs={{0,8},{4,12},{8,0},{12,4},{16,24},{20,28},{24,16},{28,20},{1,9},{5... | collective-permute-start | bytes 786440 | tf_op jit(solution)/shard_map/ppermute | solution.py:41
  11.5 8.9 %collective-permute-start = (bf16[1152,128]{1,0:T(8,128)(2,1)S(1)}, bf16[1152,128]{1,0:T(8,128)(2,1)S(1)}, u32[]{:S(2)}, u32[]{:S(2)}) collective-permute-start(bf16[1152,128]{1,0:T(8,128)(2,1)S(1)} %get-tuple-element.99), channel_id=1, source_target_pairs={{0,4},{4,0},{8,12},{12,8},{16,20},{20,16},{24,28},{28,24},{1,5},{5... | collective-permute-start | bytes 884744 | tf_op jit(solution)/shard_map/ppermute | solution.py:41
  17.7 9.2 %collective-permute-start.12 = (bf16[1024,128]{1,0:T(8,128)(2,1)S(1)}, bf16[1024,128]{1,0:T(8,128)(2,1)S(1)}, u32[]{:S(2)}, u32[]{:S(2)}) collective-permute-start(bf16[1024,128]{1,0:T(8,128)(2,1)S(1)} %get-tuple-element.122), channel_id=1, source_target_pairs={{0,4},{4,0},{8,12},{12,8},{16,20},{20,16},{24,28},{28,24},{1,5},{5... | collective-permute-start | bytes 786440 | tf_op jit(solution)/shard_map/ppermute | solution.py:41
  18.3 11.4 %collective-permute-start.18 = (bf16[1024,128]{1,0:T(8,128)(2,1)S(1)}, bf16[1024,128]{1,0:T(8,128)(2,1)S(1)}, u32[]{:S(2)}, u32[]{:S(2)}) collective-permute-start(bf16[1024,128]{1,0:T(8,128)(2,1)S(1)} %get-tuple-element.128), channel_id=1, source_target_pairs={{0,8},{4,12},{8,0},{12,4},{16,24},{20,28},{24,16},{28,20},{1,9},{5... | collective-permute-start | bytes 786440 | tf_op jit(solution)/shard_map/ppermute | solution.py:41
  20.5 10.9 %collective-permute-start.1 = (bf16[640,128]{1,0:T(8,128)(2,1)S(1)}, bf16[640,128]{1,0:T(8,128)(2,1)S(1)}, u32[]{:S(2)}, u32[]{:S(2)}) collective-permute-start(bf16[640,128]{1,0:T(8,128)(2,1)S(1)} %get-tuple-element.102), channel_id=1, source_target_pairs={{0,8},{4,12},{8,0},{12,4},{16,24},{20,28},{24,16},{28,20},{1,9},{5... | collective-permute-start | bytes 491528 | tf_op jit(solution)/shard_map/ppermute | solution.py:41
  21.1 15.1 %collective-permute-start.7 = (bf16[512,128]{1,0:T(8,128)(2,1)S(1)}, bf16[512,128]{1,0:T(8,128)(2,1)S(1)}, u32[]{:S(2)}, u32[]{:S(2)}) collective-permute-start(bf16[512,128]{1,0:T(8,128)(2,1)S(1)} %get-tuple-element.118), channel_id=1, source_target_pairs={{0,4},{4,0},{8,12},{12,8},{16,20},{20,16},{24,28},{28,24},{1,5},{5... | collective-permute-start | bytes 393224 | tf_op jit(solution)/shard_map/ppermute | solution.py:41
  27.0 12.3 %collective-permute-start.13 = (bf16[512,128]{1,0:T(8,128)(2,1)S(1)}, bf16[512,128]{1,0:T(8,128)(2,1)S(1)}, u32[]{:S(2)}, u32[]{:S(2)}) collective-permute-start(bf16[512,128]{1,0:T(8,128)(2,1)S(1)} %get-tuple-element.124), channel_id=1, source_target_pairs={{0,16},{4,20},{8,24},{12,28},{16,0},{20,4},{24,8},{28,12},{1,17},{... | collective-permute-start | bytes 393224 | tf_op jit(solution)/shard_map/ppermute | solution.py:41
  29.8 9.7 %collective-permute-start.19 = (bf16[512,128]{1,0:T(8,128)(2,1)S(1)}, bf16[512,128]{1,0:T(8,128)(2,1)S(1)}, u32[]{:S(2)}, u32[]{:S(2)}) collective-permute-start(bf16[512,128]{1,0:T(8,128)(2,1)S(1)} %get-tuple-element.130), channel_id=1, source_target_pairs={{0,4},{4,0},{8,12},{12,8},{16,20},{20,16},{24,28},{28,24},{1,5},{5... | collective-permute-start | bytes 393224 | tf_op jit(solution)/shard_map/ppermute | solution.py:41
  31.4 12.1 %collective-permute-start.2 = (bf16[384,128]{1,0:T(8,128)(2,1)S(1)}, bf16[384,128]{1,0:T(8,128)(2,1)S(1)}, u32[]{:S(2)}, u32[]{:S(2)}) collective-permute-start(bf16[384,128]{1,0:T(8,128)(2,1)S(1)} %get-tuple-element.105), channel_id=1, source_target_pairs={{0,16},{4,20},{8,24},{12,28},{16,0},{20,4},{24,8},{28,12},{1,17},{... | collective-permute-start | bytes 294920 | tf_op jit(solution)/shard_map/ppermute | solution.py:41
  36.3 9.7 %collective-permute-start.8 = (bf16[256,128]{1,0:T(8,128)(2,1)S(1)}, bf16[256,128]{1,0:T(8,128)(2,1)S(1)}, u32[]{:S(2)}, u32[]{:S(2)}) collective-permute-start(bf16[256,128]{1,0:T(8,128)(2,1)S(1)} %get-tuple-element.120), channel_id=1, source_target_pairs={{0,16},{4,20},{8,24},{12,28},{16,0},{20,4},{24,8},{28,12},{1,17},{... | collective-permute-start | bytes 196616 | tf_op jit(solution)/shard_map/ppermute | solution.py:41
  39.4 9.6 %collective-permute-start.14 = (bf16[256,128]{1,0:T(8,128)(2,1)S(1)}, bf16[256,128]{1,0:T(8,128)(2,1)S(1)}, u32[]{:S(2)}, u32[]{:S(2)}) collective-permute-start(bf16[256,128]{1,0:T(8,128)(2,1)S(1)} %get-tuple-element.126), channel_id=1, source_target_pairs={{0,8},{4,12},{8,0},{12,4},{16,24},{20,28},{24,16},{28,20},{1,9},{5... | collective-permute-start | bytes 196616 | tf_op jit(solution)/shard_map/ppermute | solution.py:41
  39.5 9.6 %collective-permute-start.20 = (bf16[256,128]{1,0:T(8,128)(2,1)S(1)}, bf16[256,128]{1,0:T(8,128)(2,1)S(1)}, u32[]{:S(2)}, u32[]{:S(2)}) collective-permute-start(bf16[256,128]{1,0:T(8,128)(2,1)S(1)} %get-tuple-element.132), channel_id=1, source_target_pairs={{0,16},{4,20},{8,24},{12,28},{16,0},{20,4},{24,8},{28,12},{1,17},{... | collective-permute-start | bytes 196616 | tf_op jit(solution)/shard_map/ppermute | solution.py:41
  45.9 5.9 %collective-permute-start.3 = (bf16[384,128]{1,0:T(8,128)(2,1)S(1)}, bf16[384,128]{1,0:T(8,128)(2,1)S(1)}, u32[]{:S(2)}, u32[]{:S(2)}) collective-permute-start(bf16[384,128]{1,0:T(8,128)(2,1)S(1)} %get-tuple-element.111.r_0_), channel_id=1, source_target_pairs={{0,16},{4,20},{8,24},{12,28},{16,0},{20,4},{24,8},{28,12},{1,17},{... | collective-permute-start | bytes 294920 | tf_op jit(solution)/shard_map/ppermute | solution.py:41
  46.0 8.6 %collective-permute-start.9 = (bf16[256,128]{1,0:T(8,128)(2,1)S(1)}, bf16[256,128]{1,0:T(8,128)(2,1)S(1)}, u32[]{:S(2)}, u32[]{:S(2)}) collective-permute-start(bf16[256,128]{1,0:T(8,128)(2,1)S(1)} %shard_map.114.sent), channel_id=1, source_target_pairs={{0,16},{4,20},{8,24},{12,28},{16,0},{20,4},{24,8},{28,12},{1,17},{... | collective-permute-start | bytes 196616 | tf_op jit(solution)/shard_map/ppermute | solution.py:41
  49.0 8.2 %collective-permute-start.15 = (bf16[256,128]{1,0:T(8,128)(2,1)S(1)}, bf16[256,128]{1,0:T(8,128)(2,1)S(1)}, u32[]{:S(2)}, u32[]{:S(2)}) collective-permute-start(bf16[256,128]{1,0:T(8,128)(2,1)S(1)} %shard_map.119.sent), channel_id=1, source_target_pairs={{0,8},{4,12},{8,0},{12,4},{16,24},{20,28},{24,16},{28,20},{1,9},{5... | collective-permute-start | bytes 196616 | tf_op jit(solution)/shard_map/ppermute | solution.py:41
  49.1 8.2 %collective-permute-start.21 = (bf16[256,128]{1,0:T(8,128)(2,1)S(1)}, bf16[256,128]{1,0:T(8,128)(2,1)S(1)}, u32[]{:S(2)}, u32[]{:S(2)}) collective-permute-start(bf16[256,128]{1,0:T(8,128)(2,1)S(1)} %shard_map.124.sent), channel_id=1, source_target_pairs={{0,16},{4,20},{8,24},{12,28},{16,0},{20,4},{24,8},{28,12},{1,17},{... | collective-permute-start | bytes 196616 | tf_op jit(solution)/shard_map/ppermute | solution.py:41
  51.9 13.5 %collective-permute-start.4 = (bf16[640,128]{1,0:T(8,128)(2,1)S(1)}, bf16[640,128]{1,0:T(8,128)(2,1)S(1)}, u32[]{:S(2)}, u32[]{:S(2)}) collective-permute-start(bf16[640,128]{1,0:T(8,128)(2,1)S(1)} %get-tuple-element.113.r_0_), channel_id=1, source_target_pairs={{0,8},{4,12},{8,0},{12,4},{16,24},{20,28},{24,16},{28,20},{1,9},{5... | collective-permute-start | bytes 491528 | tf_op jit(solution)/shard_map/ppermute | solution.py:41
  57.2 6.5 %collective-permute-start.16 = (bf16[512,128]{1,0:T(8,128)(2,1)S(1)}, bf16[512,128]{1,0:T(8,128)(2,1)S(1)}, u32[]{:S(2)}, u32[]{:S(2)}) collective-permute-start(bf16[512,128]{1,0:T(8,128)(2,1)S(1)} %shard_map.120.sent), channel_id=1, source_target_pairs={{0,16},{4,20},{8,24},{12,28},{16,0},{20,4},{24,8},{28,12},{1,17},{... | collective-permute-start | bytes 393224 | tf_op jit(solution)/shard_map/ppermute | solution.py:41
  57.3 6.6 %collective-permute-start.22 = (bf16[512,128]{1,0:T(8,128)(2,1)S(1)}, bf16[512,128]{1,0:T(8,128)(2,1)S(1)}, u32[]{:S(2)}, u32[]{:S(2)}) collective-permute-start(bf16[512,128]{1,0:T(8,128)(2,1)S(1)} %shard_map.125.sent), channel_id=1, source_target_pairs={{0,4},{4,0},{8,12},{12,8},{16,20},{20,16},{24,28},{28,24},{1,5},{5... | collective-permute-start | bytes 393224 | tf_op jit(solution)/shard_map/ppermute | solution.py:41
  60.6 8.6 %collective-permute-start.11 = (bf16[1024,128]{1,0:T(8,128)(2,1)S(1)}, bf16[1024,128]{1,0:T(8,128)(2,1)S(1)}, u32[]{:S(2)}, u32[]{:S(2)}) collective-permute-start(bf16[1024,128]{1,0:T(8,128)(2,1)S(1)} %shard_map.116.r_7_.r_11_), channel_id=1, source_target_pairs={{0,8},{4,12},{8,0},{12,4},{16,24},{20,28},{24,16},{28,20},{1,9},{5... | collective-permute-start | bytes 786440 | tf_op jit(solution)/shard_map/ppermute | solution.py:41
  63.7 6.6 %collective-permute-start.17 = (bf16[1024,128]{1,0:T(8,128)(2,1)S(1)}, bf16[1024,128]{1,0:T(8,128)(2,1)S(1)}, u32[]{:S(2)}, u32[]{:S(2)}) collective-permute-start(bf16[1024,128]{1,0:T(8,128)(2,1)S(1)} %shard_map.121.r_8_.r_12_), channel_id=1, source_target_pairs={{0,4},{4,0},{8,12},{12,8},{16,20},{20,16},{24,28},{28,24},{1,5},{5... | collective-permute-start | bytes 786440 | tf_op jit(solution)/shard_map/ppermute | solution.py:41
  63.9 7.0 %collective-permute-start.23 = (bf16[1024,128]{1,0:T(8,128)(2,1)S(1)}, bf16[1024,128]{1,0:T(8,128)(2,1)S(1)}, u32[]{:S(2)}, u32[]{:S(2)}) collective-permute-start(bf16[1024,128]{1,0:T(8,128)(2,1)S(1)} %shard_map.126.r_9_.r_13_), channel_id=1, source_target_pairs={{0,8},{4,12},{8,0},{12,4},{16,24},{20,28},{24,16},{28,20},{1,9},{5... | collective-permute-start | bytes 786440 | tf_op jit(solution)/shard_map/ppermute | solution.py:41
  65.4 8.1 %collective-permute-start.5 = (bf16[1152,128]{1,0:T(8,128)(2,1)S(1)}, bf16[1152,128]{1,0:T(8,128)(2,1)S(1)}, u32[]{:S(2)}, u32[]{:S(2)}) collective-permute-start(bf16[1152,128]{1,0:T(8,128)(2,1)S(1)} %get-tuple-element.115.r_6_.r_10_), channel_id=1, source_target_pairs={{0,4},{4,0},{8,12},{12,8},{16,20},{20,16},{24,28},{28,24},{1,5},{5... | collective-permute-start | bytes 884744 | tf_op jit(solution)/shard_map/ppermute | solution.py:41
  78.5 8.4 %collective-permute-start.25 = (f32[512,128]{1,0:T(8,128)S(1)}, f32[512,128]{1,0:T(8,128)S(1)}, u32[]{:S(2)}, u32[]{:S(2)}) collective-permute-start(f32[512,128]{1,0:T(8,128)S(1)} %add.12), channel_id=1, source_target_pairs={{0,2},{1,3},{2,0},{3,1},{4,6},{5,7},{6,4},{7,5},{8,10},{9,11},{10,... | collective-permute-start | bytes 786440 | tf_op jit(solution)/shard_map/ppermute | solution.py:41
  91.1 10.3 %collective-permute-start.27 = (bf16[1216,128]{1,0:T(8,128)(2,1)S(1)}, bf16[1216,128]{1,0:T(8,128)(2,1)S(1)}, u32[]{:S(2)}, u32[]{:S(2)}) collective-permute-start(bf16[1216,128]{1,0:T(8,128)(2,1)S(1)} %get-tuple-element.141), channel_id=1, source_target_pairs={{0,4},{4,0},{8,12},{12,8},{16,20},{20,16},{24,28},{28,24},{1,5},{5... | collective-permute-start | bytes 933896 | tf_op jit(solution)/shard_map/ppermute | solution.py:41
  93.2 17.7 %collective-permute-start.33 = (bf16[1024,128]{1,0:T(8,128)(2,1)S(1)}, bf16[1024,128]{1,0:T(8,128)(2,1)S(1)}, u32[]{:S(2)}, u32[]{:S(2)}) collective-permute-start(bf16[1024,128]{1,0:T(8,128)(2,1)S(1)} %get-tuple-element.156), channel_id=1, source_target_pairs={{0,8},{4,12},{8,0},{12,4},{16,24},{20,28},{24,16},{28,20},{1,9},{5... | collective-permute-start | bytes 786440 | tf_op jit(solution)/shard_map/ppermute | solution.py:41
  94.6 16.8 %collective-permute-start.39 = (bf16[1024,128]{1,0:T(8,128)(2,1)S(1)}, bf16[1024,128]{1,0:T(8,128)(2,1)S(1)}, u32[]{:S(2)}, u32[]{:S(2)}) collective-permute-start(bf16[1024,128]{1,0:T(8,128)(2,1)S(1)} %get-tuple-element.164), channel_id=1, source_target_pairs={{0,4},{4,0},{8,12},{12,8},{16,20},{20,16},{24,28},{28,24},{1,5},{5... | collective-permute-start | bytes 786440 | tf_op jit(solution)/shard_map/ppermute | solution.py:41
  94.7 19.7 %collective-permute-start.45 = (bf16[1024,128]{1,0:T(8,128)(2,1)S(1)}, bf16[1024,128]{1,0:T(8,128)(2,1)S(1)}, u32[]{:S(2)}, u32[]{:S(2)}) collective-permute-start(bf16[1024,128]{1,0:T(8,128)(2,1)S(1)} %get-tuple-element.170), channel_id=1, source_target_pairs={{0,8},{4,12},{8,0},{12,4},{16,24},{20,28},{24,16},{28,20},{1,9},{5... | collective-permute-start | bytes 786440 | tf_op jit(solution)/shard_map/ppermute | solution.py:41
  101.5 9.3 %collective-permute-start.28 = (bf16[704,128]{1,0:T(8,128)(2,1)S(1)}, bf16[704,128]{1,0:T(8,128)(2,1)S(1)}, u32[]{:S(2)}, u32[]{:S(2)}) collective-permute-start(bf16[704,128]{1,0:T(8,128)(2,1)S(1)} %get-tuple-element.144), channel_id=1, source_target_pairs={{0,8},{4,12},{8,0},{12,4},{16,24},{20,28},{24,16},{28,20},{1,9},{5... | collective-permute-start | bytes 540680 | tf_op jit(solution)/shard_map/ppermute | solution.py:41
  110.8 10.4 %collective-permute-start.29 = (bf16[448,128]{1,0:T(8,128)(2,1)S(1)}, bf16[448,128]{1,0:T(8,128)(2,1)S(1)}, u32[]{:S(2)}, u32[]{:S(2)}) collective-permute-start(bf16[448,128]{1,0:T(8,128)(2,1)S(1)} %get-tuple-element.147), channel_id=1, source_target_pairs={{0,16},{4,20},{8,24},{12,28},{16,0},{20,4},{24,8},{28,12},{1,17},{... | collective-permute-start | bytes 344072 | tf_op jit(solution)/shard_map/ppermute | solution.py:41
  111.0 12.7 %collective-permute-start.34 = (bf16[512,128]{1,0:T(8,128)(2,1)S(1)}, bf16[512,128]{1,0:T(8,128)(2,1)S(1)}, u32[]{:S(2)}, u32[]{:S(2)}) collective-permute-start(bf16[512,128]{1,0:T(8,128)(2,1)S(1)} %get-tuple-element.158), channel_id=1, source_target_pairs={{0,4},{4,0},{8,12},{12,8},{16,20},{20,16},{24,28},{28,24},{1,5},{5... | collective-permute-start | bytes 393224 | tf_op jit(solution)/shard_map/ppermute | solution.py:41
  111.4 15.2 %collective-permute-start.40 = (bf16[512,128]{1,0:T(8,128)(2,1)S(1)}, bf16[512,128]{1,0:T(8,128)(2,1)S(1)}, u32[]{:S(2)}, u32[]{:S(2)}) collective-permute-start(bf16[512,128]{1,0:T(8,128)(2,1)S(1)} %get-tuple-element.166), channel_id=1, source_target_pairs={{0,16},{4,20},{8,24},{12,28},{16,0},{20,4},{24,8},{28,12},{1,17},{... | collective-permute-start | bytes 393224 | tf_op jit(solution)/shard_map/ppermute | solution.py:41
  114.5 12.3 %collective-permute-start.46 = (bf16[512,128]{1,0:T(8,128)(2,1)S(1)}, bf16[512,128]{1,0:T(8,128)(2,1)S(1)}, u32[]{:S(2)}, u32[]{:S(2)}) collective-permute-start(bf16[512,128]{1,0:T(8,128)(2,1)S(1)} %get-tuple-element.172), channel_id=1, source_target_pairs={{0,4},{4,0},{8,12},{12,8},{16,20},{20,16},{24,28},{28,24},{1,5},{5... | collective-permute-start | bytes 393224 | tf_op jit(solution)/shard_map/ppermute | solution.py:41
  123.6 8.4 %collective-permute-start.30 = (bf16[448,128]{1,0:T(8,128)(2,1)S(1)}, bf16[448,128]{1,0:T(8,128)(2,1)S(1)}, u32[]{:S(2)}, u32[]{:S(2)}) collective-permute-start(bf16[448,128]{1,0:T(8,128)(2,1)S(1)} %get-tuple-element.151.r_0_), channel_id=1, source_target_pairs={{0,16},{4,20},{8,24},{12,28},{16,0},{20,4},{24,8},{28,12},{1,17},{... | collective-permute-start | bytes 344072 | tf_op jit(solution)/shard_map/ppermute | solution.py:41
  123.7 10.2 %collective-permute-start.35 = (bf16[256,128]{1,0:T(8,128)(2,1)S(1)}, bf16[256,128]{1,0:T(8,128)(2,1)S(1)}, u32[]{:S(2)}, u32[]{:S(2)}) collective-permute-start(bf16[256,128]{1,0:T(8,128)(2,1)S(1)} %get-tuple-element.160), channel_id=1, source_target_pairs={{0,16},{4,20},{8,24},{12,28},{16,0},{20,4},{24,8},{28,12},{1,17},{... | collective-permute-start | bytes 196616 | tf_op jit(solution)/shard_map/ppermute | solution.py:41
  126.7 9.6 %collective-permute-start.41 = (bf16[256,128]{1,0:T(8,128)(2,1)S(1)}, bf16[256,128]{1,0:T(8,128)(2,1)S(1)}, u32[]{:S(2)}, u32[]{:S(2)}) collective-permute-start(bf16[256,128]{1,0:T(8,128)(2,1)S(1)} %get-tuple-element.168), channel_id=1, source_target_pairs={{0,8},{4,12},{8,0},{12,4},{16,24},{20,28},{24,16},{28,20},{1,9},{5... | collective-permute-start | bytes 196616 | tf_op jit(solution)/shard_map/ppermute | solution.py:41
  126.9 10.6 %collective-permute-start.47 = (bf16[256,128]{1,0:T(8,128)(2,1)S(1)}, bf16[256,128]{1,0:T(8,128)(2,1)S(1)}, u32[]{:S(2)}, u32[]{:S(2)}) collective-permute-start(bf16[256,128]{1,0:T(8,128)(2,1)S(1)} %get-tuple-element.174), channel_id=1, source_target_pairs={{0,16},{4,20},{8,24},{12,28},{16,0},{20,4},{24,8},{28,12},{1,17},{... | collective-permute-start | bytes 196616 | tf_op jit(solution)/shard_map/ppermute | solution.py:41
  132.0 11.9 %collective-permute-start.31 = (bf16[704,128]{1,0:T(8,128)(2,1)S(1)}, bf16[704,128]{1,0:T(8,128)(2,1)S(1)}, u32[]{:S(2)}, u32[]{:S(2)}) collective-permute-start(bf16[704,128]{1,0:T(8,128)(2,1)S(1)} %get-tuple-element.153.r_0_), channel_id=1, source_target_pairs={{0,8},{4,12},{8,0},{12,4},{16,24},{20,28},{24,16},{28,20},{1,9},{5... | collective-permute-start | bytes 540680 | tf_op jit(solution)/shard_map/ppermute | solution.py:41
  134.0 6.5 %collective-permute-start.36 = (bf16[256,128]{1,0:T(8,128)(2,1)S(1)}, bf16[256,128]{1,0:T(8,128)(2,1)S(1)}, u32[]{:S(2)}, u32[]{:S(2)}) collective-permute-start(bf16[256,128]{1,0:T(8,128)(2,1)S(1)} %shard_map.137.sent), channel_id=1, source_target_pairs={{0,16},{4,20},{8,24},{12,28},{16,0},{20,4},{24,8},{28,12},{1,17},{... | collective-permute-start | bytes 196616 | tf_op jit(solution)/shard_map/ppermute | solution.py:41
  137.5 5.9 %collective-permute-start.48 = (bf16[256,128]{1,0:T(8,128)(2,1)S(1)}, bf16[256,128]{1,0:T(8,128)(2,1)S(1)}, u32[]{:S(2)}, u32[]{:S(2)}) collective-permute-start(bf16[256,128]{1,0:T(8,128)(2,1)S(1)} %shard_map.148.sent), channel_id=1, source_target_pairs={{0,16},{4,20},{8,24},{12,28},{16,0},{20,4},{24,8},{28,12},{1,17},{... | collective-permute-start | bytes 196616 | tf_op jit(solution)/shard_map/ppermute | solution.py:41
  140.5 6.3 %collective-permute-start.37 = (bf16[512,128]{1,0:T(8,128)(2,1)S(1)}, bf16[512,128]{1,0:T(8,128)(2,1)S(1)}, u32[]{:S(2)}, u32[]{:S(2)}) collective-permute-start(bf16[512,128]{1,0:T(8,128)(2,1)S(1)} %shard_map.138.sent), channel_id=1, source_target_pairs={{0,4},{4,0},{8,12},{12,8},{16,20},{20,16},{24,28},{28,24},{1,5},{5... | collective-permute-start | bytes 393224 | tf_op jit(solution)/shard_map/ppermute | solution.py:41
  142.0 7.4 %collective-permute-start.43 = (bf16[512,128]{1,0:T(8,128)(2,1)S(1)}, bf16[512,128]{1,0:T(8,128)(2,1)S(1)}, u32[]{:S(2)}, u32[]{:S(2)}) collective-permute-start(bf16[512,128]{1,0:T(8,128)(2,1)S(1)} %shard_map.144.sent), channel_id=1, source_target_pairs={{0,16},{4,20},{8,24},{12,28},{16,0},{20,4},{24,8},{28,12},{1,17},{... | collective-permute-start | bytes 393224 | tf_op jit(solution)/shard_map/ppermute | solution.py:41
  143.4 8.1 %collective-permute-start.49 = (bf16[512,128]{1,0:T(8,128)(2,1)S(1)}, bf16[512,128]{1,0:T(8,128)(2,1)S(1)}, u32[]{:S(2)}, u32[]{:S(2)}) collective-permute-start(bf16[512,128]{1,0:T(8,128)(2,1)S(1)} %shard_map.149.sent), channel_id=1, source_target_pairs={{0,4},{4,0},{8,12},{12,8},{16,20},{20,16},{24,28},{28,24},{1,5},{5... | collective-permute-start | bytes 393224 | tf_op jit(solution)/shard_map/ppermute | solution.py:41
  144.0 16.6 %collective-permute-start.32 = (bf16[1216,128]{1,0:T(8,128)(2,1)S(1)}, bf16[1216,128]{1,0:T(8,128)(2,1)S(1)}, u32[]{:S(2)}, u32[]{:S(2)}) collective-permute-start(bf16[1216,128]{1,0:T(8,128)(2,1)S(1)} %get-tuple-element.155.r_6_), channel_id=1, source_target_pairs={{0,4},{4,0},{8,12},{12,8},{16,20},{20,16},{24,28},{28,24},{1,5},{5... | collective-permute-start | bytes 933896 | tf_op jit(solution)/shard_map/ppermute | solution.py:41
  146.8 8.1 %collective-permute-start.38 = (bf16[1024,128]{1,0:T(8,128)(2,1)S(1)}, bf16[1024,128]{1,0:T(8,128)(2,1)S(1)}, u32[]{:S(2)}, u32[]{:S(2)}) collective-permute-start(bf16[1024,128]{1,0:T(8,128)(2,1)S(1)} %shard_map.139.r_7_), channel_id=1, source_target_pairs={{0,8},{4,12},{8,0},{12,4},{16,24},{20,28},{24,16},{28,20},{1,9},{5... | collective-permute-start | bytes 786440 | tf_op jit(solution)/shard_map/ppermute | solution.py:41
  149.4 11.2 %collective-permute-start.44 = (bf16[1024,128]{1,0:T(8,128)(2,1)S(1)}, bf16[1024,128]{1,0:T(8,128)(2,1)S(1)}, u32[]{:S(2)}, u32[]{:S(2)}) collective-permute-start(bf16[1024,128]{1,0:T(8,128)(2,1)S(1)} %shard_map.145.r_8_), channel_id=1, source_target_pairs={{0,4},{4,0},{8,12},{12,8},{16,20},{20,16},{24,28},{28,24},{1,5},{5... | collective-permute-start | bytes 786440 | tf_op jit(solution)/shard_map/ppermute | solution.py:41
  151.6 9.0 %collective-permute-start.50 = (bf16[1024,128]{1,0:T(8,128)(2,1)S(1)}, bf16[1024,128]{1,0:T(8,128)(2,1)S(1)}, u32[]{:S(2)}, u32[]{:S(2)}) collective-permute-start(bf16[1024,128]{1,0:T(8,128)(2,1)S(1)} %shard_map.150.r_9_), channel_id=1, source_target_pairs={{0,8},{4,12},{8,0},{12,4},{16,24},{20,28},{24,16},{28,20},{1,9},{5... | collective-permute-start | bytes 786440 | tf_op jit(solution)/shard_map/ppermute | solution.py:41
  166.2 8.5 %collective-permute-start.52 = (f32[520,128]{1,0:T(8,128)S(1)}, f32[520,128]{1,0:T(8,128)S(1)}, u32[]{:S(2)}, u32[]{:S(2)}) collective-permute-start(f32[520,128]{1,0:T(8,128)S(1)} %add.14), channel_id=1, source_target_pairs={{0,2},{1,3},{2,0},{3,1},{4,6},{5,7},{6,4},{7,5},{8,10},{9,11},{10,... | collective-permute-start | bytes 798728 | tf_op jit(solution)/shard_map/ppermute | solution.py:41
  (13 other events, 194.3 us)

commit v2 on v1

--- a/solution.py
+++ b/solution.py
@@ -409,19 +409,26 @@
     return jnp.broadcast_to(side, (plan.cols, LANES)).T[0:1, :]
 
 
-def values_body(plan, far, place, *refs):
-    second = plan.carry > 0
-    kept, refs = refs[: 2 * len(plan.sets)], refs[2 * len(plan.sets) :]
+def stage_sets(plan, stage):
+    return plan.sets if stage == 0 else [plan.sets[stage - 1]]
+
+
+def values_body(plan, stage, place, *refs):
+    second, far, final = plan.carry > 0, stage > 0, stage == len(plan.sets)
+    sets = stage_sets(plan, stage)
+    parts = [part for group in sets for part in group]
+    kept, refs = refs[: 2 * len(sets)], refs[2 * len(sets) :]
     scale, refs = refs[0], refs[1:]
-    held, refs = refs[: plan.parts], refs[plan.parts :]
+    held, refs = dict(zip(parts, refs)), refs[len(parts) :]
     if second:
-        earlier, dots, refs = refs[: plan.parts], refs[plan.parts], refs[plan.parts + 1 :]
+        earlier, dots, refs = dict(zip(parts, refs)), refs[len(parts)], refs[len(parts) + 1 :]
         alpha = dots[0:1, :] / dots[1:2, :]
         alpha = jnp.broadcast_to(alpha, (LANES, plan.cols)).T[:, :1]
     if far:
         before, refs = refs[0], refs[1:]
         if second:
-            inner_before, refs = refs[0], refs[1:]
+            lines_before, refs = refs[0], refs[1:]
+    if stage == 1:
         term, keep_p, gather_hot, *refs = refs
     *outs, acc = refs
     turned = (((1,), (1,)), ((), ()))
@@ -432,7 +439,7 @@
         return jnp.concatenate(tiles, axis=1)
 
     spread, inner = None, None
-    for number, group in enumerate(plan.sets):
+    for number, group in enumerate(sets):
         geno, freq = kept[2 * number : 2 * number + 2]
         for index, part in enumerate(group):
             order = positions(plan.orders[part])
@@ -456,22 +463,31 @@
     values = scale[...] * (acc[...] - lane_total(plan, spread))
     if second:
         inner = scale[...] * lane_total(plan, inner)
-    if not far:
+    if far:
+        values = before[...] + values
+    carried = []
+    if stage == 1:
+        home, under = home_rows(plan, place, term, keep_p, held[0], gather_hot)
+        values = values + home
+        if second:
+            gamma, cross, own_part, pedigree = decode(under, 4)
+            inner = inner + lines_before[0:1, :] + pedigree
+            carried = [gamma, cross, own_part]
+    elif far and second:
+        inner = inner + lines_before[0:1, :]
+        carried = [lines_before[i : i + 1, :] for i in (1, 2, 3)]
+    if second:
+        outs[-1][...] = stack_rows([inner, *carried])
+    if not final:
         outs[0][...] = values
-        if second:
-            outs[1][...] = stack_rows([inner])
         return
-    home, under = home_rows(plan, place, term, keep_p, held[0], gather_hot)
-    acc[...] = before[...] + values + home
+    acc[...] = values
     own, other = outs[:2]
     rows = plan.rows // 2
     at = (place[1] & 1) * rows
     own[0:rows] = acc[pl.ds(pl.multiple_of(at, rows), rows), :]
     other[0:rows] = acc[pl.ds(pl.multiple_of(rows - at, rows), rows), :]
     if second:
-        gamma, cross, own_part, pedigree = decode(under, 4)
-        outs[2][...] = stack_rows([gamma, cross, own_part])
-        inner = inner + inner_before[0:1, :] + pedigree
         own[rows:] = stack_rows([inner])
         other[rows:] = stack_rows([inner])
 
@@ -500,9 +516,9 @@
                solution, residual, full):
     q = apply_operator(place, field, diagonal, own, other, full)
     alpha0 = dots[0:1, :] / dots[1:2, :]
-    gamma = more[0:1, :]
+    gamma = more[1:2, :]
     rows = field.shape[0] // 2
-    delta = more[1:2, :] - alpha0 * (more[2:3, :] + own[rows : rows + 1, :])
+    delta = more[2:3, :] - alpha0 * (more[3:4, :] + own[rows : rows + 1, :])
     beta = gamma / dots[0:1, :]
     alpha = gamma / (delta - beta * gamma / alpha0)
     left = right[...] - alpha0 * field[...]
@@ -624,20 +640,25 @@
                     (x,) = call(join_body, (x, got_e), outs, placed=False)
         tail = ((rows // 2 + (8 if op else 0), cols), F32)
         acc = ()
-        for far in (0, 1):
-            ins = [x for pair in kept for x in pair] + [scale] + [pair[far] for pair in pairs]
-            outs = [tail, tail] if far else [square]
+        for stage in range(len(groups) + 1):
+            used = [part for group in stage_sets(plan, stage) for part in group]
+            stores = kept if stage == 0 else [kept[stage - 1]]
+            far = min(stage, 1)
+            ins = [x for pair in stores for x in pair] + [scale]
+            ins += [pairs[part][far] for part in used]
+            outs = [tail, tail] if stage == len(groups) else [square]
             if op:
-                ins += [pair[far] for pair in earlier] + [more]
+                ins += [earlier[part][far] for part in used] + [more]
                 outs.append(lines)
-            if far:
-                ins += [*acc, term, keep_p, gather_hot]
+            ins += acc
+            if stage == 1:
+                ins += [term, keep_p, gather_hot]
             acc = call(
-                lambda *r, far=far: values_body(plan, far, *r),
+                lambda *r, stage=stage: values_body(plan, stage, *r),
                 (place, *ins),
                 outs,
                 scratch=full,
-                flops=work // 2,
+                flops=work * len(used) // (2 * parts),
             )
         own, other, *sums = acc
         value = own + swap(other, "snp", 1)

time: 179 us -> 179 us (level)
  waiting for transfers between devices: 77.7 us -> 69.9 us
  starting transfers between devices: 58.9 us -> 65.8 us
    ppermute x54, waiting for transfers between devices: 77.7 us -> 69.9 us  [swap(): return lax.ppermute(x, axis, [(i, i ^ bit) for i in range(size)])]
    ppermute x54, starting transfers between devices: 58.9 us -> 65.8 us  [swap(): return lax.ppermute(x, axis, [(i, i ^ bit) for i in range(size)])]
    pallas_call x50 -> x52, Pallas kernels: 40.5 us -> 41.6 us  [call(): pl.pallas_call(body, in_specs=[SMEM, *specs] if placed else [VMEM] * len(...]
  transfers between devices with their start and end apart: 54 -> 54, of which waited for: 28 -> 27; matrix products, arithmetic and copies ran while one was open for 0% -> 0% of each run, Pallas kernels for 12% -> 14%
where the time goes in v2:
time: 179 us
  waiting for transfers between devices  69.9 us (39%)
  starting transfers between devices  65.8 us (37%)
  Pallas kernels  41.6 us (23%)
    ppermute x54, waiting for transfers between devices, swap(): return lax.ppermute(x, axis, [(i, i ^ bit) for i in range(size)])  69.9 us
    ppermute x54, starting transfers between devices, swap(): return lax.ppermute(x, axis, [(i, i ^ bit) for i in range(size)])  65.8 us
    pallas_call x52, Pallas kernels, call(): pl.pallas_call(body, in_specs=[SMEM, *specs] if placed else [VMEM] * len(...  41.6 us
  transfers between devices with their start and end apart: 54, of which 27 were waited for; matrix products, arithmetic and copies ran while one was open for 0% of the time, Pallas kernels for 14%

profile of v2, /device:TPU:0, one launch (start us, length us, event | category | flops | bytes accessed | tf_op | source)
XLA Modules:
  0.0 178.8 jit_solution(16145271397821579015)
XLA Ops:
  0.7 7.7 %shard_map.104 = (bf16[1024,4096]{1,0:T(8,128)(2,1)S(1)}, f32[1,4096]{1,0:T(1,128)S(1)}, bf16[512,1024]{1,0:T(8,128)(2,1)S(1)}, bf16[128,1024]{1,0:T(8,128)(2,1)...) custom-call(s32[2]{0:T(128)S(1)} %pad_add_fusion.r_0_.place, ...), custom_call_target="tpu_custom_call" | custom-call | flops 2147483648 | bytes 17336328 | tf_op jit(solution)/shard_map/pallas_call | solution.py:21
  8.4 3.1 %collective-permute-start.18 = (bf16[1024,128]{1,0:T(8,128)(2,1)S(1)}, bf16[1024,128]{1,0:T(8,128)(2,1)S(1)}, u32[]{:S(2)}, u32[]{:S(2)}) collective-permute-start(bf16[1024,128]{1,0:T(8,128)(2,1)S(1)} %get-tuple-element.130), channel_id=1, source_target_pairs={{0,8},{4,12},{8,0},{12,4},{16,24},{20,28},{24,16},{28,20},{1,9},{5... | collective-permute-start | bytes 786440 | tf_op jit(solution)/shard_map/ppermute | solution.py:41
  13.0 4.6 %shard_map.105 = (bf16[1024,4096]{1,0:T(8,128)(2,1)S(1)}, f32[1,4096]{1,0:T(1,128)S(1)}, bf16[1024,128]{1,0:T(8,128)(2,1)S(1)}, bf16[1024,128]{1,0:T(8,128)(2,1)...) custom-call(s32[2]{0:T(128)S(1)} %pad_add_fusion.r_0_.place, bf16[1024,8192]{1,0:T(8,128)(2,1)} %r_1_.4, ...), custom_call_target="tpu_custom_call" | custom-call | flops 2147483648 | bytes 17137672 | tf_op jit(solution)/shard_map/pallas_call | solution.py:21
  18.3 2.1 %collective-permute-done.12.r_0_ = bf16[1152,128]{1,0:T(8,128)(2,1)S(1)} collective-permute-done((bf16[1152,128]{1,0:T(8,128)(2,1)S(1)}, bf16[1152,128]{1,0:T(8,128)(2,1)S(1)}, u32[]{:S(2)}, u32[]{:S(2)}) %collective-permute-start.12) | collective-permute-done | bytes 294944 | tf_op jit(solution)/shard_map/ppermute | solution.py:41
  21.1 2.5 %collective-permute-start.19 = (bf16[512,128]{1,0:T(8,128)(2,1)S(1)}, bf16[512,128]{1,0:T(8,128)(2,1)S(1)}, u32[]{:S(2)}, u32[]{:S(2)}) collective-permute-start(bf16[512,128]{1,0:T(8,128)(2,1)S(1)} %get-tuple-element.132), channel_id=1, source_target_pairs={{0,4},{4,0},{8,12},{12,8},{16,20},{20,16},{24,28},{28,24},{1,5},{5... | collective-permute-start | bytes 393224 | tf_op jit(solution)/shard_map/ppermute | solution.py:41
  23.7 3.3 %collective-permute-done.got = bf16[1024,128]{1,0:T(8,128)(2,1)S(1)} collective-permute-done((bf16[1024,128]{1,0:T(8,128)(2,1)S(1)}, bf16[1024,128]{1,0:T(8,128)(2,1)S(1)}, u32[]{:S(2)}, u32[]{:S(2)}) %collective-permute-start) | collective-permute-done | bytes 262176 | tf_op jit(solution)/shard_map/ppermute | solution.py:41
  27.0 2.6 %collective-permute-start.1 = (bf16[512,128]{1,0:T(8,128)(2,1)S(1)}, bf16[512,128]{1,0:T(8,128)(2,1)S(1)}, u32[]{:S(2)}, u32[]{:S(2)}) collective-permute-start(bf16[512,128]{1,0:T(8,128)(2,1)S(1)} %get-tuple-element.101), channel_id=1, source_target_pairs={{0,16},{4,20},{8,24},{12,28},{16,0},{20,4},{24,8},{28,12},{1,17},{... | collective-permute-start | bytes 393224 | tf_op jit(solution)/shard_map/ppermute | solution.py:41
  29.7 1.7 collective-permute-start.7
  31.4 2.2 %collective-permute-start.14 = (bf16[384,128]{1,0:T(8,128)(2,1)S(1)}, bf16[384,128]{1,0:T(8,128)(2,1)S(1)}, u32[]{:S(2)}, u32[]{:S(2)}) collective-permute-start(bf16[384,128]{1,0:T(8,128)(2,1)S(1)} %get-tuple-element.119), channel_id=1, source_target_pairs={{0,16},{4,20},{8,24},{12,28},{16,0},{20,4},{24,8},{28,12},{1,17},{... | collective-permute-start | bytes 294920 | tf_op jit(solution)/shard_map/ppermute | solution.py:41
  33.6 2.6 %shard_map.118 = (bf16[512,1024]{1,0:T(8,128)(2,1)S(1)}, bf16[1024,512]{1,0:T(8,128)(2,1)S(1)}, f32[1024,128]{1,0:T(8,128)S(1)}, bf16[1024,512]{1,0:T(8,128)(2,1)S(1)}) custom-call(s32[2]{0:T(128)S(1)} %pad_add_fusion.r_0_.place, s32[1,1024]{1,0:T(1,128)S(1)} %bitcast.11, s32[1,1024]{1,0:T(1,128)S(1)} %bitcast.12, f32[1,1024]{1,0:T(1,128)S(1)} %bitcast.13, ...), custom_call_target="tpu_custom_call" | custom-call | bytes 14344 | tf_op jit(solution)/shard_map/pallas_call | solution.py:21
  37.1 2.2 %collective-permute-done.1.got = bf16[512,128]{1,0:T(8,128)(2,1)S(1)} collective-permute-done((bf16[512,128]{1,0:T(8,128)(2,1)S(1)}, bf16[512,128]{1,0:T(8,128)(2,1)S(1)}, u32[]{:S(2)}, u32[]{:S(2)}) %collective-permute-start.1) | collective-permute-done | bytes 131104 | tf_op jit(solution)/shard_map/ppermute | solution.py:41
  39.5 3.0 %collective-permute-start.8 = (bf16[256,128]{1,0:T(8,128)(2,1)S(1)}, bf16[256,128]{1,0:T(8,128)(2,1)S(1)}, u32[]{:S(2)}, u32[]{:S(2)}) collective-permute-start(bf16[256,128]{1,0:T(8,128)(2,1)S(1)} %get-tuple-element.109), channel_id=1, source_target_pairs={{0,16},{4,20},{8,24},{12,28},{16,0},{20,4},{24,8},{28,12},{1,17},{... | collective-permute-start | bytes 196616 | tf_op jit(solution)/shard_map/ppermute | solution.py:41
  43.4 2.3 %shard_map.119 = (bf16[384,128]{1,0:T(8,128)(2,1)S(1)}, bf16[128,128]{1,0:T(8,128)(2,1)S(1)}, f32[1024,128]{1,0:T(8,128)S(1)}, f32[1024,128]{1,0:T(8,128)S(1)}) custom-call(s32[2]{0:T(128)S(1)} %pad_add_fusion.r_0_.place, bf16[384,128]{1,0:T(8,128)(2,1)S(1)} %collective-permute-done.14.r_1_, bf16[256,128]{1,0:T(8,128)(2,1)S(1)} %get-tuple-element.120.r_2_, ...), custom_call_target="tpu_custom_call" | custom-call | bytes 3342344 | tf_op jit(solution)/shard_map/pallas_call | solution.py:21
  45.8 3.0 %collective-permute-start.21 = (bf16[256,128]{1,0:T(8,128)(2,1)S(1)}, bf16[256,128]{1,0:T(8,128)(2,1)S(1)}, u32[]{:S(2)}, u32[]{:S(2)}) collective-permute-start(bf16[256,128]{1,0:T(8,128)(2,1)S(1)} %shard_map.124.sent), channel_id=1, source_target_pairs={{0,16},{4,20},{8,24},{12,28},{16,0},{20,4},{24,8},{28,12},{1,17},{... | collective-permute-start | bytes 196616 | tf_op jit(solution)/shard_map/ppermute | solution.py:41
  48.9 1.7 collective-permute-start.9
  51.8 2.7 %collective-permute-done.21.got = bf16[256,128]{1,0:T(8,128)(2,1)S(1)} collective-permute-done((bf16[256,128]{1,0:T(8,128)(2,1)S(1)}, bf16[256,128]{1,0:T(8,128)(2,1)S(1)}, u32[]{:S(2)}, u32[]{:S(2)}) %collective-permute-start.21) | collective-permute-done | bytes 65568 | tf_op jit(solution)/shard_map/ppermute | solution.py:41
  54.6 2.6 %collective-permute-start.22 = (bf16[512,128]{1,0:T(8,128)(2,1)S(1)}, bf16[512,128]{1,0:T(8,128)(2,1)S(1)}, u32[]{:S(2)}, u32[]{:S(2)}) collective-permute-start(bf16[512,128]{1,0:T(8,128)(2,1)S(1)} %shard_map.125.sent), channel_id=1, source_target_pairs={{0,4},{4,0},{8,12},{12,8},{16,20},{20,16},{24,28},{28,24},{1,5},{5... | collective-permute-start | bytes 393224 | tf_op jit(solution)/shard_map/ppermute | solution.py:41
  57.3 1.8 collective-permute-start.10
  60.4 3.9 %collective-permute-done.4.got = bf16[512,128]{1,0:T(8,128)(2,1)S(1)} collective-permute-done((bf16[512,128]{1,0:T(8,128)(2,1)S(1)}, bf16[512,128]{1,0:T(8,128)(2,1)S(1)}, u32[]{:S(2)}, u32[]{:S(2)}) %collective-permute-start.4) | collective-permute-done | bytes 131104 | tf_op jit(solution)/shard_map/ppermute | solution.py:41
  64.6 2.1 %collective-permute-start.11 = (bf16[1024,128]{1,0:T(8,128)(2,1)S(1)}, bf16[1024,128]{1,0:T(8,128)(2,1)S(1)}, u32[]{:S(2)}, u32[]{:S(2)}) collective-permute-start(bf16[1024,128]{1,0:T(8,128)(2,1)S(1)} %shard_map.115.r_9_.r_13_), channel_id=1, source_target_pairs={{0,8},{4,12},{8,0},{12,4},{16,24},{20,28},{24,16},{28,20},{1,9},{5... | collective-permute-start | bytes 786440 | tf_op jit(solution)/shard_map/ppermute | solution.py:41
  66.9 3.1 %shard_map.127.r_6_ = f32[1024,128]{1,0:T(8,128)S(1)} custom-call(s32[2]{0:T(128)S(1)} %pad_add_fusion.r_0_.place, bf16[1024,4096]{1,0:T(8,128)(2,1)S(1)} %get-tuple-element.111.r_1_.r_5_, f32[1,4096]{1,0:T(1,128)S(1)} %get-tuple-element.112.r_2_.r_6_, bf16[1024,4096]{1,0:T(8,128)(2,1)S(1)} %get-tuple-element.97.r_3_.r_1_.r_0_, ...), custom_call_target="tpu_custom_call" | custom-call | flops 1073741824 | bytes 17891848 | tf_op jit(solution)/shard_map/pallas_call | solution.py:21
  70.0 3.9 %collective-permute-done.17.r_4_.r_6_ = bf16[1152,128]{1,0:T(8,128)(2,1)S(1)} collective-permute-done((bf16[1152,128]{1,0:T(8,128)(2,1)S(1)}, bf16[1152,128]{1,0:T(8,128)(2,1)S(1)}, u32[]{:S(2)}, u32[]{:S(2)}) %collective-permute-start.17) | collective-permute-done | bytes 294944 | tf_op jit(solution)/shard_map/ppermute | solution.py:41
  73.9 2.2 %shard_map.128.r_6_ = f32[1024,128]{1,0:T(8,128)S(1)} custom-call(s32[2]{0:T(128)S(1)} %pad_add_fusion.r_0_.place, bf16[1024,4096]{1,0:T(8,128)(2,1)S(1)} %get-tuple-element.111.r_1_.r_5_, f32[1,4096]{1,0:T(1,128)S(1)} %get-tuple-element.112.r_2_.r_6_, f32[1,128]{1,0:T(1,128)S(1)} %multiply_bitcast_fusion.r_5_.r_3_, ...), custom_call_target="tpu_custom_call" | custom-call | flops 536870912 | bytes 11092488 | tf_op jit(solution)/shard_map/pallas_call | solution.py:21
  76.2 1.9 %shard_map.129 = (f32[512,128]{1,0:T(8,128)S(1)}, f32[512,128]{1,0:T(8,128)S(1)}) custom-call(s32[2]{0:T(128)S(1)} %pad_add_fusion.r_0_.place, bf16[1024,4096]{1,0:T(8,128)(2,1)S(1)} %get-tuple-element.97.r_3_.r_1_.r_0_, f32[1,4096]{1,0:T(1,128)S(1)} %get-tuple-element.98.r_4_.r_2_.r_1_, f32[1,128]{1,0:T(1,128)S(1)} %multiply_bitcast_fusion.r_5_.r_3_, ...), custom_call_target="tpu_custom_call" | custom-call | flops 536870912 | bytes 9454088 | tf_op jit(solution)/shard_map/pallas_call | solution.py:21
  79.8 1.6 collective-permute-start.25
  81.4 6.8 %collective-permute-done.25 = f32[512,128]{1,0:T(8,128)S(1)} collective-permute-done((f32[512,128]{1,0:T(8,128)S(1)}, f32[512,128]{1,0:T(8,128)S(1)}, u32[]{:S(2)}, u32[]{:S(2)}) %collective-permute-start.25) | collective-permute-done | bytes 262176 | tf_op jit(solution)/shard_map/ppermute | solution.py:41
  89.8 2.5 %shard_map.130 = (f32[1024,128]{1,0:T(8,128)S(1)}, bf16[128,1024]{1,0:T(8,128)(2,1)S(1)}, f32[128,128]{1,0:T(8,128)S(1)}, bf16[1216,128]{1,0:T(8,128)(2,1)S(1)},...) custom-call(s32[2]{0:T(128)S(1)} %pad_add_fusion.r_0_.place, ...), custom_call_target="tpu_custom_call" | custom-call | flops 2147483648 | bytes 11026440 | tf_op jit(solution)/shard_map/pallas_call | solution.py:21
  93.9 7.9 %collective-permute-done.39.r_0_ = bf16[1216,128]{1,0:T(8,128)(2,1)S(1)} collective-permute-done((bf16[1216,128]{1,0:T(8,128)(2,1)S(1)}, bf16[1216,128]{1,0:T(8,128)(2,1)S(1)}, u32[]{:S(2)}, u32[]{:S(2)}) %collective-permute-start.39) | collective-permute-done | bytes 311328 | tf_op jit(solution)/shard_map/ppermute | solution.py:41
  104.9 2.0 %collective-permute-start.33 = (bf16[1024,128]{1,0:T(8,128)(2,1)S(1)}, bf16[1024,128]{1,0:T(8,128)(2,1)S(1)}, u32[]{:S(2)}, u32[]{:S(2)}) collective-permute-start(bf16[1024,128]{1,0:T(8,128)(2,1)S(1)} %get-tuple-element.151), channel_id=1, source_target_pairs={{0,8},{4,12},{8,0},{12,4},{16,24},{20,28},{24,16},{28,20},{1,9},{5... | collective-permute-start | bytes 786440 | tf_op jit(solution)/shard_map/ppermute | solution.py:41
  106.9 1.9 %collective-permute-done.40.r_0_ = bf16[704,128]{1,0:T(8,128)(2,1)S(1)} collective-permute-done((bf16[704,128]{1,0:T(8,128)(2,1)S(1)}, bf16[704,128]{1,0:T(8,128)(2,1)S(1)}, u32[]{:S(2)}, u32[]{:S(2)}) %collective-permute-start.40) | collective-permute-done | bytes 180256 | tf_op jit(solution)/shard_map/ppermute | solution.py:41
  109.6 2.0 %collective-permute-start.46 = (bf16[512,128]{1,0:T(8,128)(2,1)S(1)}, bf16[512,128]{1,0:T(8,128)(2,1)S(1)}, u32[]{:S(2)}, u32[]{:S(2)}) collective-permute-start(bf16[512,128]{1,0:T(8,128)(2,1)S(1)} %get-tuple-element.175), channel_id=1, source_target_pairs={{0,4},{4,0},{8,12},{12,8},{16,20},{20,16},{24,28},{28,24},{1,5},{5... | collective-permute-start | bytes 393224 | tf_op jit(solution)/shard_map/ppermute | solution.py:41
  111.6 3.6 %collective-permute-done.41.r_1_ = bf16[448,128]{1,0:T(8,128)(2,1)S(1)} collective-permute-done((bf16[448,128]{1,0:T(8,128)(2,1)S(1)}, bf16[448,128]{1,0:T(8,128)(2,1)S(1)}, u32[]{:S(2)}, u32[]{:S(2)}) %collective-permute-start.41) | collective-permute-done | bytes 114720 | tf_op jit(solution)/shard_map/ppermute | solution.py:41
  115.2 2.4 %shard_map.144 = (bf16[448,128]{1,0:T(8,128)(2,1)S(1)}, bf16[192,128]{1,0:T(8,128)(2,1)S(1)}, f32[1024,128]{1,0:T(8,128)S(1)}, f32[8,128]{1,0:T(8,128)S(1)}) custom-call(s32[2]{0:T(128)S(1)} %pad_add_fusion.r_0_.place, bf16[448,128]{1,0:T(8,128)(2,1)S(1)} %collective-permute-done.41.r_1_, bf16[256,128]{1,0:T(8,128)(2,1)S(1)} %get-tuple-element.164.r_2_, ...), custom_call_target="tpu_custom_call" | custom-call | bytes 4947976 | tf_op jit(solution)/shard_map/pallas_call | solution.py:21
  117.7 2.1 %collective-permute-start.42 = (bf16[448,128]{1,0:T(8,128)(2,1)S(1)}, bf16[448,128]{1,0:T(8,128)(2,1)S(1)}, u32[]{:S(2)}, u32[]{:S(2)}) collective-permute-start(bf16[448,128]{1,0:T(8,128)(2,1)S(1)} %get-tuple-element.168.r_0_), channel_id=1, source_target_pairs={{0,16},{4,20},{8,24},{12,28},{16,0},{20,4},{24,8},{28,12},{1,17},{... | collective-permute-start | bytes 344072 | tf_op jit(solution)/shard_map/ppermute | solution.py:41
  120.9 3.3 %collective-permute-start.34 = (bf16[512,128]{1,0:T(8,128)(2,1)S(1)}, bf16[512,128]{1,0:T(8,128)(2,1)S(1)}, u32[]{:S(2)}, u32[]{:S(2)}) collective-permute-start(bf16[512,128]{1,0:T(8,128)(2,1)S(1)} %get-tuple-element.153), channel_id=1, source_target_pairs={{0,4},{4,0},{8,12},{12,8},{16,20},{20,16},{24,28},{28,24},{1,5},{5... | collective-permute-start | bytes 393224 | tf_op jit(solution)/shard_map/ppermute | solution.py:41
  124.3 4.9 %collective-permute-done.42.r_1_ = bf16[448,128]{1,0:T(8,128)(2,1)S(1)} collective-permute-done((bf16[448,128]{1,0:T(8,128)(2,1)S(1)}, bf16[448,128]{1,0:T(8,128)(2,1)S(1)}, u32[]{:S(2)}, u32[]{:S(2)}) %collective-permute-start.42) | collective-permute-done | bytes 114720 | tf_op jit(solution)/shard_map/ppermute | solution.py:41
  129.3 2.3 %collective-permute-done.28.got = bf16[512,128]{1,0:T(8,128)(2,1)S(1)} collective-permute-done((bf16[512,128]{1,0:T(8,128)(2,1)S(1)}, bf16[512,128]{1,0:T(8,128)(2,1)S(1)}, u32[]{:S(2)}, u32[]{:S(2)}) %collective-permute-start.28) | collective-permute-done | bytes 131104 | tf_op jit(solution)/shard_map/ppermute | solution.py:41
  131.8 2.1 %collective-permute-start.35 = (bf16[256,128]{1,0:T(8,128)(2,1)S(1)}, bf16[256,128]{1,0:T(8,128)(2,1)S(1)}, u32[]{:S(2)}, u32[]{:S(2)}) collective-permute-start(bf16[256,128]{1,0:T(8,128)(2,1)S(1)} %get-tuple-element.155), channel_id=1, source_target_pairs={{0,16},{4,20},{8,24},{12,28},{16,0},{20,4},{24,8},{28,12},{1,17},{... | collective-permute-start | bytes 196616 | tf_op jit(solution)/shard_map/ppermute | solution.py:41
  134.9 4.2 %collective-permute-done.29.got = bf16[256,128]{1,0:T(8,128)(2,1)S(1)} collective-permute-done((bf16[256,128]{1,0:T(8,128)(2,1)S(1)}, bf16[256,128]{1,0:T(8,128)(2,1)S(1)}, u32[]{:S(2)}, u32[]{:S(2)}) %collective-permute-start.29) | collective-permute-done | bytes 65568 | tf_op jit(solution)/shard_map/ppermute | solution.py:41
  139.2 2.1 %collective-permute-start.36 = (bf16[256,128]{1,0:T(8,128)(2,1)S(1)}, bf16[256,128]{1,0:T(8,128)(2,1)S(1)}, u32[]{:S(2)}, u32[]{:S(2)}) collective-permute-start(bf16[256,128]{1,0:T(8,128)(2,1)S(1)} %shard_map.139.sent), channel_id=1, source_target_pairs={{0,16},{4,20},{8,24},{12,28},{16,0},{20,4},{24,8},{28,12},{1,17},{... | collective-permute-start | bytes 196616 | tf_op jit(solution)/shard_map/ppermute | solution.py:41
  141.4 2.3 %collective-permute-start.49 = (bf16[512,128]{1,0:T(8,128)(2,1)S(1)}, bf16[512,128]{1,0:T(8,128)(2,1)S(1)}, u32[]{:S(2)}, u32[]{:S(2)}) collective-permute-start(bf16[512,128]{1,0:T(8,128)(2,1)S(1)} %shard_map.150.sent), channel_id=1, source_target_pairs={{0,4},{4,0},{8,12},{12,8},{16,20},{20,16},{24,28},{28,24},{1,5},{5... | collective-permute-start | bytes 393224 | tf_op jit(solution)/shard_map/ppermute | solution.py:41
  144.5 4.6 %collective-permute-start.37 = (bf16[512,128]{1,0:T(8,128)(2,1)S(1)}, bf16[512,128]{1,0:T(8,128)(2,1)S(1)}, u32[]{:S(2)}, u32[]{:S(2)}) collective-permute-start(bf16[512,128]{1,0:T(8,128)(2,1)S(1)} %shard_map.140.sent), channel_id=1, source_target_pairs={{0,4},{4,0},{8,12},{12,8},{16,20},{20,16},{24,28},{28,24},{1,5},{5... | collective-permute-start | bytes 393224 | tf_op jit(solution)/shard_map/ppermute | solution.py:41
  153.8 3.4 %shard_map.152 = (f32[1024,128]{1,0:T(8,128)S(1)}, f32[8,128]{1,0:T(8,128)S(1)}) custom-call(s32[2]{0:T(128)S(1)} %pad_add_fusion.r_0_.place, bf16[1024,4096]{1,0:T(8,128)(2,1)S(1)} %get-tuple-element.111.r_1_.r_5_, f32[1,4096]{1,0:T(1,128)S(1)} %get-tuple-element.112.r_2_.r_6_, bf16[1024,4096]{1,0:T(8,128)(2,1)S(1)} %get-tuple-element.97.r_3_.r_1_.r_0_, ...), custom_call_target="tpu_custom_call" | custom-call | flops 1073741824 | bytes 18993672 | tf_op jit(solution)/shard_map/pallas_call | solution.py:21
  158.3 2.3 %shard_map.153 = (f32[1024,128]{1,0:T(8,128)S(1)}, f32[8,128]{1,0:T(8,128)S(1)}) custom-call(s32[2]{0:T(128)S(1)} %pad_add_fusion.r_0_.place, bf16[1024,4096]{1,0:T(8,128)(2,1)S(1)} %get-tuple-element.111.r_1_.r_5_, f32[1,4096]{1,0:T(1,128)S(1)} %get-tuple-element.112.r_2_.r_6_, f32[1,128]{1,0:T(1,128)S(1)} %multiply_bitcast_fusion.r_5_.r_3_, ...), custom_call_target="tpu_custom_call" | custom-call | flops 536870912 | bytes 11690504 | tf_op jit(solution)/shard_map/pallas_call | solution.py:21
  161.2 2.0 %shard_map.154 = (f32[520,128]{1,0:T(8,128)S(1)}, f32[520,128]{1,0:T(8,128)S(1)}, f32[8,128]{1,0:T(8,128)S(1)}) custom-call(s32[2]{0:T(128)S(1)} %pad_add_fusion.r_0_.place, bf16[1024,4096]{1,0:T(8,128)(2,1)S(1)} %get-tuple-element.97.r_3_.r_1_.r_0_, f32[1,4096]{1,0:T(1,128)S(1)} %get-tuple-element.98.r_4_.r_2_.r_1_, ...), custom_call_target="tpu_custom_call" | custom-call | flops 536870912 | bytes 9986568 | tf_op jit(solution)/shard_map/pallas_call | solution.py:21
  164.8 3.5 %collective-permute-start.52 = (f32[520,128]{1,0:T(8,128)S(1)}, f32[520,128]{1,0:T(8,128)S(1)}, u32[]{:S(2)}, u32[]{:S(2)}) collective-permute-start(f32[520,128]{1,0:T(8,128)S(1)} %add.14), channel_id=1, source_target_pairs={{0,2},{1,3},{2,0},{3,1},{4,6},{5,7},{6,4},{7,5},{8,10},{9,11},{10,... | collective-permute-start | bytes 798728 | tf_op jit(solution)/shard_map/ppermute | solution.py:41
  168.3 6.7 %collective-permute-done.52 = f32[520,128]{1,0:T(8,128)S(1)} collective-permute-done((f32[520,128]{1,0:T(8,128)S(1)}, f32[520,128]{1,0:T(8,128)S(1)}, u32[]{:S(2)}, u32[]{:S(2)}) %collective-permute-start.52) | collective-permute-done | bytes 266272 | tf_op jit(solution)/shard_map/ppermute | solution.py:41
  176.6 2.1 %shard_map.155 = (f32[1024,128]{1,0:T(8,128)}, f32[1024,128]{1,0:T(8,128)}) custom-call(s32[2]{0:T(128)S(1)} %pad_add_fusion.r_0_.place, f32[1024,128]{1,0:T(8,128)S(1)} %get-tuple-element.142.r_4_.field, f32[1024,128]{1,0:T(8,128)S(1)} %copy-done.1, f32[520,128]{1,0:T(8,128)S(1)} %add.15.own, f32[520,128]{1,0:T(8,128)S(1)} %collective-permute-done.53.other, ...), custom_call_target="tpu_custom_call" | custom-call | bytes 2113544 | tf_op jit(solution)/shard_map/pallas_call | solution.py:21
  (132 shorter events, 30.0 us)
Async XLA Ops:
  8.4 12.6 %collective-permute-start.18 = (bf16[1024,128]{1,0:T(8,128)(2,1)S(1)}, bf16[1024,128]{1,0:T(8,128)(2,1)S(1)}, u32[]{:S(2)}, u32[]{:S(2)}) collective-permute-start(bf16[1024,128]{1,0:T(8,128)(2,1)S(1)} %get-tuple-element.130), channel_id=1, source_target_pairs={{0,8},{4,12},{8,0},{12,4},{16,24},{20,28},{24,16},{28,20},{1,9},{5... | collective-permute-start | bytes 786440 | tf_op jit(solution)/shard_map/ppermute | solution.py:41
  11.5 8.9 %collective-permute-start.12 = (bf16[1152,128]{1,0:T(8,128)(2,1)S(1)}, bf16[1152,128]{1,0:T(8,128)(2,1)S(1)}, u32[]{:S(2)}, u32[]{:S(2)}) collective-permute-start(bf16[1152,128]{1,0:T(8,128)(2,1)S(1)} %get-tuple-element.113), channel_id=1, source_target_pairs={{0,4},{4,0},{8,12},{12,8},{16,20},{20,16},{24,28},{28,24},{1,5},{5... | collective-permute-start | bytes 884744 | tf_op jit(solution)/shard_map/ppermute | solution.py:41
  17.7 9.2 %collective-permute-start = (bf16[1024,128]{1,0:T(8,128)(2,1)S(1)}, bf16[1024,128]{1,0:T(8,128)(2,1)S(1)}, u32[]{:S(2)}, u32[]{:S(2)}) collective-permute-start(bf16[1024,128]{1,0:T(8,128)(2,1)S(1)} %get-tuple-element.99), channel_id=1, source_target_pairs={{0,4},{4,0},{8,12},{12,8},{16,20},{20,16},{24,28},{28,24},{1,5},{5... | collective-permute-start | bytes 786440 | tf_op jit(solution)/shard_map/ppermute | solution.py:41
  18.3 11.4 %collective-permute-start.6 = (bf16[1024,128]{1,0:T(8,128)(2,1)S(1)}, bf16[1024,128]{1,0:T(8,128)(2,1)S(1)}, u32[]{:S(2)}, u32[]{:S(2)}) collective-permute-start(bf16[1024,128]{1,0:T(8,128)(2,1)S(1)} %get-tuple-element.105), channel_id=1, source_target_pairs={{0,8},{4,12},{8,0},{12,4},{16,24},{20,28},{24,16},{28,20},{1,9},{5... | collective-permute-start | bytes 786440 | tf_op jit(solution)/shard_map/ppermute | solution.py:41
  20.4 10.9 %collective-permute-start.13 = (bf16[640,128]{1,0:T(8,128)(2,1)S(1)}, bf16[640,128]{1,0:T(8,128)(2,1)S(1)}, u32[]{:S(2)}, u32[]{:S(2)}) collective-permute-start(bf16[640,128]{1,0:T(8,128)(2,1)S(1)} %get-tuple-element.116), channel_id=1, source_target_pairs={{0,8},{4,12},{8,0},{12,4},{16,24},{20,28},{24,16},{28,20},{1,9},{5... | collective-permute-start | bytes 491528 | tf_op jit(solution)/shard_map/ppermute | solution.py:41
  21.1 15.1 %collective-permute-start.19 = (bf16[512,128]{1,0:T(8,128)(2,1)S(1)}, bf16[512,128]{1,0:T(8,128)(2,1)S(1)}, u32[]{:S(2)}, u32[]{:S(2)}) collective-permute-start(bf16[512,128]{1,0:T(8,128)(2,1)S(1)} %get-tuple-element.132), channel_id=1, source_target_pairs={{0,4},{4,0},{8,12},{12,8},{16,20},{20,16},{24,28},{28,24},{1,5},{5... | collective-permute-start | bytes 393224 | tf_op jit(solution)/shard_map/ppermute | solution.py:41
  27.0 12.3 %collective-permute-start.1 = (bf16[512,128]{1,0:T(8,128)(2,1)S(1)}, bf16[512,128]{1,0:T(8,128)(2,1)S(1)}, u32[]{:S(2)}, u32[]{:S(2)}) collective-permute-start(bf16[512,128]{1,0:T(8,128)(2,1)S(1)} %get-tuple-element.101), channel_id=1, source_target_pairs={{0,16},{4,20},{8,24},{12,28},{16,0},{20,4},{24,8},{28,12},{1,17},{... | collective-permute-start | bytes 393224 | tf_op jit(solution)/shard_map/ppermute | solution.py:41
  29.7 9.7 %collective-permute-start.7 = (bf16[512,128]{1,0:T(8,128)(2,1)S(1)}, bf16[512,128]{1,0:T(8,128)(2,1)S(1)}, u32[]{:S(2)}, u32[]{:S(2)}) collective-permute-start(bf16[512,128]{1,0:T(8,128)(2,1)S(1)} %get-tuple-element.107), channel_id=1, source_target_pairs={{0,4},{4,0},{8,12},{12,8},{16,20},{20,16},{24,28},{28,24},{1,5},{5... | collective-permute-start | bytes 393224 | tf_op jit(solution)/shard_map/ppermute | solution.py:41
  31.4 12.0 %collective-permute-start.14 = (bf16[384,128]{1,0:T(8,128)(2,1)S(1)}, bf16[384,128]{1,0:T(8,128)(2,1)S(1)}, u32[]{:S(2)}, u32[]{:S(2)}) collective-permute-start(bf16[384,128]{1,0:T(8,128)(2,1)S(1)} %get-tuple-element.119), channel_id=1, source_target_pairs={{0,16},{4,20},{8,24},{12,28},{16,0},{20,4},{24,8},{28,12},{1,17},{... | collective-permute-start | bytes 294920 | tf_op jit(solution)/shard_map/ppermute | solution.py:41
  36.2 9.6 %collective-permute-start.20 = (bf16[256,128]{1,0:T(8,128)(2,1)S(1)}, bf16[256,128]{1,0:T(8,128)(2,1)S(1)}, u32[]{:S(2)}, u32[]{:S(2)}) collective-permute-start(bf16[256,128]{1,0:T(8,128)(2,1)S(1)} %get-tuple-element.134), channel_id=1, source_target_pairs={{0,16},{4,20},{8,24},{12,28},{16,0},{20,4},{24,8},{28,12},{1,17},{... | collective-permute-start | bytes 196616 | tf_op jit(solution)/shard_map/ppermute | solution.py:41
  39.3 9.5 %collective-permute-start.2 = (bf16[256,128]{1,0:T(8,128)(2,1)S(1)}, bf16[256,128]{1,0:T(8,128)(2,1)S(1)}, u32[]{:S(2)}, u32[]{:S(2)}) collective-permute-start(bf16[256,128]{1,0:T(8,128)(2,1)S(1)} %get-tuple-element.103), channel_id=1, source_target_pairs={{0,8},{4,12},{8,0},{12,4},{16,24},{20,28},{24,16},{28,20},{1,9},{5... | collective-permute-start | bytes 196616 | tf_op jit(solution)/shard_map/ppermute | solution.py:41
  39.5 9.4 %collective-permute-start.8 = (bf16[256,128]{1,0:T(8,128)(2,1)S(1)}, bf16[256,128]{1,0:T(8,128)(2,1)S(1)}, u32[]{:S(2)}, u32[]{:S(2)}) collective-permute-start(bf16[256,128]{1,0:T(8,128)(2,1)S(1)} %get-tuple-element.109), channel_id=1, source_target_pairs={{0,16},{4,20},{8,24},{12,28},{16,0},{20,4},{24,8},{28,12},{1,17},{... | collective-permute-start | bytes 196616 | tf_op jit(solution)/shard_map/ppermute | solution.py:41
  45.7 6.0 %collective-permute-start.15 = (bf16[384,128]{1,0:T(8,128)(2,1)S(1)}, bf16[384,128]{1,0:T(8,128)(2,1)S(1)}, u32[]{:S(2)}, u32[]{:S(2)}) collective-permute-start(bf16[384,128]{1,0:T(8,128)(2,1)S(1)} %get-tuple-element.125.r_0_), channel_id=1, source_target_pairs={{0,16},{4,20},{8,24},{12,28},{16,0},{20,4},{24,8},{28,12},{1,17},{... | collective-permute-start | bytes 294920 | tf_op jit(solution)/shard_map/ppermute | solution.py:41
  45.8 8.8 %collective-permute-start.21 = (bf16[256,128]{1,0:T(8,128)(2,1)S(1)}, bf16[256,128]{1,0:T(8,128)(2,1)S(1)}, u32[]{:S(2)}, u32[]{:S(2)}) collective-permute-start(bf16[256,128]{1,0:T(8,128)(2,1)S(1)} %shard_map.124.sent), channel_id=1, source_target_pairs={{0,16},{4,20},{8,24},{12,28},{16,0},{20,4},{24,8},{28,12},{1,17},{... | collective-permute-start | bytes 196616 | tf_op jit(solution)/shard_map/ppermute | solution.py:41
  48.8 8.3 %collective-permute-start.3 = (bf16[256,128]{1,0:T(8,128)(2,1)S(1)}, bf16[256,128]{1,0:T(8,128)(2,1)S(1)}, u32[]{:S(2)}, u32[]{:S(2)}) collective-permute-start(bf16[256,128]{1,0:T(8,128)(2,1)S(1)} %shard_map.108.sent), channel_id=1, source_target_pairs={{0,8},{4,12},{8,0},{12,4},{16,24},{20,28},{24,16},{28,20},{1,9},{5... | collective-permute-start | bytes 196616 | tf_op jit(solution)/shard_map/ppermute | solution.py:41
  48.9 8.3 %collective-permute-start.9 = (bf16[256,128]{1,0:T(8,128)(2,1)S(1)}, bf16[256,128]{1,0:T(8,128)(2,1)S(1)}, u32[]{:S(2)}, u32[]{:S(2)}) collective-permute-start(bf16[256,128]{1,0:T(8,128)(2,1)S(1)} %shard_map.113.sent), channel_id=1, source_target_pairs={{0,16},{4,20},{8,24},{12,28},{16,0},{20,4},{24,8},{28,12},{1,17},{... | collective-permute-start | bytes 196616 | tf_op jit(solution)/shard_map/ppermute | solution.py:41
  51.8 15.0 %collective-permute-start.16 = (bf16[640,128]{1,0:T(8,128)(2,1)S(1)}, bf16[640,128]{1,0:T(8,128)(2,1)S(1)}, u32[]{:S(2)}, u32[]{:S(2)}) collective-permute-start(bf16[640,128]{1,0:T(8,128)(2,1)S(1)} %get-tuple-element.127.r_0_), channel_id=1, source_target_pairs={{0,8},{4,12},{8,0},{12,4},{16,24},{20,28},{24,16},{28,20},{1,9},{5... | collective-permute-start | bytes 491528 | tf_op jit(solution)/shard_map/ppermute | solution.py:41
  54.6 5.7 %collective-permute-start.22 = (bf16[512,128]{1,0:T(8,128)(2,1)S(1)}, bf16[512,128]{1,0:T(8,128)(2,1)S(1)}, u32[]{:S(2)}, u32[]{:S(2)}) collective-permute-start(bf16[512,128]{1,0:T(8,128)(2,1)S(1)} %shard_map.125.sent), channel_id=1, source_target_pairs={{0,4},{4,0},{8,12},{12,8},{16,20},{20,16},{24,28},{28,24},{1,5},{5... | collective-permute-start | bytes 393224 | tf_op jit(solution)/shard_map/ppermute | solution.py:41
  57.2 7.1 %collective-permute-start.4 = (bf16[512,128]{1,0:T(8,128)(2,1)S(1)}, bf16[512,128]{1,0:T(8,128)(2,1)S(1)}, u32[]{:S(2)}, u32[]{:S(2)}) collective-permute-start(bf16[512,128]{1,0:T(8,128)(2,1)S(1)} %shard_map.109.sent), channel_id=1, source_target_pairs={{0,16},{4,20},{8,24},{12,28},{16,0},{20,4},{24,8},{28,12},{1,17},{... | collective-permute-start | bytes 393224 | tf_op jit(solution)/shard_map/ppermute | solution.py:41
  57.3 7.3 %collective-permute-start.10 = (bf16[512,128]{1,0:T(8,128)(2,1)S(1)}, bf16[512,128]{1,0:T(8,128)(2,1)S(1)}, u32[]{:S(2)}, u32[]{:S(2)}) collective-permute-start(bf16[512,128]{1,0:T(8,128)(2,1)S(1)} %shard_map.114.sent), channel_id=1, source_target_pairs={{0,4},{4,0},{8,12},{12,8},{16,20},{20,16},{24,28},{28,24},{1,5},{5... | collective-permute-start | bytes 393224 | tf_op jit(solution)/shard_map/ppermute | solution.py:41
  60.3 9.7 %collective-permute-start.23 = (bf16[1024,128]{1,0:T(8,128)(2,1)S(1)}, bf16[1024,128]{1,0:T(8,128)(2,1)S(1)}, u32[]{:S(2)}, u32[]{:S(2)}) collective-permute-start(bf16[1024,128]{1,0:T(8,128)(2,1)S(1)} %shard_map.126.r_7_.r_11_), channel_id=1, source_target_pairs={{0,8},{4,12},{8,0},{12,4},{16,24},{20,28},{24,16},{28,20},{1,9},{5... | collective-permute-start | bytes 786440 | tf_op jit(solution)/shard_map/ppermute | solution.py:41
  64.4 11.9 %collective-permute-start.5 = (bf16[1024,128]{1,0:T(8,128)(2,1)S(1)}, bf16[1024,128]{1,0:T(8,128)(2,1)S(1)}, u32[]{:S(2)}, u32[]{:S(2)}) collective-permute-start(bf16[1024,128]{1,0:T(8,128)(2,1)S(1)} %shard_map.110.r_8_.r_12_), channel_id=1, source_target_pairs={{0,4},{4,0},{8,12},{12,8},{16,20},{20,16},{24,28},{28,24},{1,5},{5... | collective-permute-start | bytes 786440 | tf_op jit(solution)/shard_map/ppermute | solution.py:41
  64.6 11.6 %collective-permute-start.11 = (bf16[1024,128]{1,0:T(8,128)(2,1)S(1)}, bf16[1024,128]{1,0:T(8,128)(2,1)S(1)}, u32[]{:S(2)}, u32[]{:S(2)}) collective-permute-start(bf16[1024,128]{1,0:T(8,128)(2,1)S(1)} %shard_map.115.r_9_.r_13_), channel_id=1, source_target_pairs={{0,8},{4,12},{8,0},{12,4},{16,24},{20,28},{24,16},{28,20},{1,9},{5... | collective-permute-start | bytes 786440 | tf_op jit(solution)/shard_map/ppermute | solution.py:41
  66.8 7.1 %collective-permute-start.17 = (bf16[1152,128]{1,0:T(8,128)(2,1)S(1)}, bf16[1152,128]{1,0:T(8,128)(2,1)S(1)}, u32[]{:S(2)}, u32[]{:S(2)}) collective-permute-start(bf16[1152,128]{1,0:T(8,128)(2,1)S(1)} %get-tuple-element.129.r_6_.r_10_), channel_id=1, source_target_pairs={{0,4},{4,0},{8,12},{12,8},{16,20},{20,16},{24,28},{28,24},{1,5},{5... | collective-permute-start | bytes 884744 | tf_op jit(solution)/shard_map/ppermute | solution.py:41
  79.8 8.4 %collective-permute-start.25 = (f32[512,128]{1,0:T(8,128)S(1)}, f32[512,128]{1,0:T(8,128)S(1)}, u32[]{:S(2)}, u32[]{:S(2)}) collective-permute-start(f32[512,128]{1,0:T(8,128)S(1)} %add.12), channel_id=1, source_target_pairs={{0,2},{1,3},{2,0},{3,1},{4,6},{5,7},{6,4},{7,5},{8,10},{9,11},{10,... | collective-permute-start | bytes 786440 | tf_op jit(solution)/shard_map/ppermute | solution.py:41
  92.3 9.5 %collective-permute-start.39 = (bf16[1216,128]{1,0:T(8,128)(2,1)S(1)}, bf16[1216,128]{1,0:T(8,128)(2,1)S(1)}, u32[]{:S(2)}, u32[]{:S(2)}) collective-permute-start(bf16[1216,128]{1,0:T(8,128)(2,1)S(1)} %get-tuple-element.157), channel_id=1, source_target_pairs={{0,4},{4,0},{8,12},{12,8},{16,20},{20,16},{24,28},{28,24},{1,5},{5... | collective-permute-start | bytes 933896 | tf_op jit(solution)/shard_map/ppermute | solution.py:41
  93.9 15.7 %collective-permute-start.45 = (bf16[1024,128]{1,0:T(8,128)(2,1)S(1)}, bf16[1024,128]{1,0:T(8,128)(2,1)S(1)}, u32[]{:S(2)}, u32[]{:S(2)}) collective-permute-start(bf16[1024,128]{1,0:T(8,128)(2,1)S(1)} %get-tuple-element.173), channel_id=1, source_target_pairs={{0,8},{4,12},{8,0},{12,4},{16,24},{20,28},{24,16},{28,20},{1,9},{5... | collective-permute-start | bytes 786440 | tf_op jit(solution)/shard_map/ppermute | solution.py:41
  101.8 7.0 %collective-permute-start.40 = (bf16[704,128]{1,0:T(8,128)(2,1)S(1)}, bf16[704,128]{1,0:T(8,128)(2,1)S(1)}, u32[]{:S(2)}, u32[]{:S(2)}) collective-permute-start(bf16[704,128]{1,0:T(8,128)(2,1)S(1)} %get-tuple-element.160), channel_id=1, source_target_pairs={{0,8},{4,12},{8,0},{12,4},{16,24},{20,28},{24,16},{28,20},{1,9},{5... | collective-permute-start | bytes 540680 | tf_op jit(solution)/shard_map/ppermute | solution.py:41
  103.4 16.3 %collective-permute-start.27 = (bf16[1024,128]{1,0:T(8,128)(2,1)S(1)}, bf16[1024,128]{1,0:T(8,128)(2,1)S(1)}, u32[]{:S(2)}, u32[]{:S(2)}) collective-permute-start(bf16[1024,128]{1,0:T(8,128)(2,1)S(1)} %get-tuple-element.145), channel_id=1, source_target_pairs={{0,4},{4,0},{8,12},{12,8},{16,20},{20,16},{24,28},{28,24},{1,5},{5... | collective-permute-start | bytes 786440 | tf_op jit(solution)/shard_map/ppermute | solution.py:41
  104.9 15.9 %collective-permute-start.33 = (bf16[1024,128]{1,0:T(8,128)(2,1)S(1)}, bf16[1024,128]{1,0:T(8,128)(2,1)S(1)}, u32[]{:S(2)}, u32[]{:S(2)}) collective-permute-start(bf16[1024,128]{1,0:T(8,128)(2,1)S(1)} %get-tuple-element.151), channel_id=1, source_target_pairs={{0,8},{4,12},{8,0},{12,4},{16,24},{20,28},{24,16},{28,20},{1,9},{5... | collective-permute-start | bytes 786440 | tf_op jit(solution)/shard_map/ppermute | solution.py:41
  108.8 6.4 %collective-permute-start.41 = (bf16[448,128]{1,0:T(8,128)(2,1)S(1)}, bf16[448,128]{1,0:T(8,128)(2,1)S(1)}, u32[]{:S(2)}, u32[]{:S(2)}) collective-permute-start(bf16[448,128]{1,0:T(8,128)(2,1)S(1)} %get-tuple-element.163), channel_id=1, source_target_pairs={{0,16},{4,20},{8,24},{12,28},{16,0},{20,4},{24,8},{28,12},{1,17},{... | collective-permute-start | bytes 344072 | tf_op jit(solution)/shard_map/ppermute | solution.py:41
  109.6 14.6 %collective-permute-start.46 = (bf16[512,128]{1,0:T(8,128)(2,1)S(1)}, bf16[512,128]{1,0:T(8,128)(2,1)S(1)}, u32[]{:S(2)}, u32[]{:S(2)}) collective-permute-start(bf16[512,128]{1,0:T(8,128)(2,1)S(1)} %get-tuple-element.175), channel_id=1, source_target_pairs={{0,4},{4,0},{8,12},{12,8},{16,20},{20,16},{24,28},{28,24},{1,5},{5... | collective-permute-start | bytes 393224 | tf_op jit(solution)/shard_map/ppermute | solution.py:41
  117.7 11.5 %collective-permute-start.42 = (bf16[448,128]{1,0:T(8,128)(2,1)S(1)}, bf16[448,128]{1,0:T(8,128)(2,1)S(1)}, u32[]{:S(2)}, u32[]{:S(2)}) collective-permute-start(bf16[448,128]{1,0:T(8,128)(2,1)S(1)} %get-tuple-element.168.r_0_), channel_id=1, source_target_pairs={{0,16},{4,20},{8,24},{12,28},{16,0},{20,4},{24,8},{28,12},{1,17},{... | collective-permute-start | bytes 344072 | tf_op jit(solution)/shard_map/ppermute | solution.py:41
  119.8 11.8 %collective-permute-start.28 = (bf16[512,128]{1,0:T(8,128)(2,1)S(1)}, bf16[512,128]{1,0:T(8,128)(2,1)S(1)}, u32[]{:S(2)}, u32[]{:S(2)}) collective-permute-start(bf16[512,128]{1,0:T(8,128)(2,1)S(1)} %get-tuple-element.147), channel_id=1, source_target_pairs={{0,16},{4,20},{8,24},{12,28},{16,0},{20,4},{24,8},{28,12},{1,17},{... | collective-permute-start | bytes 393224 | tf_op jit(solution)/shard_map/ppermute | solution.py:41
  120.9 10.9 %collective-permute-start.34 = (bf16[512,128]{1,0:T(8,128)(2,1)S(1)}, bf16[512,128]{1,0:T(8,128)(2,1)S(1)}, u32[]{:S(2)}, u32[]{:S(2)}) collective-permute-start(bf16[512,128]{1,0:T(8,128)(2,1)S(1)} %get-tuple-element.153), channel_id=1, source_target_pairs={{0,4},{4,0},{8,12},{12,8},{16,20},{20,16},{24,28},{28,24},{1,5},{5... | collective-permute-start | bytes 393224 | tf_op jit(solution)/shard_map/ppermute | solution.py:41
  124.2 9.7 %collective-permute-start.47 = (bf16[256,128]{1,0:T(8,128)(2,1)S(1)}, bf16[256,128]{1,0:T(8,128)(2,1)S(1)}, u32[]{:S(2)}, u32[]{:S(2)}) collective-permute-start(bf16[256,128]{1,0:T(8,128)(2,1)S(1)} %get-tuple-element.177), channel_id=1, source_target_pairs={{0,16},{4,20},{8,24},{12,28},{16,0},{20,4},{24,8},{28,12},{1,17},{... | collective-permute-start | bytes 196616 | tf_op jit(solution)/shard_map/ppermute | solution.py:41
  129.2 19.9 %collective-permute-start.43 = (bf16[704,128]{1,0:T(8,128)(2,1)S(1)}, bf16[704,128]{1,0:T(8,128)(2,1)S(1)}, u32[]{:S(2)}, u32[]{:S(2)}) collective-permute-start(bf16[704,128]{1,0:T(8,128)(2,1)S(1)} %get-tuple-element.170.r_0_), channel_id=1, source_target_pairs={{0,8},{4,12},{8,0},{12,4},{16,24},{20,28},{24,16},{28,20},{1,9},{5... | collective-permute-start | bytes 540680 | tf_op jit(solution)/shard_map/ppermute | solution.py:41
  131.7 7.4 %collective-permute-start.29 = (bf16[256,128]{1,0:T(8,128)(2,1)S(1)}, bf16[256,128]{1,0:T(8,128)(2,1)S(1)}, u32[]{:S(2)}, u32[]{:S(2)}) collective-permute-start(bf16[256,128]{1,0:T(8,128)(2,1)S(1)} %get-tuple-element.149), channel_id=1, source_target_pairs={{0,8},{4,12},{8,0},{12,4},{16,24},{20,28},{24,16},{28,20},{1,9},{5... | collective-permute-start | bytes 196616 | tf_op jit(solution)/shard_map/ppermute | solution.py:41
  131.8 7.4 %collective-permute-start.35 = (bf16[256,128]{1,0:T(8,128)(2,1)S(1)}, bf16[256,128]{1,0:T(8,128)(2,1)S(1)}, u32[]{:S(2)}, u32[]{:S(2)}) collective-permute-start(bf16[256,128]{1,0:T(8,128)(2,1)S(1)} %get-tuple-element.155), channel_id=1, source_target_pairs={{0,16},{4,20},{8,24},{12,28},{16,0},{20,4},{24,8},{28,12},{1,17},{... | collective-permute-start | bytes 196616 | tf_op jit(solution)/shard_map/ppermute | solution.py:41
  133.9 7.4 %collective-permute-start.48 = (bf16[256,128]{1,0:T(8,128)(2,1)S(1)}, bf16[256,128]{1,0:T(8,128)(2,1)S(1)}, u32[]{:S(2)}, u32[]{:S(2)}) collective-permute-start(bf16[256,128]{1,0:T(8,128)(2,1)S(1)} %shard_map.149.sent), channel_id=1, source_target_pairs={{0,16},{4,20},{8,24},{12,28},{16,0},{20,4},{24,8},{28,12},{1,17},{... | collective-permute-start | bytes 196616 | tf_op jit(solution)/shard_map/ppermute | solution.py:41
  141.4 7.9 %collective-permute-start.49 = (bf16[512,128]{1,0:T(8,128)(2,1)S(1)}, bf16[512,128]{1,0:T(8,128)(2,1)S(1)}, u32[]{:S(2)}, u32[]{:S(2)}) collective-permute-start(bf16[512,128]{1,0:T(8,128)(2,1)S(1)} %shard_map.150.sent), channel_id=1, source_target_pairs={{0,4},{4,0},{8,12},{12,8},{16,20},{20,16},{24,28},{28,24},{1,5},{5... | collective-permute-start | bytes 393224 | tf_op jit(solution)/shard_map/ppermute | solution.py:41
  143.7 7.2 %collective-permute-start.31 = (bf16[512,128]{1,0:T(8,128)(2,1)S(1)}, bf16[512,128]{1,0:T(8,128)(2,1)S(1)}, u32[]{:S(2)}, u32[]{:S(2)}) collective-permute-start(bf16[512,128]{1,0:T(8,128)(2,1)S(1)} %shard_map.135.sent), channel_id=1, source_target_pairs={{0,16},{4,20},{8,24},{12,28},{16,0},{20,4},{24,8},{28,12},{1,17},{... | collective-permute-start | bytes 393224 | tf_op jit(solution)/shard_map/ppermute | solution.py:41
  144.5 8.5 %collective-permute-start.37 = (bf16[512,128]{1,0:T(8,128)(2,1)S(1)}, bf16[512,128]{1,0:T(8,128)(2,1)S(1)}, u32[]{:S(2)}, u32[]{:S(2)}) collective-permute-start(bf16[512,128]{1,0:T(8,128)(2,1)S(1)} %shard_map.140.sent), channel_id=1, source_target_pairs={{0,4},{4,0},{8,12},{12,8},{16,20},{20,16},{24,28},{28,24},{1,5},{5... | collective-permute-start | bytes 393224 | tf_op jit(solution)/shard_map/ppermute | solution.py:41
  149.2 9.2 %collective-permute-start.44 = (bf16[1216,128]{1,0:T(8,128)(2,1)S(1)}, bf16[1216,128]{1,0:T(8,128)(2,1)S(1)}, u32[]{:S(2)}, u32[]{:S(2)}) collective-permute-start(bf16[1216,128]{1,0:T(8,128)(2,1)S(1)} %get-tuple-element.172.r_6_), channel_id=1, source_target_pairs={{0,4},{4,0},{8,12},{12,8},{16,20},{20,16},{24,28},{28,24},{1,5},{5... | collective-permute-start | bytes 933896 | tf_op jit(solution)/shard_map/ppermute | solution.py:41
  149.3 8.6 %collective-permute-start.50 = (bf16[1024,128]{1,0:T(8,128)(2,1)S(1)}, bf16[1024,128]{1,0:T(8,128)(2,1)S(1)}, u32[]{:S(2)}, u32[]{:S(2)}) collective-permute-start(bf16[1024,128]{1,0:T(8,128)(2,1)S(1)} %shard_map.151.r_7_), channel_id=1, source_target_pairs={{0,8},{4,12},{8,0},{12,4},{16,24},{20,28},{24,16},{28,20},{1,9},{5... | collective-permute-start | bytes 786440 | tf_op jit(solution)/shard_map/ppermute | solution.py:41
  151.0 10.2 %collective-permute-start.32 = (bf16[1024,128]{1,0:T(8,128)(2,1)S(1)}, bf16[1024,128]{1,0:T(8,128)(2,1)S(1)}, u32[]{:S(2)}, u32[]{:S(2)}) collective-permute-start(bf16[1024,128]{1,0:T(8,128)(2,1)S(1)} %shard_map.136.r_8_), channel_id=1, source_target_pairs={{0,4},{4,0},{8,12},{12,8},{16,20},{20,16},{24,28},{28,24},{1,5},{5... | collective-permute-start | bytes 786440 | tf_op jit(solution)/shard_map/ppermute | solution.py:41
  153.0 8.1 %collective-permute-start.38 = (bf16[1024,128]{1,0:T(8,128)(2,1)S(1)}, bf16[1024,128]{1,0:T(8,128)(2,1)S(1)}, u32[]{:S(2)}, u32[]{:S(2)}) collective-permute-start(bf16[1024,128]{1,0:T(8,128)(2,1)S(1)} %shard_map.141.r_9_), channel_id=1, source_target_pairs={{0,8},{4,12},{8,0},{12,4},{16,24},{20,28},{24,16},{28,20},{1,9},{5... | collective-permute-start | bytes 786440 | tf_op jit(solution)/shard_map/ppermute | solution.py:41
  164.8 10.2 %collective-permute-start.52 = (f32[520,128]{1,0:T(8,128)S(1)}, f32[520,128]{1,0:T(8,128)S(1)}, u32[]{:S(2)}, u32[]{:S(2)}) collective-permute-start(f32[520,128]{1,0:T(8,128)S(1)} %add.14), channel_id=1, source_target_pairs={{0,2},{1,3},{2,0},{3,1},{4,6},{5,7},{6,4},{7,5},{8,10},{9,11},{10,... | collective-permute-start | bytes 798728 | tf_op jit(solution)/shard_map/ppermute | solution.py:41
  (13 other events, 191.7 us)
